TPU v7x, 256 devices: a whole 4x4x8 slice. The times are simulated.
256 devices in a mesh: ctx: 64 (over z, x, core), dp: 4 (over y).
Axes of the slice: x: 4, y: 4, z: 8, core: 2. Of those that a mesh axis runs over, the one named last changes fastest.
Arguments:
- query: bfloat16 [4, 32768, 1024], P('dp', 'ctx'), may hold values from -6 to 6
- key: bfloat16 [4, 32768, 1024], P('dp', 'ctx'), may hold values from -6 to 6
- value: bfloat16 [4, 32768, 1024], P('dp', 'ctx'), may hold values from -12 to 12
- log_decay: float32 [4, 8, 32768], P('dp', None, 'ctx'), may hold values from -2 to 0
- grad_out: bfloat16 [4, 32768, 1024], P('dp', 'ctx'), may hold values from -32 to 32
- query_map: bfloat16 [8, 128, 128], replicated, may hold values from -0.5 to 0.5
- key_map: bfloat16 [8, 128, 128], replicated, may hold values from -0.5 to 0.5
Outputs:
- output: bfloat16 [4, 32768, 1024], P('dp', 'ctx')
- grad_query: bfloat16 [4, 32768, 1024], P('dp', 'ctx')
- grad_key: bfloat16 [4, 32768, 1024], P('dp', 'ctx')
- grad_value: bfloat16 [4, 32768, 1024], P('dp', 'ctx')
- query_map_grad: float32 [8, 128, 128], replicated
- key_map_grad: float32 [8, 128, 128], replicated
All inputs are finite; a program needn't handle non-finite values.
Results may differ from a plain program's by a relative error of at most 0.0073.
Values sent between devices are 32-bit elements; how exact they have to be, the bound alone decides.
No kernel may reach another device: no remote copies, remote signals or barrier semaphores. Data moves between devices by JAX's collectives and lax.ppermute only.
A program may use at most 128 MiB of HBM per device.

v0:
```python
import math

import jax
import jax.numpy as jnp
from jax import lax
from jax.sharding import PartitionSpec as P

BLOCK = 256


def prefix(value, axis, combine, identity, reverse):
    count, mine = (lax.axis_size(axis), lax.axis_index(axis))
    everything = jax.tree.map(lambda part: lax.all_gather(part, axis), value)
    start = jax.tree.map(
        lambda part, zero: jnp.broadcast_to(jnp.asarray(zero, part.dtype), part.shape),
        value,
        identity,
    )

    def step(k, before):
        at = count - 1 - k if reverse else k
        reached = at > mine if reverse else at < mine
        new = combine(before, jax.tree.map(lambda part: part[at], everything))
        return jax.tree.map(lambda a, b: jnp.where(reached, a, b), new, before)

    return lax.fori_loop(0, count, step, start)


def combine(earlier, latter):
    return (earlier[0] * latter[0], latter[0][:, None, None] * earlier[1] + latter[1])


def silu_slope(pre_act):
    sigmoid_val = jax.nn.sigmoid(pre_act)
    return sigmoid_val * (1.0 + pre_act * (1.0 - sigmoid_val))


def feature_map(inputs, weight, block_len):
    head_count, head_width = (weight.shape[0], weight.shape[1])
    split_in = inputs.reshape(inputs.shape[0], head_count, head_width)
    pre_act = jnp.einsum("lhd,hde->hle", split_in, weight, preferred_element_type=jnp.float32)
    features_out = jax.nn.silu(pre_act).astype(jnp.bfloat16)
    return (pre_act, features_out.reshape(head_count, -1, block_len, head_width))


def heads_blocks(array, head_count, block_len):
    rows = array.shape[0]
    return array.reshape(rows // block_len, block_len, head_count, -1).transpose(2, 0, 1, 3)


def unblock(array):
    head_count, block_count, block_len, head_width = array.shape
    return array.transpose(1, 2, 0, 3).reshape(1, block_count * block_len, head_count * head_width)


def scan_forward(pair, identity):
    return prefix(pair, "ctx", combine, identity, False)


def scan_backward(pair, identity):
    return prefix(pair, "ctx", combine, identity, True)


def local(query, key, value, log_decay, grad_out, query_map, key_map):
    head_count, head_width = (query_map.shape[0], query_map.shape[1])
    tokens = query.shape[1]
    block_count = tokens // BLOCK
    out_scale = 1.0 / (head_width * math.sqrt(BLOCK))
    query_rows, key_rows = (query[0], key[0])
    pre_query, query_feat = feature_map(query_rows, query_map, BLOCK)
    pre_key, key_feat = feature_map(key_rows, key_map, BLOCK)
    value_heads = heads_blocks(value[0], head_count, BLOCK)
    grad_heads = heads_blocks(grad_out[0], head_count, BLOCK)
    cumulative = jnp.cumsum(log_decay[0].reshape(head_count, block_count, BLOCK), axis=-1)
    totals = cumulative[..., -1]
    decay_now = jnp.exp(totals)
    causal_mask = jnp.arange(BLOCK)[:, None] >= jnp.arange(BLOCK)[None, :]
    differ = cumulative[..., :, None] - cumulative[..., None, :]
    weights = jnp.where(causal_mask, jnp.exp(jnp.where(causal_mask, differ, 0.0)), 0.0)
    key_dec = (
        key_feat.astype(jnp.float32) * jnp.exp(totals[..., None] - cumulative)[..., None]
    ).astype(jnp.bfloat16)
    query_dec = (query_feat.astype(jnp.float32) * jnp.exp(cumulative)[..., None]).astype(
        jnp.bfloat16
    )
    updates = jnp.einsum(
        "hntd,hnte->hnde", key_dec, value_heads, preferred_element_type=jnp.float32
    )
    contribs = jnp.einsum(
        "hnsd,hnse->hnde", query_dec, grad_heads, preferred_element_type=jnp.float32
    )
    identity = (
        jnp.ones((head_count,), jnp.float32),
        jnp.zeros((head_count, head_width, head_width), jnp.float32),
    )
    device_pair = identity
    for block_index in range(block_count):
        device_pair = combine(device_pair, (decay_now[:, block_index], updates[:, block_index]))
    device_adjoint = identity
    for block_index in range(block_count - 1, -1, -1):
        device_adjoint = combine(
            device_adjoint, (decay_now[:, block_index], contribs[:, block_index])
        )
    incoming = scan_forward((device_pair[0], device_pair[1]), identity)
    entering = incoming[1]
    chained = [entering]
    block_index = 0
    chained.append(decay_now[:, block_index, None, None] * chained[-1] + updates[:, block_index])
    states = jnp.stack(chained, axis=1)
    state_round = states.astype(jnp.bfloat16)
    scores = jnp.einsum("hnsd,hntd->hnst", query_feat, key_feat, preferred_element_type=jnp.float32)
    block_probs = (scores * weights).astype(jnp.bfloat16)
    intra_out = jnp.einsum(
        "hnst,hntd->hnsd", block_probs, value_heads, preferred_element_type=jnp.float32
    )
    inter_out = jnp.einsum(
        "hnsd,hnde->hnse", query_dec, state_round, preferred_element_type=jnp.float32
    )
    output = (out_scale * (intra_out + inter_out)).astype(jnp.bfloat16)
    grad_scores = (
        jnp.einsum("hnse,hnte->hnst", grad_heads, value_heads, preferred_element_type=jnp.float32)
        * weights
    ).astype(jnp.bfloat16)
    grad_qfeat = out_scale * (
        jnp.einsum("hnst,hntd->hnsd", grad_scores, key_feat, preferred_element_type=jnp.float32)
        + jnp.exp(cumulative)[..., None]
        * jnp.einsum("hnse,hnde->hnsd", grad_heads, state_round, preferred_element_type=jnp.float32)
    )
    grad_pre_query = (
        grad_qfeat.reshape(head_count, tokens, head_width) * silu_slope(pre_query)
    ).astype(jnp.bfloat16)
    grad_query = jnp.einsum(
        "hle,hde->lhd", grad_pre_query, query_map, preferred_element_type=jnp.float32
    ).astype(jnp.bfloat16)
    query_part = jnp.einsum(
        "lhd,hle->hde",
        query_rows.reshape(tokens, head_count, head_width),
        grad_pre_query,
        preferred_element_type=jnp.float32,
    )
    outgoing = scan_backward((device_adjoint[0], device_adjoint[1]), identity)
    trailing = [outgoing[1]]
    block_index = 1
    trailing.insert(
        0, contribs[:, block_index] + decay_now[:, block_index, None, None] * trailing[0]
    )
    after_round = jnp.stack(trailing, axis=1).astype(jnp.bfloat16)
    grad_value = out_scale * (
        jnp.einsum("hnst,hnsd->hntd", block_probs, grad_heads, preferred_element_type=jnp.float32)
        + jnp.einsum("hntd,hnde->hnte", key_dec, after_round, preferred_element_type=jnp.float32)
    )
    grad_kfeat = out_scale * (
        jnp.einsum("hnst,hnsd->hntd", grad_scores, query_feat, preferred_element_type=jnp.float32)
        + jnp.exp(totals[..., None] - cumulative)[..., None]
        * jnp.einsum(
            "hnte,hnde->hntd", value_heads, after_round, preferred_element_type=jnp.float32
        )
    )
    grad_pre_key = (
        grad_kfeat.reshape(head_count, tokens, head_width) * silu_slope(pre_key)
    ).astype(jnp.bfloat16)
    grad_key = jnp.einsum(
        "hle,hde->lhd", grad_pre_key, key_map, preferred_element_type=jnp.float32
    ).astype(jnp.bfloat16)
    key_part = jnp.einsum(
        "lhd,hle->hde",
        key_rows.reshape(tokens, head_count, head_width),
        grad_pre_key,
        preferred_element_type=jnp.float32,
    )
    query_map_grad, key_map_grad = lax.psum((query_part, key_part), ("ctx", "dp"))
    return (
        unblock(output),
        grad_query.reshape(1, tokens, head_count * head_width),
        grad_key.reshape(1, tokens, head_count * head_width),
        unblock(grad_value.astype(jnp.bfloat16)),
        query_map_grad,
        key_map_grad,
    )


def solution(mesh):
    return jax.shard_map(
        local,
        mesh=mesh,
        in_specs=(
            P("dp", "ctx", None),
            P("dp", "ctx", None),
            P("dp", "ctx", None),
            P("dp", None, "ctx"),
            P("dp", "ctx", None),
            P(),
            P(),
        ),
        out_specs=(
            P("dp", "ctx", None),
            P("dp", "ctx", None),
            P("dp", "ctx", None),
            P("dp", "ctx", None),
            P(),
            P(),
        ),
        check_vma=False,
    )
```

profile of v0, /device:TPU:1, one launch (start us, length us, event | category | flops | bytes accessed | tf_op | source)
XLA Modules:
  0.0 742.1 jit_solution(9720998795194737838)
XLA Ops:
  9.7 1.5 copy.169
  11.3 1.9 multiply_convert_fusion.7
  19.9 132.0 %all-reduce = f32[512]{0:T(512)S(1)} all-reduce(f32[512]{0:T(512)S(1)} %get-tuple-element.326), channel_id=2, replica_groups=mesh['ctx'=64,'dp'=4] {'ctx'}, use_global_device_ids=true, to_apply=%add | all-reduce | flops 512 | bytes 4096
  152.1 1.5 copy.171
  153.6 2.5 copy.170
  156.1 1.5 multiply_convert_fusion
  157.6 1.3 copy-done.6
  159.0 2.1 fusion.48
  161.0 5.5 all-gather.6.cloned.1.call-done
  166.5 78.5 %while.31 = (s32[]{:T(128)}, f32[8,128,128]{2,1,0:T(8,128)S(1)}, s32[]{:T(128)}, f32[64,8]{1,0:T(8,128)S(1)}, f32[64,8,128,128]{3,2,1,0:T(8,128)}, /*index=5*/s32[]{:T(128)}, s32[]{:T(128)}, s32[]{:T(128)}, s32[]{:T(128)}) while((s32[]{:T(128)}, f32[8,128,128]{2,1,0:T(8,128)S(1)}, s32[]{:T(128)}, f32[64,8]{1,0:T(8,128)S(1)}, ...), condition=%wide.region_5.6_spmd.clone, body=%wide.region_4.5_spmd.clone.sunk | while | flops 524296 | bytes 1573127 | solution.py:26
  167.8 1.2 fusion.68
  169.0 1.2 fusion.68
  170.2 1.2 fusion.68
  171.5 1.2 fusion.68
  172.7 1.2 fusion.68
  177.6 1.2 fusion.68
  186.2 1.2 fusion.68
  194.8 1.2 fusion.68
  200.9 1.2 fusion.68
  209.5 1.2 fusion.68
  218.1 1.2 fusion.68
  224.2 1.2 fusion.68
  232.8 1.2 fusion.68
  241.4 1.2 fusion.68
  245.1 1.2 fusion.45
  246.3 2.1 fusion.3
  248.4 2.3 fusion.2
  251.7 2.0 fusion.16
  255.8 2.7 multiply_convert_fusion.1
  261.5 1.6 copy.149
  263.2 2.3 reshape.163
  265.5 2.7 convolution_convert_fusion
  268.2 2.3 copy.155
  270.5 3.0 convolution_bitcast_fusion
  273.5 3.8 fusion.47
  277.2 2.1 fusion.18
  279.3 115.0 %all-gather.4.cloned.1.call-done = f32[64,8,128,128]{3,2,1,0:T(8,128)} async-done(((f32[1,8,128,128]{3,2,1,0:T(8,128)}), f32[64,8,128,128]{3,2,1,0:T(8,128)}) %all-gather.4.cloned.1.call-update) | async-done | bytes 33554448 | tf_op jit(solution)/shard_map/all_gather | solution.py:13
  394.3 77.7 %while.30 = (s32[]{:T(128)}, f32[8,128,128]{2,1,0:T(8,128)S(1)}, s32[]{:T(128)}, f32[64,8]{1,0:T(8,128)S(1)}, f32[64,8,128,128]{3,2,1,0:T(8,128)}, /*index=5*/s32[]{:T(128)}, s32[]{:T(128)}) while((s32[]{:T(128)}, f32[8,128,128]{2,1,0:T(8,128)S(1)}, s32[]{:T(128)}, f32[64,8]{1,0:T(8,128)S(1)}, f32[64,8,128,128]{3,2,1,0:T(8,128)}, ...), condition=%wide.region_3.4_spmd.clone, body=%wide.region_2.3_spmd.clone.sunk | while | flops 524292 | bytes 1573065 | solution.py:26
  394.3 1.3 fusion.67
  472.2 2.2 fusion.5
  475.9 1.3 convolution_bitcast_fusion.1
  477.2 1.5 convolution_convert_fusion.1
  478.7 1.3 copy.154
  480.1 2.1 fusion.6
  482.9 1.3 reshape.158
  484.2 247.3 %all-reduce.4.cloned.1.call-done = (f32[8,128,128]{1,2,0:T(8,128)}, f32[8,128,128]{1,2,0:T(8,128)}) async-done(((f32[8,128,128]{1,2,0:T(8,128)}, f32[8,128,128]{1,2,0:T(8,128)}), (f32[8,128,128]{1,2,0:T(8,128)}, f32[8,128,128]{1,2,0:T(8,128)})) %all-reduce.4.cloned.1.call-update) | async-done | bytes 1048592 | tf_op jit(solution)/shard_map/psum | solution.py:171
  731.5 2.0 copy.156
  733.5 2.0 copy.157
  (336 shorter events, 150.8 us)
Async XLA Ops:
  7.2 241.2 %copy-start = (bf16[8,128,128]{2,1,0:T(8,128)(2,1)S(1)}, bf16[8,128,128]{2,1,0:T(8,128)(2,1)}, u32[]{:S(2)}) copy-start(bf16[8,128,128]{2,1,0:T(8,128)(2,1)} %param.17) | copy-start | bytes 786436
  7.2 4.1 copy-start.23
  7.2 159.4 %all-gather.6.cloned.1.call-start = ((), (), s32[]{:S(2)}) async-start(), calls=%async_computation.1 | async-start | bytes 34078720 | tf_op jit(solution)/shard_map/all_gather | solution.py:13
  11.2 2.0 copy-start.14
  13.2 1.0 copy-start.12
  13.2 1.6 copy-start.22
  13.2 2.5 copy-start.28
  14.2 3.8 copy-start.4
  15.7 4.2 copy-start.24
  17.9 1.0 copy-start.9
  19.9 374.4 %all-gather.4.cloned.1.call-start = ((), (), s32[]{:S(2)}) async-start(), calls=%async_computation | async-start | bytes 34078720 | tf_op jit(solution)/shard_map/all_gather | solution.py:13
  156.1 2.9 copy-start.13
  157.6 1.3 copy-start.6
  246.2 2.1 copy-start.16
  250.7 1.0 copy-start.1
  250.7 4.0 copy-start.26
  250.7 4.0 copy-start.27
  253.7 0.9 copy-start.10
  255.6 475.9 %all-reduce.4.cloned.1.call-start = ((), (), s32[]{:S(2)}) async-start(), calls=%async_computation.2 | async-start | bytes 2097152 | tf_op jit(solution)/shard_map/psum | solution.py:171
  258.6 1.4 copy-start.7
  258.6 2.0 copy-start.2
  270.5 3.0 copy-start.3
  273.5 3.8 copy-start.8
  394.3 77.8 %copy-start.11 = (f32[8,2,128,128]{3,2,1,0:T(8,128)S(1)}, f32[8,2,128,128]{3,2,1,0:T(8,128)}, u32[]{:S(2)}) copy-start(f32[8,2,128,128]{3,2,1,0:T(8,128)} %copy-done.10) | copy-start | bytes 3145732
  394.3 77.8 %copy-start.25 = (f32[8]{0:T(128)S(1)}, f32[8]{0:T(128)}, u32[]{:S(2)}) copy-start(f32[8]{0:T(128)} %copy-done.24) | copy-start | bytes 100
  472.2 2.3 copy-start.17
  472.2 2.3 copy-start.19
  472.2 2.4 copy-start.21
  474.6 1.2 copy-start.15
  477.2 2.8 copy-start.5
  478.7 1.3 copy-start.18
  478.7 1.3 copy-start.20
Sparse Core Ops, SparseCore 0:
  20.0 146.5 all-gather.5
  255.7 138.5 all-gather.3
  477.3 254.0 all-reduce.3
where the time goes:
time: 750 us; the launch traced here: 742 us
  waiting for transfers between devices  368 us (49%)
  other arithmetic  156 us (21%)
  blocking collectives  132 us (18%)
  matrix products  35.6 us (5%)
  local copies, waits for them, and re-layouts  30.6 us (4%)
  between operations  14.9 us (2%)
    psum x1, waiting for transfers between devices, local(): lax.psum((query_part, key_part), ('ctx', 'dp'))  247 us
    select_n x128, other arithmetic, step(): return jax.tree.map(lambda a, b: jnp.where(reached, a, b), new, before)  150 us
    unnamed x1, blocking collectives  132 us
    all_gather x2, waiting for transfers between devices, prefix(): everything = jax.tree.map(lambda part: lax.all_gather(part, axis), value)  120 us
    unnamed x68, local copies, waits for them, and re-layouts  21.1 us
  transfers between devices with their start and end apart: 3, of which 3 were waited for; matrix products, arithmetic and copies ran while one was open for 5% of the time, Pallas kernels for 0%

commit v1 on v0

v1 whole, which is shorter than its diff:
```python
import math

import jax
import jax.numpy as jnp
from jax import lax
from jax.experimental import pallas as pl
from jax.experimental.pallas import tpu as pltpu
from jax.sharding import Mesh, PartitionSpec as P

BLOCK = 256
HEADS = 8
DH = 128
TOK = 512
HPB = 2
SCALE = 1.0 / (DH * math.sqrt(BLOCK))
F32 = jnp.float32
BF16 = jnp.bfloat16
CHIPS = 32
ROWS = HEADS * DH // CHIPS


def dot(a, b, dims=((1,), (0,))):
    return lax.dot_general(a, b, (dims, ((), ())), preferred_element_type=F32)


NT = ((1,), (1,))
TN = ((0,), (0,))


def split3(x):
    hi = x.astype(BF16)
    rest = x - hi.astype(F32)
    mid = rest.astype(BF16)
    low = (rest - mid.astype(F32)).astype(BF16)
    return jnp.concatenate([hi, mid, low], axis=1)


def lower3():
    t = lax.broadcasted_iota(jnp.int32, (BLOCK, BLOCK), 0)
    s = lax.broadcasted_iota(jnp.int32, (BLOCK, BLOCK), 1)
    low = jnp.where(s <= t, 1.0, 0.0).astype(BF16)
    return jnp.concatenate([low, low, low], axis=1)


def cumul_cols(low, row):
    return dot(low, split3(jnp.broadcast_to(row, (DH, BLOCK))), NT)


def cumul_rows(low, row):
    return dot(split3(jnp.broadcast_to(row, (8, BLOCK))), low, NT)


def sigmoid(u):
    return 1.0 / (1.0 + jnp.exp(-u))


def k1_body(core, q_ref, k_ref, v_ref, g_ref, ld_ref, wq_ref, wk_ref,
            qf_ref, kf_ref, mine_ref, send_ref, up_ref, con_ref, dec_ref):
    step = pl.program_id(0)
    first = core[0] == 0
    low = lower3()
    for i in range(HPB):
        lanes = slice(i * DH, (i + 1) * DH)
        ups, cons, tots = [], [], []
        for b in range(2):
            rows = slice(b * BLOCK, (b + 1) * BLOCK)
            row = ld_ref[pl.ds(step * HPB + i, 1), rows]
            cum = cumul_cols(low, row)
            tot = cum[BLOCK - 1:BLOCK, :]
            pre_q = dot(q_ref[rows, lanes], wq_ref[i])
            pre_k = dot(k_ref[rows, lanes], wk_ref[i])
            qf = (pre_q * sigmoid(pre_q)).astype(BF16)
            kf = (pre_k * sigmoid(pre_k)).astype(BF16)
            qf_ref[rows, lanes] = qf
            kf_ref[rows, lanes] = kf
            qdec = (qf.astype(F32) * jnp.exp(cum)).astype(BF16)
            kdec = (kf.astype(F32) * jnp.exp(tot - cum)).astype(BF16)
            ups.append(dot(kdec, v_ref[rows, lanes], TN))
            cons.append(dot(qdec, g_ref[rows, lanes], TN))
            tots.append(tot)
        d0, d1 = jnp.exp(tots[0]), jnp.exp(tots[1])
        up = d1 * ups[0] + ups[1]
        con = cons[0] + d0 * cons[1]
        mine_ref[i, 0:DH, :] = jnp.where(first, up, con)
        send_ref[i, 0:DH, :] = jnp.where(first, con, up)
        both = jnp.broadcast_to(d0 * d1, (8, DH))
        mine_ref[i, DH:DH + 8, :] = both
        send_ref[i, DH:DH + 8, :] = both
        up_ref[i] = ups[0]
        con_ref[i] = cons[1]
        dec_ref[i, 0:8, :] = jnp.broadcast_to(d0, (8, DH))
        dec_ref[i, 8:16, :] = jnp.broadcast_to(d1, (8, DH))


def combine_body(mine_ref, recv_ref, out_ref):
    for h in range(HEADS):
        other = recv_ref[h, DH:DH + 1, :]
        agg = other * mine_ref[h, 0:DH, :] + recv_ref[h, 0:DH, :]
        both = other * mine_ref[h, DH:DH + 1, :]
        for part in range(DH // ROWS):
            at = (h * (DH // ROWS) + part) * (ROWS + 1)
            out_ref[at:at + ROWS, :] = agg[part * ROWS:(part + 1) * ROWS, :]
            out_ref[at + ROWS:at + ROWS + 1, :] = both


def scan_body(core, in_ref, out_ref):
    first = core[0] == 0

    def pieces(k):
        at = k * (ROWS + 1)
        return in_ref[at:at + ROWS, :], in_ref[at + ROWS:at + ROWS + 1, :]

    state = jnp.zeros((ROWS, DH), F32)
    for k in range(CHIPS):
        out_ref[k * ROWS:(k + 1) * ROWS, :] = state
        part, decay = pieces(k)
        state = decay * state + part
    state = jnp.zeros((ROWS, DH), F32)
    for k in range(CHIPS - 1, -1, -1):
        rows = slice(k * ROWS, (k + 1) * ROWS)
        out_ref[rows, :] = jnp.where(first, out_ref[rows, :], state)
        part, decay = pieces(k)
        state = decay * state + part


def k2_body(q_ref, k_ref, v_ref, g_ref, ld_ref, wq_ref, wk_ref, qf_ref, kf_ref,
            aq_ref, bq_ref, ak_ref, bk_ref, oi_ref, vi_ref, qd_ref, kd_ref):
    step = pl.program_id(0)
    low = lower3()
    t = lax.broadcasted_iota(jnp.int32, (BLOCK, BLOCK), 0)
    s = lax.broadcasted_iota(jnp.int32, (BLOCK, BLOCK), 1)
    causal = s <= t
    for i in range(HPB):
        lanes = slice(i * DH, (i + 1) * DH)
        for b in range(2):
            rows = slice(b * BLOCK, (b + 1) * BLOCK)
            row = ld_ref[pl.ds(step * HPB + i, 1), rows]
            cum = cumul_cols(low, row)
            across = cumul_rows(low, row)[0:1, :]
            tot = cum[BLOCK - 1:BLOCK, :]
            wide = jnp.concatenate([cum, cum], axis=1)
            weights = jnp.exp(jnp.where(causal, wide - across, -1e9))
            qf, kf = qf_ref[rows, lanes], kf_ref[rows, lanes]
            v, g = v_ref[rows, lanes], g_ref[rows, lanes]
            probs = (dot(qf, kf, NT) * weights).astype(BF16)
            grads = (dot(g, v, NT) * weights).astype(BF16)
            oi_ref[rows, lanes] = SCALE * dot(probs, v)
            vi_ref[rows, lanes] = SCALE * dot(probs, g, TN)
            early, late = jnp.exp(cum), jnp.exp(tot - cum)
            qd_ref[rows, lanes] = (qf.astype(F32) * early).astype(BF16)
            kd_ref[rows, lanes] = (kf.astype(F32) * late).astype(BF16)
            pre_q = dot(q_ref[rows, lanes], wq_ref[i])
            sig_q = sigmoid(pre_q)
            slope_q = SCALE * (sig_q * (1.0 + pre_q * (1.0 - sig_q)))
            aq_ref[rows, lanes] = dot(grads, kf) * slope_q
            bq_ref[rows, lanes] = early * slope_q
            pre_k = dot(k_ref[rows, lanes], wk_ref[i])
            sig_k = sigmoid(pre_k)
            slope_k = SCALE * (sig_k * (1.0 + pre_k * (1.0 - sig_k)))
            ak_ref[rows, lanes] = dot(grads, qf, TN) * slope_k
            bk_ref[rows, lanes] = late * slope_k


def k3a_body(core, inc_ref, recv_ref, up_ref, con_ref, dec_ref, q_ref, k_ref, v_ref, g_ref,
             aq_ref, bq_ref, ak_ref, bk_ref,
             gpq_ref, gpk_ref, st_ref, af_ref, mine_ref, send_ref):
    first = core[0] == 0
    for i in range(HPB):
        lanes = slice(i * DH, (i + 1) * DH)
        inc, recv = inc_ref[i], recv_ref[i]
        state = jnp.where(first, inc, recv)
        after = jnp.where(first, recv, inc)
        d0, d1 = dec_ref[i, 0:1, :], dec_ref[i, 8:9, :]
        states = [state.astype(BF16), (d0 * state + up_ref[i]).astype(BF16)]
        afters = [(con_ref[i] + d1 * after).astype(BF16), after.astype(BF16)]
        for b in range(2):
            rows = slice(b * BLOCK, (b + 1) * BLOCK)
            st_ref[i, b] = states[b]
            af_ref[i, b] = afters[b]
            gpq_ref[rows, lanes] = (
                aq_ref[rows, lanes] + bq_ref[rows, lanes] * dot(g_ref[rows, lanes], states[b], NT)
            ).astype(BF16)
            gpk_ref[rows, lanes] = (
                ak_ref[rows, lanes] + bk_ref[rows, lanes] * dot(v_ref[rows, lanes], afters[b], NT)
            ).astype(BF16)
        part_q = dot(q_ref[:, lanes], gpq_ref[:, lanes], TN)
        part_k = dot(k_ref[:, lanes], gpk_ref[:, lanes], TN)
        mine_ref[i] = jnp.where(first, part_q, part_k)
        send_ref[i] = jnp.where(first, part_k, part_q)


def k3b_body(oi_ref, vi_ref, qd_ref, kd_ref, st_ref, af_ref, gpq_ref, gpk_ref, wq_ref, wk_ref,
             out_ref, gq_ref, gk_ref, gv_ref):
    for i in range(HPB):
        lanes = slice(i * DH, (i + 1) * DH)
        for b in range(2):
            rows = slice(b * BLOCK, (b + 1) * BLOCK)
            out_ref[rows, lanes] = (
                oi_ref[rows, lanes] + SCALE * dot(qd_ref[rows, lanes], st_ref[i, b])
            ).astype(BF16)
            gv_ref[rows, lanes] = (
                vi_ref[rows, lanes] + SCALE * dot(kd_ref[rows, lanes], af_ref[i, b])
            ).astype(BF16)
            gq_ref[rows, lanes] = dot(gpq_ref[rows, lanes], wq_ref[i], NT).astype(BF16)
            gk_ref[rows, lanes] = dot(gpk_ref[rows, lanes], wk_ref[i], NT).astype(BF16)


def spread_body(in_ref, out_ref):
    total = in_ref[0]
    for k in range(1, in_ref.shape[0]):
        total = total + in_ref[k]
    for k in range(out_ref.shape[0]):
        out_ref[k] = total


def add_body(a_ref, b_ref, out_ref):
    out_ref[...] = a_ref[...] + b_ref[...]


def smem():
    return pl.BlockSpec(memory_space=pltpu.SMEM)


def seq():
    return pl.BlockSpec((TOK, HPB * DH), lambda i: (0, i))


def per_head(*tail):
    zeros = (0,) * len(tail)
    return pl.BlockSpec((HPB,) + tail, lambda i: (i,) + zeros)


def whole(*shape):
    zeros = (0,) * len(shape)
    return pl.BlockSpec(shape, lambda i: zeros)


def shape(dims, kind=F32):
    return jax.ShapeDtypeStruct(dims, kind)


def call(body, name, ins, outs, out_shapes, flops=0, grid=HEADS // HPB, after=0):
    return pl.pallas_call(
        lambda *refs: body(*refs[after:]),
        grid=(grid,),
        in_specs=[pl.BlockSpec(memory_space=pl.ANY)] * after + ins,
        out_specs=outs,
        out_shape=out_shapes,
        name=name,
        cost_estimate=pl.CostEstimate(flops=flops, transcendentals=0, bytes_accessed=1 << 20),
        compiler_params=pltpu.CompilerParams(dimension_semantics=("arbitrary",)),
    )


def exchange(x, axes):
    return lax.all_to_all(x, axes, 0, 0, tiled=True)


def swap_cores(x):
    return lax.ppermute(x, "c", [(0, 1), (1, 0)])


SEQ_B = shape((TOK, HEADS * DH), BF16)
SEQ_F = shape((TOK, HEADS * DH), F32)
MAT = shape((HEADS, DH, DH), F32)


def local(query, key, value, log_decay, grad_out, query_map, key_map):
    core = lax.axis_index("c").astype(jnp.int32).reshape(1)
    q, k, v, g = (a[0] for a in (query, key, value, grad_out))
    ld = log_decay[0]
    maps = (query_map, key_map)
    seqs = (q, k, v, g)
    ld_spec = whole(HEADS, TOK)
    map_specs = [per_head(DH, DH)] * 2
    qf, kf, mine, send, up0, con1, dec = call(
        k1_body, "k1",
        [smem()] + [seq()] * 4 + [ld_spec] + map_specs,
        [seq(), seq(), per_head(DH + 8, DH), per_head(DH + 8, DH),
         per_head(DH, DH), per_head(DH, DH), per_head(16, DH)],
        [SEQ_B, SEQ_B, shape((HEADS, DH + 8, DH)), shape((HEADS, DH + 8, DH)), MAT, MAT,
         shape((HEADS, 16, DH))],
    )(core, *seqs, ld, *maps)
    recv = swap_cores(send)
    packed = call(
        combine_body, "combine",
        [whole(HEADS, DH + 8, DH)] * 2, whole(CHIPS * (ROWS + 1), DH),
        shape((CHIPS * (ROWS + 1), DH)), grid=1,
    )(mine, recv)
    swapped = exchange(packed.reshape(CHIPS, (ROWS + 1) * DH), ("z", "x"))
    aq, bq, ak, bk, oi, vi, qd, kd = call(
        k2_body, "k2",
        [seq()] * 4 + [ld_spec] + map_specs + [seq()] * 2,
        [seq()] * 8,
        [SEQ_F] * 6 + [SEQ_B] * 2,
        flops=1 << 30,
        after=1,
    )(packed, *seqs, ld, *maps, qf, kf)
    scanned = call(
        scan_body, "scan",
        [smem(), whole(CHIPS * (ROWS + 1), DH)], whole(CHIPS * ROWS, DH),
        shape((CHIPS * ROWS, DH)), grid=1, after=1,
    )(qd, core, swapped.reshape(CHIPS * (ROWS + 1), DH))
    inc = exchange(scanned.reshape(CHIPS, ROWS * DH), ("z", "x")).reshape(HEADS, DH, DH)
    passed = mine[:, DH:DH + 1, :] * inc + mine[:, :DH, :]
    recv = swap_cores(passed)
    gpq, gpk, st, af, mine, send = call(
        k3a_body, "k3a",
        [smem()] + [per_head(DH, DH)] * 4 + [per_head(16, DH)] + [seq()] * 8,
        [seq(), seq(), per_head(2, DH, DH), per_head(2, DH, DH), per_head(DH, DH), per_head(DH, DH)],
        [SEQ_B, SEQ_B, shape((HEADS, 2, DH, DH), BF16), shape((HEADS, 2, DH, DH), BF16), MAT, MAT],
    )(core, inc, recv, up0, con1, dec, *seqs, aq, bq, ak, bk)
    recv = swap_cores(send)
    chip = call(add_body, "add", [whole(HEADS, DH, DH)] * 2, whole(HEADS, DH, DH), MAT, grid=1)(
        mine, recv
    )
    pieces = exchange(chip.reshape(16, -1), ("x", "dp"))
    rows = HEADS * DH // 16
    out, gq, gk, gv = call(
        k3b_body, "k3b",
        [seq()] * 4 + [per_head(2, DH, DH)] * 2 + [seq()] * 2 + map_specs,
        [seq()] * 4,
        [SEQ_B] * 4,
        flops=1 << 30,
        after=1,
    )(chip, oi, vi, qd, kd, st, af, gpq, gpk, *maps)
    spread = call(spread_body, "spread_z", [whole(16, rows, DH)], whole(8, rows, DH),
                  shape((8, rows, DH)), grid=1, after=1)(out, pieces.reshape(16, rows, DH))
    pieces = exchange(spread.reshape(8, -1), "z")
    spread = call(spread_body, "spread_xy", [whole(8, rows, DH)], whole(16, rows, DH),
                  shape((16, rows, DH)), grid=1)(pieces.reshape(8, rows, DH))
    own = exchange(spread.reshape(16, -1), ("x", "dp")).reshape(HEADS, DH, DH)
    other = swap_cores(own)
    first = core[0] == 0
    query_map_grad = jnp.where(first, own, other)
    key_map_grad = jnp.where(first, other, own)
    return (out[None], gq[None], gk[None], gv[None], query_map_grad, key_map_grad)


def solution(mesh):
    fine = Mesh(mesh.devices.reshape(8, 4, 2, 4), ("z", "x", "c", "dp"))
    ctx = ("z", "x", "c")
    act = P("dp", ctx, None)
    return jax.shard_map(
        local,
        mesh=fine,
        in_specs=(act, act, act, P("dp", None, ctx), act, P(), P()),
        out_specs=(act, act, act, act, P(), P()),
        check_vma=False,
    )
```

time: 750 us -> 143 us (0.19)
  waiting for transfers between devices: 368 us -> 29 us
  other arithmetic: 156 us -> 1.11 us
  blocking collectives: 132 us -> 26.9 us
  Pallas kernels: 0 us -> 48.2 us
  matrix products: 35.6 us -> 0 us
  starting transfers between devices: 0.3 us -> 32.5 us
  local copies, waits for them, and re-layouts: 30.6 us -> 3.99 us
  between operations: 14.9 us -> 0.72 us
    psum x1 -> x0, waiting for transfers between devices: 247 us -> none  [local(): lax.psum((query_part, key_part), ('ctx', 'dp'))]
    select_n x128 -> x1, other arithmetic: 150 us -> 1.05 us  [local(): key_map_grad = jnp.where(first, other, own)]
    unnamed x1 -> x0, blocking collectives: 132 us -> none
    all_gather x2 -> x0, waiting for transfers between devices: 120 us -> none  [prefix(): everything = jax.tree.map(lambda part: lax.all_gather(part, axis), value)]
    pallas_call x0 -> x9, Pallas kernels: none -> 48.2 us  [the longest x1 13.5 us: local(): call(k2_body, 'k2', [seq()] * 4 + [ld_spec] + map_specs + [seq()] * 2, [s...]
    dot_general x18 -> x0, matrix products: 35.6 us -> none  [the longest x2 4.22 us: feature_map(): jnp.einsum('lhd,hde->hle', split_in, weight, preferred_element_type=jnp.f...]
    all_to_all x0 -> x2, blocking collectives: none -> 26.9 us  [exchange(): return lax.all_to_all(x, axes, 0, 0, tiled=True)]
    all_to_all x0 -> x3, waiting for transfers between devices: none -> 22.4 us  [exchange(): return lax.all_to_all(x, axes, 0, 0, tiled=True)]
  transfers between devices with their start and end apart: 3 -> 7, of which waited for: 3 -> 7; matrix products, arithmetic and copies ran while one was open for 5% -> 0% of each run, Pallas kernels for 0% -> 14%
where the time goes in v1:
time: 143 us
  Pallas kernels  48.2 us (34%)
  starting transfers between devices  32.5 us (23%)
  waiting for transfers between devices  29 us (20%)
  blocking collectives  26.9 us (19%)
  local copies, waits for them, and re-layouts  3.99 us (3%)
    all_to_all x2, blocking collectives, exchange(): return lax.all_to_all(x, axes, 0, 0, tiled=True)  26.9 us
    all_to_all x3, waiting for transfers between devices, exchange(): return lax.all_to_all(x, axes, 0, 0, tiled=True)  22.4 us
    all_to_all x3, starting transfers between devices, exchange(): return lax.all_to_all(x, axes, 0, 0, tiled=True)  21.4 us
    pallas_call x1, Pallas kernels, local(): call(k2_body, 'k2', [seq()] * 4 + [ld_spec] + map_specs + [seq()] * 2, [s...  13.5 us
    ppermute x4, starting transfers between devices, swap_cores(): return lax.ppermute(x, 'c', [(0, 1), (1, 0)])  11.2 us
    pallas_call x1, Pallas kernels, local(): call(k1_body, 'k1', [smem()] + [seq()] * 4 + [ld_spec] + map_specs, [seq(...  10.2 us
    pallas_call x1, Pallas kernels, local(): call(k3a_body, 'k3a', [smem()] + [per_head(DH, DH)] * 4 + [per_head(16, D...  8.24 us
    pallas_call x1, Pallas kernels, local(): call(k3b_body, 'k3b', [seq()] * 4 + [per_head(2, DH, DH)] * 2 + [seq()] *...  6.63 us
  transfers between devices with their start and end apart: 7, of which 7 were waited for; matrix products, arithmetic and copies ran while one was open for 0% of the time, Pallas kernels for 14%

profile of v1, /device:TPU:1, one launch (start us, length us, event | category | flops | bytes accessed | tf_op | source)
XLA Modules:
  0.0 142.5 jit_solution(11574900719413107350)
XLA Ops:
  0.6 10.2 %k1.1 = (bf16[512,1024]{1,0:T(8,128)(2,1)}, bf16[512,1024]{1,0:T(8,128)(2,1)}, f32[8,136,128]{2,1,0:T(8,128)}, f32[8,136,128]{2,1,0:T(8,128)}, f32[8,128,128]{2,...) custom-call(s32[1]{0:T(128)} %bitcast.refs_0_.refs_1_, bf16[512,1024]{1,0:T(8,128)(2,1)} %bitcast.26, ...), custom_call_target="tpu_custom_call" | custom-call | bytes 1048576 | tf_op jit(solution)/shard_map/k1/pallas_call | solution.py:276
  10.8 3.3 %collective-permute-start = (f32[8,136,128]{2,1,0:T(8,128)}, f32[8,136,128]{2,1,0:T(8,128)S(1)}, u32[]{:S(2)}, u32[]{:S(2)}) collective-permute-start(f32[8,136,128]{2,1,0:T(8,128)} %get-tuple-element.32), channel_id=1, source_target_pairs={{0,4},{4,0},{1,5},{5,1},{2,6},{6,2},{3,7},{7,3},{8,12},{12,8},{9,1... | collective-permute-start | bytes 1671176 | tf_op jit(solution)/shard_map/ppermute | solution.py:260
  14.1 1.8 %collective-permute-done.refs_1_ = f32[8,136,128]{2,1,0:T(8,128)S(1)} collective-permute-done((f32[8,136,128]{2,1,0:T(8,128)}, f32[8,136,128]{2,1,0:T(8,128)S(1)}, u32[]{:S(2)}, u32[]{:S(2)}) %collective-permute-start) | collective-permute-done | bytes 557088 | tf_op jit(solution)/shard_map/ppermute | solution.py:260
  15.9 0.0 copy-start.4
  15.9 0.8 copy-done.4
  16.7 2.1 %combine.1.refs_0_ = f32[1056,128]{1,0:T(8,128)} custom-call(f32[8,136,128]{2,1,0:T(8,128)} %get-tuple-element.31.refs_0_, f32[8,136,128]{2,1,0:T(8,128)} %copy-done.4), custom_call_target="tpu_custom_call" | custom-call | bytes 1048576 | tf_op jit(solution)/shard_map/combine/pallas_call | solution.py:285
  18.8 9.3 %all-to-all-start = ((f32[32,1,4224]{2,1,0:T(1,128)}), f32[32,1,4224]{2,1,0:T(1,128)S(1)}, u32[]{:S(2)}, u32[]{:S(2)}) async-start(f32[32,1,4224]{2,1,0:T(1,128)} %bitcast.38), calls=%async_computation | async-start | bytes 1081344 | tf_op jit(solution)/shard_map/all_to_all | solution.py:256
  28.1 13.5 %k2.1 = (f32[512,1024]{1,0:T(8,128)}, f32[512,1024]{1,0:T(8,128)}, f32[512,1024]{1,0:T(8,128)}, f32[512,1024]{1,0:T(8,128)}, f32[512,1024]{1,0:T(8,128)}, /*inde...) custom-call(f32[1056,128]{1,0:T(8,128)} %combine.1.refs_0_, bf16[512,1024]{1,0:T(8,128)(2,1)} %bitcast.27, ...), custom_call_target="tpu_custom_call" | custom-call | flops 1073741824 | bytes 1048576 | tf_op jit(solution)/shard_map/k2/pallas_call | solution.py:291
  41.7 0.0 copy-start.2
  41.7 3.3 %all-to-all-done = f32[32,1,4224]{2,1,0:T(1,128)S(1)} async-done(((f32[32,1,4224]{2,1,0:T(1,128)}), f32[32,1,4224]{2,1,0:T(1,128)S(1)}, u32[]{:S(2)}, u32[]{:S(2)}) %all-to-all-start) | async-done | bytes 540704 | tf_op jit(solution)/shard_map/all_to_all | solution.py:256
  44.9 0.0 copy-start.1
  44.9 0.8 copy-done.1
  45.7 2.0 %scan.1 = f32[1024,128]{1,0:T(8,128)} custom-call(bf16[512,1024]{1,0:T(8,128)(2,1)} %get-tuple-element.35.refs_0_.refs_3_, s32[1]{0:T(128)} %bitcast.refs_0_.refs_1_, f32[1056,128]{1,0:T(8,128)} %bitcast.42), custom_call_target="tpu_custom_call" | custom-call | bytes 1048576 | tf_op jit(solution)/shard_map/scan/pallas_call | solution.py:299
  47.7 5.9 %all-to-all-start.1 = ((f32[32,1,4096]{2,1,0:T(1,128)}), f32[32,1,4096]{2,1,0:T(1,128)S(1)}, u32[]{:S(2)}, u32[]{:S(2)}) async-start(f32[32,1,4096]{2,1,0:T(1,128)} %bitcast.46), calls=%async_computation.1 | async-start | bytes 1048576 | tf_op jit(solution)/shard_map/all_to_all | solution.py:256
  53.7 0.0 copy-done.2
  53.7 15.4 %all-to-all-done.1 = f32[32,1,4096]{2,1,0:T(1,128)S(1)} async-done(((f32[32,1,4096]{2,1,0:T(1,128)}), f32[32,1,4096]{2,1,0:T(1,128)S(1)}, u32[]{:S(2)}, u32[]{:S(2)}) %all-to-all-start.1) | async-done | bytes 524320 | tf_op jit(solution)/shard_map/all_to_all | solution.py:256
  69.1 0.0 copy-start
  69.1 0.1 slice_add_fusion
  69.1 3.4 %collective-permute-start.1 = (f32[8,128,128]{2,1,0:T(8,128)S(1)}, f32[8,128,128]{2,1,0:T(8,128)S(1)}, u32[]{:S(2)}, u32[]{:S(2)}) collective-permute-start(f32[8,128,128]{2,1,0:T(8,128)S(1)} %slice_add_fusion), channel_id=1, source_target_pairs={{0,4},{4,0},{1,5},{5,1},{2,6},{6,2},{3,7},{7,3},{8,12},{12,8},{9,1... | collective-permute-start | bytes 1572872 | tf_op jit(solution)/shard_map/ppermute | solution.py:260
  72.5 1.5 %collective-permute-done.1.refs_2_ = f32[8,128,128]{2,1,0:T(8,128)S(1)} collective-permute-done((f32[8,128,128]{2,1,0:T(8,128)S(1)}, f32[8,128,128]{2,1,0:T(8,128)S(1)}, u32[]{:S(2)}, u32[]{:S(2)}) %collective-permute-start.1) | collective-permute-done | bytes 524320 | tf_op jit(solution)/shard_map/ppermute | solution.py:260
  74.0 0.0 copy-start.5
  74.0 0.0 copy-done
  74.1 0.8 copy-done.5
  74.8 8.2 %k3a.1 = (bf16[512,1024]{1,0:T(8,128)(2,1)}, bf16[512,1024]{1,0:T(8,128)(2,1)}, bf16[8,2,128,128]{3,2,1,0:T(8,128)(2,1)}, bf16[8,2,128,128]{3,2,1,0:T(8,128)(2,1...) custom-call(s32[1]{0:T(128)} %bitcast.refs_0_.refs_1_, f32[8,128,128]{2,1,0:T(8,128)} %bitcast.40, ...), custom_call_target="tpu_custom_call" | custom-call | bytes 1048576 | tf_op jit(solution)/shard_map/k3a/pallas_call | solution.py:307
  83.1 0.5 collective-permute-start.2
  83.5 1.8 %collective-permute-done.2.refs_1_ = f32[8,128,128]{2,1,0:T(8,128)S(1)} collective-permute-done((f32[8,128,128]{2,1,0:T(8,128)}, f32[8,128,128]{2,1,0:T(8,128)S(1)}, u32[]{:S(2)}, u32[]{:S(2)}) %collective-permute-start.2) | collective-permute-done | bytes 524320 | tf_op jit(solution)/shard_map/ppermute | solution.py:260
  85.3 0.0 copy-start.6
  85.3 0.8 copy-done.6
  86.1 2.0 %add.6.refs_0_ = f32[8,128,128]{2,1,0:T(8,128)} custom-call(f32[8,128,128]{2,1,0:T(8,128)} %get-tuple-element.43.refs_0_, f32[8,128,128]{2,1,0:T(8,128)} %copy-done.6), custom_call_target="tpu_custom_call" | custom-call | bytes 1048576 | tf_op jit(solution)/shard_map/add/pallas_call | solution.py:314
  88.1 6.1 %all-to-all-start.2 = ((f32[16,1,8192]{2,1,0:T(1,128)}), f32[16,1,8192]{2,1,0:T(1,128)S(1)}, u32[]{:S(2)}, u32[]{:S(2)}) async-start(f32[16,1,8192]{2,1,0:T(1,128)} %bitcast.41), calls=%async_computation.2 | async-start | bytes 1048576 | tf_op jit(solution)/shard_map/all_to_all | solution.py:256
  94.2 6.6 %k3b.1 = (bf16[512,1024]{1,0:T(8,128)(2,1)}, bf16[512,1024]{1,0:T(8,128)(2,1)}, bf16[512,1024]{1,0:T(8,128)(2,1)}, bf16[512,1024]{1,0:T(8,128)(2,1)}) custom-call(f32[8,128,128]{2,1,0:T(8,128)} %add.6.refs_0_, f32[512,1024]{1,0:T(8,128)} %get-tuple-element.45.refs_1_, f32[512,1024]{1,0:T(8,128)} %get-tuple-element.46.refs_2_, ...), custom_call_target="tpu_custom_call" | custom-call | flops 1073741824 | bytes 1048576 | tf_op jit(solution)/shard_map/k3b/pallas_call | solution.py:319
  100.9 3.7 %all-to-all-done.2 = f32[16,1,8192]{2,1,0:T(1,128)S(1)} async-done(((f32[16,1,8192]{2,1,0:T(1,128)}), f32[16,1,8192]{2,1,0:T(1,128)S(1)}, u32[]{:S(2)}, u32[]{:S(2)}) %all-to-all-start.2) | async-done | bytes 524320 | tf_op jit(solution)/shard_map/all_to_all | solution.py:256
  104.6 0.0 copy-start.3
  104.6 0.8 copy-done.3
  105.4 1.8 %spread_z.1 = f32[8,64,128]{2,1,0:T(8,128)} custom-call(bf16[512,1024]{1,0:T(8,128)(2,1)} %get-tuple-element.52.refs_0_, f32[16,64,128]{2,1,0:T(8,128)} %bitcast.43), custom_call_target="tpu_custom_call" | custom-call | bytes 1048576 | tf_op jit(solution)/shard_map/spread_z/pallas_call | solution.py:327
  107.2 13.2 %all_to_all.45 = f32[8,1,8192]{2,1,0:T(1,128)} all-to-all(f32[8,1,8192]{2,1,0:T(1,128)} %bitcast.49), channel_id=1, replica_groups=mesh['z'=8,'x'=4,'c'=2,'dp'=4] {'z'}, dimensions={0} | all-to-all | bytes 524288 | tf_op jit(solution)/shard_map/all_to_all | solution.py:256
  120.4 1.8 %spread_xy.1 = f32[16,64,128]{2,1,0:T(8,128)} custom-call(f32[8,64,128]{2,1,0:T(8,128)} %bitcast.50), custom_call_target="tpu_custom_call" | custom-call | bytes 1048576 | tf_op jit(solution)/shard_map/spread_xy/pallas_call | solution.py:330
  122.2 13.7 %all_to_all.46 = f32[16,1,8192]{2,1,0:T(1,128)S(1)} all-to-all(f32[16,1,8192]{2,1,0:T(1,128)} %bitcast.47), channel_id=1, replica_groups=mesh['z'=8,'x'=4,'c'=2,'dp'=4] {'x','dp'}, dimensions={0} | all-to-all | bytes 1048576 | tf_op jit(solution)/shard_map/all_to_all | solution.py:256
  135.9 4.1 %collective-permute-start.3 = (f32[8,128,128]{2,1,0:T(8,128)S(1)}, f32[8,128,128]{2,1,0:T(8,128)S(1)}, u32[]{:S(2)}, u32[]{:S(2)}) collective-permute-start(f32[8,128,128]{2,1,0:T(8,128)S(1)} %bitcast.44), channel_id=1, source_target_pairs={{0,4},{4,0},{1,5},{5,1},{2,6},{6,2},{3,7},{7,3},{8,12},{12,8},{9,1... | collective-permute-start | bytes 1572872 | tf_op jit(solution)/shard_map/ppermute | solution.py:260
  140.0 1.5 %collective-permute-done.3 = f32[8,128,128]{2,1,0:T(8,128)S(1)} collective-permute-done((f32[8,128,128]{2,1,0:T(8,128)S(1)}, f32[8,128,128]{2,1,0:T(8,128)S(1)}, u32[]{:S(2)}, u32[]{:S(2)}) %collective-permute-start.3) | collective-permute-done | bytes 524320 | tf_op jit(solution)/shard_map/ppermute | solution.py:260
  141.5 1.1 broadcast_select_fusion
  (1 shorter events, 0.0 us)
Async XLA Ops:
  10.8 5.1 %collective-permute-start = (f32[8,136,128]{2,1,0:T(8,128)}, f32[8,136,128]{2,1,0:T(8,128)S(1)}, u32[]{:S(2)}, u32[]{:S(2)}) collective-permute-start(f32[8,136,128]{2,1,0:T(8,128)} %get-tuple-element.32), channel_id=1, source_target_pairs={{0,4},{4,0},{1,5},{5,1},{2,6},{6,2},{3,7},{7,3},{8,12},{12,8},{9,1... | collective-permute-start | bytes 1671176 | tf_op jit(solution)/shard_map/ppermute | solution.py:260
  15.9 0.8 copy-start.4
  18.8 26.2 %all-to-all-start = ((f32[32,1,4224]{2,1,0:T(1,128)}), f32[32,1,4224]{2,1,0:T(1,128)S(1)}, u32[]{:S(2)}, u32[]{:S(2)}) async-start(f32[32,1,4224]{2,1,0:T(1,128)} %bitcast.38), calls=%async_computation | async-start | bytes 1081344 | tf_op jit(solution)/shard_map/all_to_all | solution.py:256
  41.7 12.0 %copy-start.2 = (f32[8,136,128]{2,1,0:T(8,128)S(1)}, f32[8,136,128]{2,1,0:T(8,128)}, u32[]{:S(2)}) copy-start(f32[8,136,128]{2,1,0:T(8,128)} %get-tuple-element.31.refs_0_) | copy-start | bytes 1671172
  44.9 0.8 copy-start.1
  47.7 21.4 %all-to-all-start.1 = ((f32[32,1,4096]{2,1,0:T(1,128)}), f32[32,1,4096]{2,1,0:T(1,128)S(1)}, u32[]{:S(2)}, u32[]{:S(2)}) async-start(f32[32,1,4096]{2,1,0:T(1,128)} %bitcast.46), calls=%async_computation.1 | async-start | bytes 1048576 | tf_op jit(solution)/shard_map/all_to_all | solution.py:256
  69.1 5.0 %copy-start = (f32[32,1,4096]{2,1,0:T(1,128)}, f32[32,1,4096]{2,1,0:T(1,128)S(1)}, u32[]{:S(2)}) copy-start(f32[32,1,4096]{2,1,0:T(1,128)S(1)} %all-to-all-done.1) | copy-start | bytes 1572868
  69.1 4.9 %collective-permute-start.1 = (f32[8,128,128]{2,1,0:T(8,128)S(1)}, f32[8,128,128]{2,1,0:T(8,128)S(1)}, u32[]{:S(2)}, u32[]{:S(2)}) collective-permute-start(f32[8,128,128]{2,1,0:T(8,128)S(1)} %slice_add_fusion), channel_id=1, source_target_pairs={{0,4},{4,0},{1,5},{5,1},{2,6},{6,2},{3,7},{7,3},{8,12},{12,8},{9,1... | collective-permute-start | bytes 1572872 | tf_op jit(solution)/shard_map/ppermute | solution.py:260
  74.0 0.8 copy-start.5
  83.1 2.2 %collective-permute-start.2 = (f32[8,128,128]{2,1,0:T(8,128)}, f32[8,128,128]{2,1,0:T(8,128)S(1)}, u32[]{:S(2)}, u32[]{:S(2)}) collective-permute-start(f32[8,128,128]{2,1,0:T(8,128)} %get-tuple-element.44), channel_id=1, source_target_pairs={{0,4},{4,0},{1,5},{5,1},{2,6},{6,2},{3,7},{7,3},{8,12},{12,8},{9,1... | collective-permute-start | bytes 1572872 | tf_op jit(solution)/shard_map/ppermute | solution.py:260
  85.3 0.8 copy-start.6
  88.1 16.5 %all-to-all-start.2 = ((f32[16,1,8192]{2,1,0:T(1,128)}), f32[16,1,8192]{2,1,0:T(1,128)S(1)}, u32[]{:S(2)}, u32[]{:S(2)}) async-start(f32[16,1,8192]{2,1,0:T(1,128)} %bitcast.41), calls=%async_computation.2 | async-start | bytes 1048576 | tf_op jit(solution)/shard_map/all_to_all | solution.py:256
  104.6 0.8 copy-start.3
  135.9 5.6 %collective-permute-start.3 = (f32[8,128,128]{2,1,0:T(8,128)S(1)}, f32[8,128,128]{2,1,0:T(8,128)S(1)}, u32[]{:S(2)}, u32[]{:S(2)}) collective-permute-start(f32[8,128,128]{2,1,0:T(8,128)S(1)} %bitcast.44), channel_id=1, source_target_pairs={{0,4},{4,0},{1,5},{5,1},{2,6},{6,2},{3,7},{7,3},{8,12},{12,8},{9,1... | collective-permute-start | bytes 1572872 | tf_op jit(solution)/shard_map/ppermute | solution.py:260

commit v2 on v1

--- a/solution.py
+++ b/solution.py
@@ -46,8 +46,8 @@
     return dot(low, split3(jnp.broadcast_to(row, (DH, BLOCK))), NT)
 
 
-def cumul_rows(low, row):
-    return dot(split3(jnp.broadcast_to(row, (8, BLOCK))), low, NT)
+def cumul_rows(low, rows):
+    return dot(split3(rows), low, NT)
 
 
 def sigmoid(u):
@@ -55,41 +55,44 @@
 
 
 def k1_body(core, q_ref, k_ref, v_ref, g_ref, ld_ref, wq_ref, wk_ref,
-            qf_ref, kf_ref, mine_ref, send_ref, up_ref, con_ref, dec_ref):
+            mine_ref, send_ref, up_ref, con_ref, dec_ref, cum_ref):
     step = pl.program_id(0)
     first = core[0] == 0
-    low = lower3()
+
+    @pl.when(step == 0)
+    def _():
+        low = lower3()
+        for b in range(2):
+            rows = slice(b * BLOCK, (b + 1) * BLOCK)
+            cum_ref[:, rows] = cumul_rows(low, ld_ref[:, rows])
+
     for i in range(HPB):
         lanes = slice(i * DH, (i + 1) * DH)
         ups, cons, tots = [], [], []
         for b in range(2):
             rows = slice(b * BLOCK, (b + 1) * BLOCK)
-            row = ld_ref[pl.ds(step * HPB + i, 1), rows]
-            cum = cumul_cols(low, row)
-            tot = cum[BLOCK - 1:BLOCK, :]
-            pre_q = dot(q_ref[rows, lanes], wq_ref[i])
-            pre_k = dot(k_ref[rows, lanes], wk_ref[i])
+            cum = cum_ref[pl.ds(step * HPB + i, 1), rows]
+            tot = cum[:, BLOCK - 1:BLOCK]
+            pre_q = dot(wq_ref[i], q_ref[rows, lanes], ((0,), (1,)))
+            pre_k = dot(wk_ref[i], k_ref[rows, lanes], ((0,), (1,)))
             qf = (pre_q * sigmoid(pre_q)).astype(BF16)
             kf = (pre_k * sigmoid(pre_k)).astype(BF16)
-            qf_ref[rows, lanes] = qf
-            kf_ref[rows, lanes] = kf
             qdec = (qf.astype(F32) * jnp.exp(cum)).astype(BF16)
             kdec = (kf.astype(F32) * jnp.exp(tot - cum)).astype(BF16)
-            ups.append(dot(kdec, v_ref[rows, lanes], TN))
-            cons.append(dot(qdec, g_ref[rows, lanes], TN))
-            tots.append(tot)
+            ups.append(dot(kdec, v_ref[rows, lanes]))
+            cons.append(dot(qdec, g_ref[rows, lanes]))
+            tots.append(jnp.broadcast_to(tot, (8, DH)))
         d0, d1 = jnp.exp(tots[0]), jnp.exp(tots[1])
-        up = d1 * ups[0] + ups[1]
-        con = cons[0] + d0 * cons[1]
+        up = d1[0:1] * ups[0] + ups[1]
+        con = cons[0] + d0[0:1] * cons[1]
         mine_ref[i, 0:DH, :] = jnp.where(first, up, con)
         send_ref[i, 0:DH, :] = jnp.where(first, con, up)
-        both = jnp.broadcast_to(d0 * d1, (8, DH))
-        mine_ref[i, DH:DH + 8, :] = both
-        send_ref[i, DH:DH + 8, :] = both
+        mine_ref[i, DH:DH + 8, :] = d0 * d1
+        send_ref[i, DH:DH + 8, :] = d0 * d1
         up_ref[i] = ups[0]
         con_ref[i] = cons[1]
-        dec_ref[i, 0:8, :] = jnp.broadcast_to(d0, (8, DH))
-        dec_ref[i, 8:16, :] = jnp.broadcast_to(d1, (8, DH))
+        dec_ref[i, 0:8, :] = d0
+        dec_ref[i, 8:16, :] = d1
 
 
 def combine_body(mine_ref, recv_ref, out_ref):
@@ -123,25 +126,38 @@
         state = decay * state + part
 
 
-def k2_body(q_ref, k_ref, v_ref, g_ref, ld_ref, wq_ref, wk_ref, qf_ref, kf_ref,
-            aq_ref, bq_ref, ak_ref, bk_ref, oi_ref, vi_ref, qd_ref, kd_ref):
+def k2_body(q_ref, k_ref, v_ref, g_ref, ld_ref, wq_ref, wk_ref,
+            aq_ref, bq_ref, ak_ref, bk_ref, oi_ref, vi_ref, qd_ref, kd_ref, qt_ref, kt_ref,
+            mark_ref, low_ref, cum_ref):
     step = pl.program_id(0)
-    low = lower3()
+
+    @pl.when(step == 0)
+    def _():
+        low_ref[...] = lower3()
+        for b in range(2):
+            rows = slice(b * BLOCK, (b + 1) * BLOCK)
+            cum_ref[:, rows] = cumul_rows(low_ref[...], ld_ref[:, rows])
+
     t = lax.broadcasted_iota(jnp.int32, (BLOCK, BLOCK), 0)
     s = lax.broadcasted_iota(jnp.int32, (BLOCK, BLOCK), 1)
     causal = s <= t
     for i in range(HPB):
         lanes = slice(i * DH, (i + 1) * DH)
-        for b in range(2):
-            rows = slice(b * BLOCK, (b + 1) * BLOCK)
-            row = ld_ref[pl.ds(step * HPB + i, 1), rows]
-            cum = cumul_cols(low, row)
-            across = cumul_rows(low, row)[0:1, :]
+        qt_ref[i] = q_ref[:, lanes].T
+        kt_ref[i] = k_ref[:, lanes].T
+        for b in range(2):
+            rows = slice(b * BLOCK, (b + 1) * BLOCK)
+            head = pl.ds(step * HPB + i, 1)
+            cum = cumul_cols(low_ref[...], ld_ref[head, rows])
+            across = cum_ref[head, rows]
             tot = cum[BLOCK - 1:BLOCK, :]
             wide = jnp.concatenate([cum, cum], axis=1)
             weights = jnp.exp(jnp.where(causal, wide - across, -1e9))
-            qf, kf = qf_ref[rows, lanes], kf_ref[rows, lanes]
             v, g = v_ref[rows, lanes], g_ref[rows, lanes]
+            pre_q = dot(q_ref[rows, lanes], wq_ref[i])
+            pre_k = dot(k_ref[rows, lanes], wk_ref[i])
+            sig_q, sig_k = sigmoid(pre_q), sigmoid(pre_k)
+            qf, kf = (pre_q * sig_q).astype(BF16), (pre_k * sig_k).astype(BF16)
             probs = (dot(qf, kf, NT) * weights).astype(BF16)
             grads = (dot(g, v, NT) * weights).astype(BF16)
             oi_ref[rows, lanes] = SCALE * dot(probs, v)
@@ -149,25 +165,23 @@
             early, late = jnp.exp(cum), jnp.exp(tot - cum)
             qd_ref[rows, lanes] = (qf.astype(F32) * early).astype(BF16)
             kd_ref[rows, lanes] = (kf.astype(F32) * late).astype(BF16)
-            pre_q = dot(q_ref[rows, lanes], wq_ref[i])
-            sig_q = sigmoid(pre_q)
             slope_q = SCALE * (sig_q * (1.0 + pre_q * (1.0 - sig_q)))
             aq_ref[rows, lanes] = dot(grads, kf) * slope_q
             bq_ref[rows, lanes] = early * slope_q
-            pre_k = dot(k_ref[rows, lanes], wk_ref[i])
-            sig_k = sigmoid(pre_k)
             slope_k = SCALE * (sig_k * (1.0 + pre_k * (1.0 - sig_k)))
             ak_ref[rows, lanes] = dot(grads, qf, TN) * slope_k
             bk_ref[rows, lanes] = late * slope_k
-
-
-def k3a_body(core, inc_ref, recv_ref, up_ref, con_ref, dec_ref, q_ref, k_ref, v_ref, g_ref,
+    mark_ref[...] = jnp.zeros((8, DH), F32)
+
+
+def k3a_body(core, inc_ref, recv_ref, up_ref, con_ref, dec_ref, qt_ref, kt_ref, v_ref, g_ref,
              aq_ref, bq_ref, ak_ref, bk_ref,
              gpq_ref, gpk_ref, st_ref, af_ref, mine_ref, send_ref):
     first = core[0] == 0
     for i in range(HPB):
         lanes = slice(i * DH, (i + 1) * DH)
-        inc, recv = inc_ref[i], recv_ref[i]
+        head = pl.program_id(0) * HPB + i
+        inc, recv = inc_ref[head], recv_ref[head]
         state = jnp.where(first, inc, recv)
         after = jnp.where(first, recv, inc)
         d0, d1 = dec_ref[i, 0:1, :], dec_ref[i, 8:9, :]
@@ -183,14 +197,15 @@
             gpk_ref[rows, lanes] = (
                 ak_ref[rows, lanes] + bk_ref[rows, lanes] * dot(v_ref[rows, lanes], afters[b], NT)
             ).astype(BF16)
-        part_q = dot(q_ref[:, lanes], gpq_ref[:, lanes], TN)
-        part_k = dot(k_ref[:, lanes], gpk_ref[:, lanes], TN)
+        part_q = dot(qt_ref[i], gpq_ref[:, lanes])
+        part_k = dot(kt_ref[i], gpk_ref[:, lanes])
         mine_ref[i] = jnp.where(first, part_q, part_k)
         send_ref[i] = jnp.where(first, part_k, part_q)
 
 
 def k3b_body(oi_ref, vi_ref, qd_ref, kd_ref, st_ref, af_ref, gpq_ref, gpk_ref, wq_ref, wk_ref,
-             out_ref, gq_ref, gk_ref, gv_ref):
+             out_ref, gq_ref, gk_ref, gv_ref, mark_ref):
+    mark_ref[...] = jnp.zeros((8, DH), F32)
     for i in range(HPB):
         lanes = slice(i * DH, (i + 1) * DH)
         for b in range(2):
@@ -213,10 +228,6 @@
         out_ref[k] = total
 
 
-def add_body(a_ref, b_ref, out_ref):
-    out_ref[...] = a_ref[...] + b_ref[...]
-
-
 def smem():
     return pl.BlockSpec(memory_space=pltpu.SMEM)
 
@@ -239,16 +250,34 @@
     return jax.ShapeDtypeStruct(dims, kind)
 
 
-def call(body, name, ins, outs, out_shapes, flops=0, grid=HEADS // HPB, after=0):
+def call(body, name, ins, outs, out_shapes, flops=0, grid=HEADS // HPB, after=0,
+         scratch=(), grant=None):
     return pl.pallas_call(
         lambda *refs: body(*refs[after:]),
         grid=(grid,),
         in_specs=[pl.BlockSpec(memory_space=pl.ANY)] * after + ins,
         out_specs=outs,
         out_shape=out_shapes,
+        scratch_shapes=scratch,
         name=name,
         cost_estimate=pl.CostEstimate(flops=flops, transcendentals=0, bytes_accessed=1 << 20),
-        compiler_params=pltpu.CompilerParams(dimension_semantics=("arbitrary",)),
+        compiler_params=pltpu.CompilerParams(
+            dimension_semantics=("arbitrary",), vmem_limit_bytes=grant
+        ),
+    )
+
+
+def small(body, name, ins, out_shape, out_spec, smem=0, after=0):
+    vmem = pl.BlockSpec(memory_space=pltpu.VMEM)
+    return pl.pallas_call(
+        lambda *refs: body(*refs[after:]),
+        grid=(1,),
+        in_specs=[pl.BlockSpec(memory_space=pl.ANY)] * after
+        + [pl.BlockSpec(memory_space=pltpu.SMEM)] * smem + [vmem] * ins,
+        out_specs=out_spec,
+        out_shape=out_shape,
+        name=name,
+        compiler_params=pltpu.CompilerParams(vmem_limit_bytes=8 << 20),
     )
 
 
@@ -273,62 +302,62 @@
     seqs = (q, k, v, g)
     ld_spec = whole(HEADS, TOK)
     map_specs = [per_head(DH, DH)] * 2
-    qf, kf, mine, send, up0, con1, dec = call(
+    mine, send, up0, con1, dec = call(
         k1_body, "k1",
         [smem()] + [seq()] * 4 + [ld_spec] + map_specs,
-        [seq(), seq(), per_head(DH + 8, DH), per_head(DH + 8, DH),
+        [per_head(DH + 8, DH), per_head(DH + 8, DH),
          per_head(DH, DH), per_head(DH, DH), per_head(16, DH)],
-        [SEQ_B, SEQ_B, shape((HEADS, DH + 8, DH)), shape((HEADS, DH + 8, DH)), MAT, MAT,
+        [shape((HEADS, DH + 8, DH)), shape((HEADS, DH + 8, DH)), MAT, MAT,
          shape((HEADS, 16, DH))],
+        scratch=[pltpu.VMEM((HEADS, TOK), F32)],
     )(core, *seqs, ld, *maps)
     recv = swap_cores(send)
-    packed = call(
-        combine_body, "combine",
-        [whole(HEADS, DH + 8, DH)] * 2, whole(CHIPS * (ROWS + 1), DH),
-        shape((CHIPS * (ROWS + 1), DH)), grid=1,
+    packed = small(
+        combine_body, "combine", 2, shape((CHIPS * (ROWS + 1), DH)), whole(CHIPS * (ROWS + 1), DH),
     )(mine, recv)
     swapped = exchange(packed.reshape(CHIPS, (ROWS + 1) * DH), ("z", "x"))
-    aq, bq, ak, bk, oi, vi, qd, kd = call(
+    aq, bq, ak, bk, oi, vi, qd, kd, qt, kt, mark = call(
         k2_body, "k2",
-        [seq()] * 4 + [ld_spec] + map_specs + [seq()] * 2,
-        [seq()] * 8,
-        [SEQ_F] * 6 + [SEQ_B] * 2,
+        [seq()] * 4 + [ld_spec] + map_specs,
+        [seq()] * 8 + [per_head(DH, TOK)] * 2 + [whole(8, DH)],
+        [SEQ_F] * 6 + [SEQ_B] * 2 + [shape((HEADS, DH, TOK), BF16)] * 2 + [shape((8, DH))],
         flops=1 << 30,
         after=1,
-    )(packed, *seqs, ld, *maps, qf, kf)
-    scanned = call(
-        scan_body, "scan",
-        [smem(), whole(CHIPS * (ROWS + 1), DH)], whole(CHIPS * ROWS, DH),
-        shape((CHIPS * ROWS, DH)), grid=1, after=1,
-    )(qd, core, swapped.reshape(CHIPS * (ROWS + 1), DH))
+        scratch=[pltpu.VMEM((BLOCK, 3 * BLOCK), BF16), pltpu.VMEM((HEADS, TOK), F32)],
+    )(packed, *seqs, ld, *maps)
+    scanned = small(
+        scan_body, "scan", 1, shape((CHIPS * ROWS, DH)), whole(CHIPS * ROWS, DH), smem=1, after=1,
+    )(mark, core, swapped.reshape(CHIPS * (ROWS + 1), DH))
     inc = exchange(scanned.reshape(CHIPS, ROWS * DH), ("z", "x")).reshape(HEADS, DH, DH)
     passed = mine[:, DH:DH + 1, :] * inc + mine[:, :DH, :]
     recv = swap_cores(passed)
     gpq, gpk, st, af, mine, send = call(
         k3a_body, "k3a",
-        [smem()] + [per_head(DH, DH)] * 4 + [per_head(16, DH)] + [seq()] * 8,
+        [smem()] + [pl.BlockSpec(memory_space=pltpu.VMEM)] * 2 + [per_head(DH, DH)] * 2
+        + [per_head(16, DH)] + [per_head(DH, TOK)] * 2 + [seq()] * 6,
         [seq(), seq(), per_head(2, DH, DH), per_head(2, DH, DH), per_head(DH, DH), per_head(DH, DH)],
         [SEQ_B, SEQ_B, shape((HEADS, 2, DH, DH), BF16), shape((HEADS, 2, DH, DH), BF16), MAT, MAT],
-    )(core, inc, recv, up0, con1, dec, *seqs, aq, bq, ak, bk)
+        grant=57 << 20,
+    )(core, inc, recv, up0, con1, dec, qt, kt, v, g, aq, bq, ak, bk)
     recv = swap_cores(send)
-    chip = call(add_body, "add", [whole(HEADS, DH, DH)] * 2, whole(HEADS, DH, DH), MAT, grid=1)(
-        mine, recv
-    )
+    chip = mine + recv
     pieces = exchange(chip.reshape(16, -1), ("x", "dp"))
     rows = HEADS * DH // 16
-    out, gq, gk, gv = call(
+    out, gq, gk, gv, mark = call(
         k3b_body, "k3b",
         [seq()] * 4 + [per_head(2, DH, DH)] * 2 + [seq()] * 2 + map_specs,
-        [seq()] * 4,
-        [SEQ_B] * 4,
+        [seq()] * 4 + [whole(8, DH)],
+        [SEQ_B] * 4 + [shape((8, DH))],
         flops=1 << 30,
         after=1,
     )(chip, oi, vi, qd, kd, st, af, gpq, gpk, *maps)
-    spread = call(spread_body, "spread_z", [whole(16, rows, DH)], whole(8, rows, DH),
-                  shape((8, rows, DH)), grid=1, after=1)(out, pieces.reshape(16, rows, DH))
+    spread = small(spread_body, "spread_z", 1, shape((8, rows, DH)), whole(8, rows, DH), after=1)(
+        mark, pieces.reshape(16, rows, DH)
+    )
     pieces = exchange(spread.reshape(8, -1), "z")
-    spread = call(spread_body, "spread_xy", [whole(8, rows, DH)], whole(16, rows, DH),
-                  shape((16, rows, DH)), grid=1)(pieces.reshape(8, rows, DH))
+    spread = small(spread_body, "spread_xy", 1, shape((16, rows, DH)), whole(16, rows, DH))(
+        pieces.reshape(8, rows, DH)
+    )
     own = exchange(spread.reshape(16, -1), ("x", "dp")).reshape(HEADS, DH, DH)
     other = swap_cores(own)
     first = core[0] == 0

time: 143 us -> 133 us (0.930)
  Pallas kernels: 48.2 us -> 38.5 us
  other arithmetic: 1.11 us -> 3.03 us
  blocking collectives: 26.9 us -> 25.1 us
    pallas_call x8 -> x7, Pallas kernels: 41.6 us -> 31.8 us  [the longest x1 14.1 us: local(): call(k2_body, 'k2', [seq()] * 4 + [ld_spec] + map_specs, [seq()] * 8 + [p...]
    add x0 -> x1, other arithmetic: none -> 1.92 us  [local(): chip = mine + recv]
    all_to_all x2, blocking collectives: 26.9 us -> 25.1 us  [exchange(): return lax.all_to_all(x, axes, 0, 0, tiled=True)]
    unnamed x14 -> x12, local copies, waits for them, and re-layouts: 3.99 us -> 3.22 us
  transfers between devices with their start and end apart: 7 -> 7, of which waited for: 7 -> 7; matrix products, arithmetic and copies ran while one was open for 0% -> 0% of each run, Pallas kernels for 14% -> 16%
where the time goes in v2:
time: 133 us; the launch traced here: 132 us
  Pallas kernels  38.5 us (29%)
  starting transfers between devices  33.2 us (25%)
  waiting for transfers between devices  28.4 us (21%)
  blocking collectives  25.1 us (19%)
  local copies, waits for them, and re-layouts  3.22 us (2%)
  other arithmetic  3.03 us (2%)
    all_to_all x2, blocking collectives, exchange(): return lax.all_to_all(x, axes, 0, 0, tiled=True)  25.1 us
    all_to_all x3, starting transfers between devices, exchange(): return lax.all_to_all(x, axes, 0, 0, tiled=True)  22 us
    all_to_all x3, waiting for transfers between devices, exchange(): return lax.all_to_all(x, axes, 0, 0, tiled=True)  21.8 us
    pallas_call x1, Pallas kernels, local(): call(k2_body, 'k2', [seq()] * 4 + [ld_spec] + map_specs, [seq()] * 8 + [p...  14.1 us
    ppermute x4, starting transfers between devices, swap_cores(): return lax.ppermute(x, 'c', [(0, 1), (1, 0)])  11.2 us
    pallas_call x1, Pallas kernels, local(): call(k3a_body, 'k3a', [smem()] + [pl.BlockSpec(memory_space=pltpu.VMEM)]...  8.95 us
    pallas_call x1, Pallas kernels, local(): call(k1_body, 'k1', [smem()] + [seq()] * 4 + [ld_spec] + map_specs, [per_...  6.86 us
    pallas_call x1, Pallas kernels, local(): call(k3b_body, 'k3b', [seq()] * 4 + [per_head(2, DH, DH)] * 2 + [seq()] *...  6.69 us
  transfers between devices with their start and end apart: 7, of which 7 were waited for; matrix products, arithmetic and copies ran while one was open for 0% of the time, Pallas kernels for 16%

profile of v2, /device:TPU:1, one launch (start us, length us, event | category | flops | bytes accessed | tf_op | source)
XLA Modules:
  0.0 132.1 jit_solution(13670981274968640634)
XLA Ops:
  0.6 6.9 %k1.1 = (f32[8,136,128]{2,1,0:T(8,128)}, f32[8,136,128]{2,1,0:T(8,128)}, f32[8,128,128]{2,1,0:T(8,128)}, f32[8,128,128]{2,1,0:T(8,128)}, f32[8,16,128]{2,1,0:T(8,128)}) custom-call(s32[1]{0:T(128)} %bitcast.refs_0_.refs_1_, bf16[512,1024]{1,0:T(8,128)(2,1)} %bitcast.39, bf16[512,1024]{1,0:T(8,128)(2,1)} %bitcast.41, bf16[512,1024]{1,0:T(8,128)(2,1)} %bitcast.31, ...), custom_call_target="tpu_custom_call" | custom-call | bytes 1048576 | tf_op jit(solution)/shard_map/k1/pallas_call | solution.py:305
  7.5 3.3 %collective-permute-start = (f32[8,136,128]{2,1,0:T(8,128)}, f32[8,136,128]{2,1,0:T(8,128)S(1)}, u32[]{:S(2)}, u32[]{:S(2)}) collective-permute-start(f32[8,136,128]{2,1,0:T(8,128)} %get-tuple-element.34), channel_id=1, source_target_pairs={{0,4},{4,0},{1,5},{5,1},{2,6},{6,2},{3,7},{7,3},{8,12},{12,8},{9,1... | collective-permute-start | bytes 1671176 | tf_op jit(solution)/shard_map/ppermute | solution.py:289
  10.8 1.8 %collective-permute-done.refs_1_ = f32[8,136,128]{2,1,0:T(8,128)S(1)} collective-permute-done((f32[8,136,128]{2,1,0:T(8,128)}, f32[8,136,128]{2,1,0:T(8,128)S(1)}, u32[]{:S(2)}, u32[]{:S(2)}) %collective-permute-start) | collective-permute-done | bytes 557088 | tf_op jit(solution)/shard_map/ppermute | solution.py:289
  12.6 0.0 copy-start
  12.6 1.1 copy-done
  13.6 0.9 combine.1.refs_0_
  14.5 9.3 %all-to-all-start = ((f32[32,1,4224]{2,1,0:T(1,128)}), f32[32,1,4224]{2,1,0:T(1,128)S(1)}, u32[]{:S(2)}, u32[]{:S(2)}) async-start(f32[32,1,4224]{2,1,0:T(1,128)} %bitcast.6), calls=%async_computation | async-start | bytes 1081344 | tf_op jit(solution)/shard_map/all_to_all | solution.py:285
  23.8 14.1 %k2.1 = (f32[512,1024]{1,0:T(8,128)}, f32[512,1024]{1,0:T(8,128)}, f32[512,1024]{1,0:T(8,128)}, f32[512,1024]{1,0:T(8,128)}, f32[512,1024]{1,0:T(8,128)}, /*inde...) custom-call(f32[1056,128]{1,0:T(8,128)} %combine.1.refs_0_, ...), custom_call_target="tpu_custom_call" | custom-call | flops 1073741824 | bytes 1048576 | tf_op jit(solution)/shard_map/k2/pallas_call | solution.py:319
  38.0 0.0 copy-start.1
  38.0 2.7 %all-to-all-done = f32[32,1,4224]{2,1,0:T(1,128)S(1)} async-done(((f32[32,1,4224]{2,1,0:T(1,128)}), f32[32,1,4224]{2,1,0:T(1,128)S(1)}, u32[]{:S(2)}, u32[]{:S(2)}) %all-to-all-start) | async-done | bytes 540704 | tf_op jit(solution)/shard_map/all_to_all | solution.py:285
  40.7 0.0 copy-start.3
  40.7 0.7 copy-done.3
  41.4 0.9 scan.1
  42.3 6.6 %all-to-all-start.1 = ((f32[32,1,4096]{2,1,0:T(1,128)}), f32[32,1,4096]{2,1,0:T(1,128)S(1)}, u32[]{:S(2)}, u32[]{:S(2)}) async-start(f32[32,1,4096]{2,1,0:T(1,128)} %bitcast.8), calls=%async_computation.1 | async-start | bytes 1048576 | tf_op jit(solution)/shard_map/all_to_all | solution.py:285
  48.9 0.0 copy-done.1
  48.9 15.4 %all-to-all-done.1 = f32[32,1,4096]{2,1,0:T(1,128)S(1)} async-done(((f32[32,1,4096]{2,1,0:T(1,128)}), f32[32,1,4096]{2,1,0:T(1,128)S(1)}, u32[]{:S(2)}, u32[]{:S(2)}) %all-to-all-start.1) | async-done | bytes 524320 | tf_op jit(solution)/shard_map/all_to_all | solution.py:285
  64.3 0.0 copy-start.4
  64.3 0.1 slice_add_fusion
  64.3 3.4 %collective-permute-start.1 = (f32[8,128,128]{2,1,0:T(8,128)S(1)}, f32[8,128,128]{2,1,0:T(8,128)S(1)}, u32[]{:S(2)}, u32[]{:S(2)}) collective-permute-start(f32[8,128,128]{2,1,0:T(8,128)S(1)} %slice_add_fusion), channel_id=1, source_target_pairs={{0,4},{4,0},{1,5},{5,1},{2,6},{6,2},{3,7},{7,3},{8,12},{12,8},{9,1... | collective-permute-start | bytes 1572872 | tf_op jit(solution)/shard_map/ppermute | solution.py:289
  67.7 1.5 %collective-permute-done.1.refs_2_ = f32[8,128,128]{2,1,0:T(8,128)S(1)} collective-permute-done((f32[8,128,128]{2,1,0:T(8,128)S(1)}, f32[8,128,128]{2,1,0:T(8,128)S(1)}, u32[]{:S(2)}, u32[]{:S(2)}) %collective-permute-start.1) | collective-permute-done | bytes 524320 | tf_op jit(solution)/shard_map/ppermute | solution.py:289
  69.2 0.0 copy-start.5
  69.3 0.0 copy-done.4
  69.3 0.8 copy-done.5
  70.0 8.9 %k3a.1 = (bf16[512,1024]{1,0:T(8,128)(2,1)}, bf16[512,1024]{1,0:T(8,128)(2,1)}, bf16[8,2,128,128]{3,2,1,0:T(8,128)(2,1)}, bf16[8,2,128,128]{3,2,1,0:T(8,128)(2,1...) custom-call(s32[1]{0:T(128)} %bitcast.refs_0_.refs_1_, f32[8,128,128]{2,1,0:T(8,128)} %bitcast.38, ...), custom_call_target="tpu_custom_call" | custom-call | bytes 1048576 | tf_op jit(solution)/shard_map/k3a/pallas_call | solution.py:334
  79.0 0.5 collective-permute-start.2
  79.5 1.7 %collective-permute-done.2 = f32[8,128,128]{2,1,0:T(8,128)S(1)} collective-permute-done((f32[8,128,128]{2,1,0:T(8,128)}, f32[8,128,128]{2,1,0:T(8,128)S(1)}, u32[]{:S(2)}, u32[]{:S(2)}) %collective-permute-start.2) | collective-permute-done | bytes 524320 | tf_op jit(solution)/shard_map/ppermute | solution.py:289
  81.2 1.9 %add.7.refs_0_ = f32[8,128,128]{2,1,0:T(8,128)} add(f32[8,128,128]{2,1,0:T(8,128)} %get-tuple-element.45, f32[8,128,128]{2,1,0:T(8,128)S(1)} %collective-permute-done.2) | non-fusion elementwise | flops 131072 | bytes 1572864 | tf_op jit(solution)/shard_map/add | solution.py:343
  83.1 6.1 %all-to-all-start.2 = ((f32[16,1,8192]{2,1,0:T(1,128)}), f32[16,1,8192]{2,1,0:T(1,128)S(1)}, u32[]{:S(2)}, u32[]{:S(2)}) async-start(f32[16,1,8192]{2,1,0:T(1,128)} %bitcast.15), calls=%async_computation.2 | async-start | bytes 1048576 | tf_op jit(solution)/shard_map/all_to_all | solution.py:285
  89.2 6.7 %k3b.1 = (bf16[512,1024]{1,0:T(8,128)(2,1)}, bf16[512,1024]{1,0:T(8,128)(2,1)}, bf16[512,1024]{1,0:T(8,128)(2,1)}, bf16[512,1024]{1,0:T(8,128)(2,1)}, f32[8,128]{1,0:T(8,128)}) custom-call(f32[8,128,128]{2,1,0:T(8,128)} %add.7.refs_0_, f32[512,1024]{1,0:T(8,128)} %get-tuple-element.47.refs_1_, f32[512,1024]{1,0:T(8,128)} %get-tuple-element.48.refs_2_, ...), custom_call_target="tpu_custom_call" | custom-call | flops 1073741824 | bytes 1048576 | tf_op jit(solution)/shard_map/k3b/pallas_call | solution.py:346
  95.9 3.7 %all-to-all-done.2 = f32[16,1,8192]{2,1,0:T(1,128)S(1)} async-done(((f32[16,1,8192]{2,1,0:T(1,128)}), f32[16,1,8192]{2,1,0:T(1,128)S(1)}, u32[]{:S(2)}, u32[]{:S(2)}) %all-to-all-start.2) | async-done | bytes 524320 | tf_op jit(solution)/shard_map/all_to_all | solution.py:285
  99.6 0.0 copy-start.2
  99.6 0.7 copy-done.2
  100.3 11.6 %all_to_all.45 = f32[8,1,8192]{2,1,0:T(1,128)S(1)} all-to-all(f32[8,1,8192]{2,1,0:T(1,128)S(1)} %bitcast.29), channel_id=1, replica_groups=mesh['z'=8,'x'=4,'c'=2,'dp'=4] {'z'}, dimensions={0} | all-to-all | bytes 524288 | tf_op jit(solution)/shard_map/all_to_all | solution.py:285
  112.0 0.1 spread_xy.1
  112.0 13.4 %all_to_all.46 = f32[16,1,8192]{2,1,0:T(1,128)S(1)} all-to-all(f32[16,1,8192]{2,1,0:T(1,128)S(1)} %bitcast.28), channel_id=1, replica_groups=mesh['z'=8,'x'=4,'c'=2,'dp'=4] {'x','dp'}, dimensions={0} | all-to-all | bytes 1048576 | tf_op jit(solution)/shard_map/all_to_all | solution.py:285
  125.5 4.1 %collective-permute-start.3 = (f32[8,128,128]{2,1,0:T(8,128)S(1)}, f32[8,128,128]{2,1,0:T(8,128)S(1)}, u32[]{:S(2)}, u32[]{:S(2)}) collective-permute-start(f32[8,128,128]{2,1,0:T(8,128)S(1)} %bitcast.43), channel_id=1, source_target_pairs={{0,4},{4,0},{1,5},{5,1},{2,6},{6,2},{3,7},{7,3},{8,12},{12,8},{9,1... | collective-permute-start | bytes 1572872 | tf_op jit(solution)/shard_map/ppermute | solution.py:289
  129.5 1.5 %collective-permute-done.3 = f32[8,128,128]{2,1,0:T(8,128)S(1)} collective-permute-done((f32[8,128,128]{2,1,0:T(8,128)S(1)}, f32[8,128,128]{2,1,0:T(8,128)S(1)}, u32[]{:S(2)}, u32[]{:S(2)}) %collective-permute-start.3) | collective-permute-done | bytes 524320 | tf_op jit(solution)/shard_map/ppermute | solution.py:289
  131.1 1.1 broadcast_select_fusion
  (2 shorter events, 0.0 us)
Async XLA Ops:
  7.5 5.1 %collective-permute-start = (f32[8,136,128]{2,1,0:T(8,128)}, f32[8,136,128]{2,1,0:T(8,128)S(1)}, u32[]{:S(2)}, u32[]{:S(2)}) collective-permute-start(f32[8,136,128]{2,1,0:T(8,128)} %get-tuple-element.34), channel_id=1, source_target_pairs={{0,4},{4,0},{1,5},{5,1},{2,6},{6,2},{3,7},{7,3},{8,12},{12,8},{9,1... | collective-permute-start | bytes 1671176 | tf_op jit(solution)/shard_map/ppermute | solution.py:289
  12.6 1.1 copy-start
  14.5 26.2 %all-to-all-start = ((f32[32,1,4224]{2,1,0:T(1,128)}), f32[32,1,4224]{2,1,0:T(1,128)S(1)}, u32[]{:S(2)}, u32[]{:S(2)}) async-start(f32[32,1,4224]{2,1,0:T(1,128)} %bitcast.6), calls=%async_computation | async-start | bytes 1081344 | tf_op jit(solution)/shard_map/all_to_all | solution.py:285
  38.0 10.9 %copy-start.1 = (f32[8,136,128]{2,1,0:T(8,128)S(1)}, f32[8,136,128]{2,1,0:T(8,128)}, u32[]{:S(2)}) copy-start(f32[8,136,128]{2,1,0:T(8,128)} %get-tuple-element.33.refs_0_) | copy-start | bytes 1671172
  40.7 0.7 copy-start.3
  42.3 22.0 %all-to-all-start.1 = ((f32[32,1,4096]{2,1,0:T(1,128)}), f32[32,1,4096]{2,1,0:T(1,128)S(1)}, u32[]{:S(2)}, u32[]{:S(2)}) async-start(f32[32,1,4096]{2,1,0:T(1,128)} %bitcast.8), calls=%async_computation.1 | async-start | bytes 1048576 | tf_op jit(solution)/shard_map/all_to_all | solution.py:285
  64.3 5.0 %copy-start.4 = (f32[32,1,4096]{2,1,0:T(1,128)}, f32[32,1,4096]{2,1,0:T(1,128)S(1)}, u32[]{:S(2)}) copy-start(f32[32,1,4096]{2,1,0:T(1,128)S(1)} %all-to-all-done.1) | copy-start | bytes 1572868
  64.3 4.9 %collective-permute-start.1 = (f32[8,128,128]{2,1,0:T(8,128)S(1)}, f32[8,128,128]{2,1,0:T(8,128)S(1)}, u32[]{:S(2)}, u32[]{:S(2)}) collective-permute-start(f32[8,128,128]{2,1,0:T(8,128)S(1)} %slice_add_fusion), channel_id=1, source_target_pairs={{0,4},{4,0},{1,5},{5,1},{2,6},{6,2},{3,7},{7,3},{8,12},{12,8},{9,1... | collective-permute-start | bytes 1572872 | tf_op jit(solution)/shard_map/ppermute | solution.py:289
  69.2 0.8 copy-start.5
  79.0 2.2 %collective-permute-start.2 = (f32[8,128,128]{2,1,0:T(8,128)}, f32[8,128,128]{2,1,0:T(8,128)S(1)}, u32[]{:S(2)}, u32[]{:S(2)}) collective-permute-start(f32[8,128,128]{2,1,0:T(8,128)} %get-tuple-element.46), channel_id=1, source_target_pairs={{0,4},{4,0},{1,5},{5,1},{2,6},{6,2},{3,7},{7,3},{8,12},{12,8},{9,1... | collective-permute-start | bytes 1572872 | tf_op jit(solution)/shard_map/ppermute | solution.py:289
  83.1 16.5 %all-to-all-start.2 = ((f32[16,1,8192]{2,1,0:T(1,128)}), f32[16,1,8192]{2,1,0:T(1,128)S(1)}, u32[]{:S(2)}, u32[]{:S(2)}) async-start(f32[16,1,8192]{2,1,0:T(1,128)} %bitcast.15), calls=%async_computation.2 | async-start | bytes 1048576 | tf_op jit(solution)/shard_map/all_to_all | solution.py:285
  99.6 0.7 copy-start.2
  125.5 5.6 %collective-permute-start.3 = (f32[8,128,128]{2,1,0:T(8,128)S(1)}, f32[8,128,128]{2,1,0:T(8,128)S(1)}, u32[]{:S(2)}, u32[]{:S(2)}) collective-permute-start(f32[8,128,128]{2,1,0:T(8,128)S(1)} %bitcast.43), channel_id=1, source_target_pairs={{0,4},{4,0},{1,5},{5,1},{2,6},{6,2},{3,7},{7,3},{8,12},{12,8},{9,1... | collective-permute-start | bytes 1572872 | tf_op jit(solution)/shard_map/ppermute | solution.py:289

commit v3 on v2

--- a/solution.py
+++ b/solution.py
@@ -126,7 +126,7 @@
         state = decay * state + part
 
 
-def k2_body(q_ref, k_ref, v_ref, g_ref, ld_ref, wq_ref, wk_ref,
+def k2_body(core, q_ref, k_ref, v_ref, g_ref, ld_ref, wq_ref, wk_ref,
             aq_ref, bq_ref, ak_ref, bk_ref, oi_ref, vi_ref, qd_ref, kd_ref, qt_ref, kt_ref,
             mark_ref, low_ref, cum_ref):
     step = pl.program_id(0)
@@ -160,64 +160,76 @@
             qf, kf = (pre_q * sig_q).astype(BF16), (pre_k * sig_k).astype(BF16)
             probs = (dot(qf, kf, NT) * weights).astype(BF16)
             grads = (dot(g, v, NT) * weights).astype(BF16)
-            oi_ref[rows, lanes] = SCALE * dot(probs, v)
-            vi_ref[rows, lanes] = SCALE * dot(probs, g, TN)
+            oi_ref[i, rows] = SCALE * dot(probs, v)
+            vi_ref[i, rows] = SCALE * dot(probs, g, TN)
             early, late = jnp.exp(cum), jnp.exp(tot - cum)
-            qd_ref[rows, lanes] = (qf.astype(F32) * early).astype(BF16)
-            kd_ref[rows, lanes] = (kf.astype(F32) * late).astype(BF16)
+            qd_ref[i, rows] = (qf.astype(F32) * early).astype(BF16)
+            kd_ref[i, rows] = (kf.astype(F32) * late).astype(BF16)
             slope_q = SCALE * (sig_q * (1.0 + pre_q * (1.0 - sig_q)))
-            aq_ref[rows, lanes] = dot(grads, kf) * slope_q
-            bq_ref[rows, lanes] = early * slope_q
+            aq_ref[i, rows] = (dot(grads, kf) * slope_q).astype(BF16)
+            bq_ref[i, rows] = (early * slope_q).astype(BF16)
             slope_k = SCALE * (sig_k * (1.0 + pre_k * (1.0 - sig_k)))
-            ak_ref[rows, lanes] = dot(grads, qf, TN) * slope_k
-            bk_ref[rows, lanes] = late * slope_k
-    mark_ref[...] = jnp.zeros((8, DH), F32)
-
-
-def k3a_body(core, inc_ref, recv_ref, up_ref, con_ref, dec_ref, qt_ref, kt_ref, v_ref, g_ref,
-             aq_ref, bq_ref, ak_ref, bk_ref,
-             gpq_ref, gpk_ref, st_ref, af_ref, mine_ref, send_ref):
+            ak_ref[i, rows] = (dot(grads, qf, TN) * slope_k).astype(BF16)
+            bk_ref[i, rows] = (late * slope_k).astype(BF16)
+    mark_ref[0] = core[0]
+
+
+def states_body(core, inc_ref, recv_ref, up_ref, con_ref, dec_ref, st_ref, af_ref):
+    first = core[0] == 0
+    for h in range(HEADS):
+        inc, recv = inc_ref[h], recv_ref[h]
+        state = jnp.where(first, inc, recv)
+        after = jnp.where(first, recv, inc)
+        st_ref[h, 0] = state.astype(BF16)
+        st_ref[h, 1] = (dec_ref[h, 0:1, :] * state + up_ref[h]).astype(BF16)
+        af_ref[h, 0] = (con_ref[h] + dec_ref[h, 8:9, :] * after).astype(BF16)
+        af_ref[h, 1] = after.astype(BF16)
+
+
+def k3a_body(core, st_ref, af_ref, qt_ref, kt_ref, v_ref, g_ref,
+             aq_ref, bq_ref, ak_ref, bk_ref, gpq_ref, gpk_ref, mine_ref, send_ref):
     first = core[0] == 0
     for i in range(HPB):
         lanes = slice(i * DH, (i + 1) * DH)
-        head = pl.program_id(0) * HPB + i
-        inc, recv = inc_ref[head], recv_ref[head]
-        state = jnp.where(first, inc, recv)
-        after = jnp.where(first, recv, inc)
-        d0, d1 = dec_ref[i, 0:1, :], dec_ref[i, 8:9, :]
-        states = [state.astype(BF16), (d0 * state + up_ref[i]).astype(BF16)]
-        afters = [(con_ref[i] + d1 * after).astype(BF16), after.astype(BF16)]
-        for b in range(2):
-            rows = slice(b * BLOCK, (b + 1) * BLOCK)
-            st_ref[i, b] = states[b]
-            af_ref[i, b] = afters[b]
-            gpq_ref[rows, lanes] = (
-                aq_ref[rows, lanes] + bq_ref[rows, lanes] * dot(g_ref[rows, lanes], states[b], NT)
+        for b in range(2):
+            rows = slice(b * BLOCK, (b + 1) * BLOCK)
+            from_state = dot(g_ref[rows, lanes], st_ref[i, b], NT)
+            from_after = dot(v_ref[rows, lanes], af_ref[i, b], NT)
+            gpq_ref[i, rows] = (
+                aq_ref[i, rows].astype(F32) + bq_ref[i, rows].astype(F32) * from_state
             ).astype(BF16)
-            gpk_ref[rows, lanes] = (
-                ak_ref[rows, lanes] + bk_ref[rows, lanes] * dot(v_ref[rows, lanes], afters[b], NT)
+            gpk_ref[i, rows] = (
+                ak_ref[i, rows].astype(F32) + bk_ref[i, rows].astype(F32) * from_after
             ).astype(BF16)
-        part_q = dot(qt_ref[i], gpq_ref[:, lanes])
-        part_k = dot(kt_ref[i], gpk_ref[:, lanes])
+        part_q = dot(qt_ref[i], gpq_ref[i])
+        part_k = dot(kt_ref[i], gpk_ref[i])
         mine_ref[i] = jnp.where(first, part_q, part_k)
         send_ref[i] = jnp.where(first, part_k, part_q)
 
 
-def k3b_body(oi_ref, vi_ref, qd_ref, kd_ref, st_ref, af_ref, gpq_ref, gpk_ref, wq_ref, wk_ref,
+def k3b_body(core, oi_ref, vi_ref, qd_ref, kd_ref, st_ref, af_ref, gpq_ref, gpk_ref, wq_ref, wk_ref,
              out_ref, gq_ref, gk_ref, gv_ref, mark_ref):
-    mark_ref[...] = jnp.zeros((8, DH), F32)
+    mark_ref[0] = core[0]
     for i in range(HPB):
         lanes = slice(i * DH, (i + 1) * DH)
         for b in range(2):
             rows = slice(b * BLOCK, (b + 1) * BLOCK)
             out_ref[rows, lanes] = (
-                oi_ref[rows, lanes] + SCALE * dot(qd_ref[rows, lanes], st_ref[i, b])
+                oi_ref[i, rows] + SCALE * dot(qd_ref[i, rows], st_ref[i, b])
             ).astype(BF16)
             gv_ref[rows, lanes] = (
-                vi_ref[rows, lanes] + SCALE * dot(kd_ref[rows, lanes], af_ref[i, b])
+                vi_ref[i, rows] + SCALE * dot(kd_ref[i, rows], af_ref[i, b])
             ).astype(BF16)
-            gq_ref[rows, lanes] = dot(gpq_ref[rows, lanes], wq_ref[i], NT).astype(BF16)
-            gk_ref[rows, lanes] = dot(gpk_ref[rows, lanes], wk_ref[i], NT).astype(BF16)
+            gq_ref[rows, lanes] = dot(gpq_ref[i, rows], wq_ref[i], NT).astype(BF16)
+            gk_ref[rows, lanes] = dot(gpk_ref[i, rows], wk_ref[i], NT).astype(BF16)
+
+
+def add_body(a_ref, b_ref, out_ref):
+    out_ref[...] = a_ref[...] + b_ref[...]
+
+
+def spread_first_body(core, in_ref, out_ref):
+    spread_body(in_ref, out_ref)
 
 
 def spread_body(in_ref, out_ref):
@@ -255,7 +267,7 @@
     return pl.pallas_call(
         lambda *refs: body(*refs[after:]),
         grid=(grid,),
-        in_specs=[pl.BlockSpec(memory_space=pl.ANY)] * after + ins,
+        in_specs=[pl.BlockSpec(memory_space=pltpu.HBM)] * after + ins,
         out_specs=outs,
         out_shape=out_shapes,
         scratch_shapes=scratch,
@@ -272,7 +284,7 @@
     return pl.pallas_call(
         lambda *refs: body(*refs[after:]),
         grid=(1,),
-        in_specs=[pl.BlockSpec(memory_space=pl.ANY)] * after
+        in_specs=[pl.BlockSpec(memory_space=pltpu.HBM)] * after
         + [pl.BlockSpec(memory_space=pltpu.SMEM)] * smem + [vmem] * ins,
         out_specs=out_spec,
         out_shape=out_shape,
@@ -292,6 +304,8 @@
 SEQ_B = shape((TOK, HEADS * DH), BF16)
 SEQ_F = shape((TOK, HEADS * DH), F32)
 MAT = shape((HEADS, DH, DH), F32)
+HELD_F = shape((HEADS, TOK, DH), F32)
+HELD_B = shape((HEADS, TOK, DH), BF16)
 
 
 def local(query, key, value, log_decay, grad_out, query_map, key_map):
@@ -314,44 +328,48 @@
     recv = swap_cores(send)
     packed = small(
         combine_body, "combine", 2, shape((CHIPS * (ROWS + 1), DH)), whole(CHIPS * (ROWS + 1), DH),
-    )(mine, recv)
+    )(pltpu.with_memory_space_constraint(mine, pltpu.HBM), recv)
     swapped = exchange(packed.reshape(CHIPS, (ROWS + 1) * DH), ("z", "x"))
     aq, bq, ak, bk, oi, vi, qd, kd, qt, kt, mark = call(
         k2_body, "k2",
-        [seq()] * 4 + [ld_spec] + map_specs,
-        [seq()] * 8 + [per_head(DH, TOK)] * 2 + [whole(8, DH)],
-        [SEQ_F] * 6 + [SEQ_B] * 2 + [shape((HEADS, DH, TOK), BF16)] * 2 + [shape((8, DH))],
+        [smem()] + [seq()] * 4 + [ld_spec] + map_specs,
+        [per_head(TOK, DH)] * 8 + [per_head(DH, TOK)] * 2 + [smem()],
+        [HELD_B] * 4 + [HELD_F] * 2 + [HELD_B] * 2 + [shape((HEADS, DH, TOK), BF16)] * 2
+        + [shape((1,), jnp.int32)],
         flops=1 << 30,
         after=1,
         scratch=[pltpu.VMEM((BLOCK, 3 * BLOCK), BF16), pltpu.VMEM((HEADS, TOK), F32)],
-    )(packed, *seqs, ld, *maps)
+    )(packed, core, *seqs, ld, *maps)
     scanned = small(
-        scan_body, "scan", 1, shape((CHIPS * ROWS, DH)), whole(CHIPS * ROWS, DH), smem=1, after=1,
-    )(mark, core, swapped.reshape(CHIPS * (ROWS + 1), DH))
+        scan_body, "scan", 1, shape((CHIPS * ROWS, DH)), whole(CHIPS * ROWS, DH), smem=1,
+    )(mark, swapped.reshape(CHIPS * (ROWS + 1), DH))
     inc = exchange(scanned.reshape(CHIPS, ROWS * DH), ("z", "x")).reshape(HEADS, DH, DH)
     passed = mine[:, DH:DH + 1, :] * inc + mine[:, :DH, :]
     recv = swap_cores(passed)
-    gpq, gpk, st, af, mine, send = call(
+    st, af = small(
+        states_body, "states", 5, [pltpu.HBM((HEADS, 2, DH, DH), BF16)] * 2,
+        [whole(HEADS, 2, DH, DH)] * 2, smem=1,
+    )(core, inc, recv, up0, con1, dec)
+    gpq, gpk, mine, send = call(
         k3a_body, "k3a",
-        [smem()] + [pl.BlockSpec(memory_space=pltpu.VMEM)] * 2 + [per_head(DH, DH)] * 2
-        + [per_head(16, DH)] + [per_head(DH, TOK)] * 2 + [seq()] * 6,
-        [seq(), seq(), per_head(2, DH, DH), per_head(2, DH, DH), per_head(DH, DH), per_head(DH, DH)],
-        [SEQ_B, SEQ_B, shape((HEADS, 2, DH, DH), BF16), shape((HEADS, 2, DH, DH), BF16), MAT, MAT],
-        grant=57 << 20,
-    )(core, inc, recv, up0, con1, dec, qt, kt, v, g, aq, bq, ak, bk)
+        [smem()] + [per_head(2, DH, DH)] * 2 + [per_head(DH, TOK)] * 2 + [seq()] * 2
+        + [per_head(TOK, DH)] * 4,
+        [per_head(TOK, DH)] * 2 + [per_head(DH, DH)] * 2,
+        [HELD_B] * 2 + [MAT, MAT],
+    )(core, st, af, qt, kt, v, g, aq, bq, ak, bk)
     recv = swap_cores(send)
-    chip = mine + recv
+    chip = small(add_body, "add", 2, MAT, whole(HEADS, DH, DH))(pltpu.with_memory_space_constraint(mine, pltpu.HBM), recv)
     pieces = exchange(chip.reshape(16, -1), ("x", "dp"))
     rows = HEADS * DH // 16
     out, gq, gk, gv, mark = call(
         k3b_body, "k3b",
-        [seq()] * 4 + [per_head(2, DH, DH)] * 2 + [seq()] * 2 + map_specs,
-        [seq()] * 4 + [whole(8, DH)],
-        [SEQ_B] * 4 + [shape((8, DH))],
+        [smem()] + [per_head(TOK, DH)] * 4 + [per_head(2, DH, DH)] * 2 + [per_head(TOK, DH)] * 2 + map_specs,
+        [seq()] * 4 + [smem()],
+        [SEQ_B] * 4 + [shape((1,), jnp.int32)],
         flops=1 << 30,
         after=1,
-    )(chip, oi, vi, qd, kd, st, af, gpq, gpk, *maps)
-    spread = small(spread_body, "spread_z", 1, shape((8, rows, DH)), whole(8, rows, DH), after=1)(
+    )(chip, core, oi, vi, qd, kd, st, af, gpq, gpk, *maps)
+    spread = small(spread_first_body, "spread_z", 1, shape((8, rows, DH)), whole(8, rows, DH), smem=1)(
         mark, pieces.reshape(16, rows, DH)
     )
     pieces = exchange(spread.reshape(8, -1), "z")

time: 133 us -> 131 us (0.985)
  local copies, waits for them, and re-layouts: 3.22 us -> 0.03 us
  Pallas kernels: 38.5 us -> 41 us
  other arithmetic: 3.03 us -> 1.11 us
    unnamed x12 -> x8, local copies, waits for them, and re-layouts: 3.22 us -> 0.02 us
    add x1 -> x0, other arithmetic: 1.92 us -> none  [local(): chip = mine + recv]
    pallas_call x4 -> x6, Pallas kernels: 29.8 us -> 30.6 us  [the longest x1 13.8 us: local(): call(k2_body, 'k2', [smem()] + [seq()] * 4 + [ld_spec] + map_specs, [per_...]
where the time goes in v3:
time: 131 us; the launch traced here: 130 us
  Pallas kernels  41 us (31%)
  starting transfers between devices  32.9 us (25%)
  waiting for transfers between devices  28.9 us (22%)
  blocking collectives  25.1 us (19%)
    all_to_all x2, blocking collectives, exchange(): return lax.all_to_all(x, axes, 0, 0, tiled=True)  25.1 us
    all_to_all x3, waiting for transfers between devices, exchange(): return lax.all_to_all(x, axes, 0, 0, tiled=True)  22.2 us
    all_to_all x3, starting transfers between devices, exchange(): return lax.all_to_all(x, axes, 0, 0, tiled=True)  21.8 us
    pallas_call x1, Pallas kernels, local(): call(k2_body, 'k2', [smem()] + [seq()] * 4 + [ld_spec] + map_specs, [per_...  13.8 us
    ppermute x4, starting transfers between devices, swap_cores(): return lax.ppermute(x, 'c', [(0, 1), (1, 0)])  11.2 us
    pallas_call x1, Pallas kernels, local(): call(k1_body, 'k1', [smem()] + [seq()] * 4 + [ld_spec] + map_specs, [per_...  6.84 us
    ppermute x4, waiting for transfers between devices, swap_cores(): return lax.ppermute(x, 'c', [(0, 1), (1, 0)])  6.62 us
    pallas_call x1, Pallas kernels, local(): call(k3a_body, 'k3a', [smem()] + [per_head(2, DH, DH)] * 2 + [per_head(DH...  6.6 us
  transfers between devices with their start and end apart: 7, of which 7 were waited for; matrix products, arithmetic and copies ran while one was open for 0% of the time, Pallas kernels for 16%

profile of v3, /device:TPU:1, one launch (start us, length us, event | category | flops | bytes accessed | tf_op | source)
XLA Modules:
  0.0 129.8 jit_solution(11022545459734974361)
XLA Ops:
  0.6 6.8 %k1.1 = (f32[8,136,128]{2,1,0:T(8,128)}, f32[8,136,128]{2,1,0:T(8,128)}, f32[8,128,128]{2,1,0:T(8,128)}, f32[8,128,128]{2,1,0:T(8,128)}, f32[8,16,128]{2,1,0:T(8,128)}) custom-call(s32[1]{0:T(128)} %bitcast.refs_0_.refs_1_, bf16[512,1024]{1,0:T(8,128)(2,1)} %bitcast.39, bf16[512,1024]{1,0:T(8,128)(2,1)} %bitcast.41, bf16[512,1024]{1,0:T(8,128)(2,1)} %bitcast.33, ...), custom_call_target="tpu_custom_call" | custom-call | bytes 1048576 | tf_op jit(solution)/shard_map/k1/pallas_call | solution.py:319
  7.5 3.3 %collective-permute-start = (f32[8,136,128]{2,1,0:T(8,128)}, f32[8,136,128]{2,1,0:T(8,128)S(1)}, u32[]{:S(2)}, u32[]{:S(2)}) collective-permute-start(f32[8,136,128]{2,1,0:T(8,128)} %get-tuple-element.34), channel_id=1, source_target_pairs={{0,4},{4,0},{1,5},{5,1},{2,6},{6,2},{3,7},{7,3},{8,12},{12,8},{9,1... | collective-permute-start | bytes 1671176 | tf_op jit(solution)/shard_map/ppermute | solution.py:301
  10.8 1.8 %collective-permute-done.refs_1_ = f32[8,136,128]{2,1,0:T(8,128)S(1)} collective-permute-done((f32[8,136,128]{2,1,0:T(8,128)}, f32[8,136,128]{2,1,0:T(8,128)S(1)}, u32[]{:S(2)}, u32[]{:S(2)}) %collective-permute-start) | collective-permute-done | bytes 557088 | tf_op jit(solution)/shard_map/ppermute | solution.py:301
  12.6 1.9 %combine.1.refs_0_ = f32[1056,128]{1,0:T(8,128)} custom-call(f32[8,136,128]{2,1,0:T(8,128)} %get-tuple-element.33.refs_0_, f32[8,136,128]{2,1,0:T(8,128)S(1)} %collective-permute-done.refs_1_), custom_call_target="tpu_custom_call" | custom-call | tf_op jit(solution)/shard_map/combine/pallas_call | solution.py:329
  14.5 9.3 %all-to-all-start = ((f32[32,1,4224]{2,1,0:T(1,128)}), f32[32,1,4224]{2,1,0:T(1,128)S(1)}, u32[]{:S(2)}, u32[]{:S(2)}) async-start(f32[32,1,4224]{2,1,0:T(1,128)} %bitcast.6), calls=%async_computation | async-start | bytes 1081344 | tf_op jit(solution)/shard_map/all_to_all | solution.py:297
  23.8 13.8 %k2.1 = (bf16[8,512,128]{2,1,0:T(8,128)(2,1)}, bf16[8,512,128]{2,1,0:T(8,128)(2,1)}, bf16[8,512,128]{2,1,0:T(8,128)(2,1)}, bf16[8,512,128]{2,1,0:T(8,128)(2,1)},...) custom-call(f32[1056,128]{1,0:T(8,128)} %combine.1.refs_0_, ...), custom_call_target="tpu_custom_call" | custom-call | flops 1073741824 | bytes 1048576 | tf_op jit(solution)/shard_map/k2/pallas_call | solution.py:333
  37.6 0.0 copy-start.3
  37.6 0.0 copy-start
  37.6 0.0 copy-start.1
  37.6 0.0 copy-start.2
  37.7 3.0 %all-to-all-done = f32[32,1,4224]{2,1,0:T(1,128)S(1)} async-done(((f32[32,1,4224]{2,1,0:T(1,128)}), f32[32,1,4224]{2,1,0:T(1,128)S(1)}, u32[]{:S(2)}, u32[]{:S(2)}) %all-to-all-start) | async-done | bytes 540704 | tf_op jit(solution)/shard_map/all_to_all | solution.py:297
  40.7 1.6 %scan.1 = f32[1024,128]{1,0:T(8,128)} custom-call(s32[1]{0:T(128)} %get-tuple-element.35.refs_0_, f32[1056,128]{1,0:T(8,128)S(1)} %bitcast.28), custom_call_target="tpu_custom_call" | custom-call | tf_op jit(solution)/shard_map/scan/pallas_call | solution.py:343
  42.3 6.3 %all-to-all-start.1 = ((f32[32,1,4096]{2,1,0:T(1,128)}), f32[32,1,4096]{2,1,0:T(1,128)S(1)}, u32[]{:S(2)}, u32[]{:S(2)}) async-start(f32[32,1,4096]{2,1,0:T(1,128)} %bitcast.8), calls=%async_computation.1 | async-start | bytes 1048576 | tf_op jit(solution)/shard_map/all_to_all | solution.py:297
  48.6 0.0 copy-done.3
  48.6 15.4 %all-to-all-done.1 = f32[32,1,4096]{2,1,0:T(1,128)S(1)} async-done(((f32[32,1,4096]{2,1,0:T(1,128)}), f32[32,1,4096]{2,1,0:T(1,128)S(1)}, u32[]{:S(2)}, u32[]{:S(2)}) %all-to-all-start.1) | async-done | bytes 524320 | tf_op jit(solution)/shard_map/all_to_all | solution.py:297
  64.0 0.1 slice_add_fusion
  64.1 3.4 %collective-permute-start.1 = (f32[8,128,128]{2,1,0:T(8,128)S(1)}, f32[8,128,128]{2,1,0:T(8,128)S(1)}, u32[]{:S(2)}, u32[]{:S(2)}) collective-permute-start(f32[8,128,128]{2,1,0:T(8,128)S(1)} %slice_add_fusion), channel_id=1, source_target_pairs={{0,4},{4,0},{1,5},{5,1},{2,6},{6,2},{3,7},{7,3},{8,12},{12,8},{9,1... | collective-permute-start | bytes 1572872 | tf_op jit(solution)/shard_map/ppermute | solution.py:301
  67.5 1.5 %collective-permute-done.1.refs_2_ = f32[8,128,128]{2,1,0:T(8,128)S(1)} collective-permute-done((f32[8,128,128]{2,1,0:T(8,128)S(1)}, f32[8,128,128]{2,1,0:T(8,128)S(1)}, u32[]{:S(2)}, u32[]{:S(2)}) %collective-permute-start.1) | collective-permute-done | bytes 524320 | tf_op jit(solution)/shard_map/ppermute | solution.py:301
  69.0 0.0 copy-done
  69.0 0.0 copy-done.1
  69.0 0.0 copy-done.2
  69.0 1.1 states.1
  70.2 6.6 %k3a.1 = (bf16[8,512,128]{2,1,0:T(8,128)(2,1)}, bf16[8,512,128]{2,1,0:T(8,128)(2,1)}, f32[8,128,128]{2,1,0:T(8,128)}, f32[8,128,128]{2,1,0:T(8,128)}) custom-call(s32[1]{0:T(128)} %bitcast.refs_0_.refs_1_, bf16[8,2,128,128]{3,2,1,0:T(8,128)(2,1)} %get-tuple-element.39.refs_1_.refs_6_, bf16[8,2,128,128]{3,2,1,0:T(8,128)(2,1)} %get-tuple-element.40.refs_2_.refs_7_, ...), custom_call_target="tpu_custom_call" | custom-call | bytes 1048576 | tf_op jit(solution)/shard_map/k3a/pallas_call | solution.py:353
  76.8 0.5 collective-permute-start.2
  77.2 1.7 %collective-permute-done.2.refs_1_ = f32[8,128,128]{2,1,0:T(8,128)S(1)} collective-permute-done((f32[8,128,128]{2,1,0:T(8,128)}, f32[8,128,128]{2,1,0:T(8,128)S(1)}, u32[]{:S(2)}, u32[]{:S(2)}) %collective-permute-start.2) | collective-permute-done | bytes 524320 | tf_op jit(solution)/shard_map/ppermute | solution.py:301
  79.0 1.9 %add.6.refs_0_ = f32[8,128,128]{2,1,0:T(8,128)} custom-call(f32[8,128,128]{2,1,0:T(8,128)} %get-tuple-element.47.refs_0_, f32[8,128,128]{2,1,0:T(8,128)S(1)} %collective-permute-done.2.refs_1_), custom_call_target="tpu_custom_call" | custom-call | tf_op jit(solution)/shard_map/add/pallas_call | solution.py:361
  80.9 6.1 %all-to-all-start.2 = ((f32[16,1,8192]{2,1,0:T(1,128)}), f32[16,1,8192]{2,1,0:T(1,128)S(1)}, u32[]{:S(2)}, u32[]{:S(2)}) async-start(f32[16,1,8192]{2,1,0:T(1,128)} %bitcast.15), calls=%async_computation.2 | async-start | bytes 1048576 | tf_op jit(solution)/shard_map/all_to_all | solution.py:297
  87.0 6.5 %k3b.1 = (bf16[512,1024]{1,0:T(8,128)(2,1)}, bf16[512,1024]{1,0:T(8,128)(2,1)}, bf16[512,1024]{1,0:T(8,128)(2,1)}, bf16[512,1024]{1,0:T(8,128)(2,1)}, s32[1]{0:T(128)}) custom-call(f32[8,128,128]{2,1,0:T(8,128)} %add.6.refs_0_, s32[1]{0:T(128)} %bitcast.refs_0_.refs_1_, f32[8,512,128]{2,1,0:T(8,128)} %get-tuple-element.49.refs_2_, ...), custom_call_target="tpu_custom_call" | custom-call | flops 1073741824 | bytes 1048576 | tf_op jit(solution)/shard_map/k3b/pallas_call | solution.py:364
  93.5 3.8 %all-to-all-done.2 = f32[16,1,8192]{2,1,0:T(1,128)S(1)} async-done(((f32[16,1,8192]{2,1,0:T(1,128)}), f32[16,1,8192]{2,1,0:T(1,128)S(1)}, u32[]{:S(2)}, u32[]{:S(2)}) %all-to-all-start.2) | async-done | bytes 524320 | tf_op jit(solution)/shard_map/all_to_all | solution.py:297
  97.4 0.6 spread_z.1
  98.0 11.6 %all_to_all.45 = f32[8,1,8192]{2,1,0:T(1,128)S(1)} all-to-all(f32[8,1,8192]{2,1,0:T(1,128)S(1)} %bitcast.32), channel_id=1, replica_groups=mesh['z'=8,'x'=4,'c'=2,'dp'=4] {'z'}, dimensions={0} | all-to-all | bytes 524288 | tf_op jit(solution)/shard_map/all_to_all | solution.py:297
  109.6 0.1 spread_xy.1
  109.7 13.4 %all_to_all.46 = f32[16,1,8192]{2,1,0:T(1,128)S(1)} all-to-all(f32[16,1,8192]{2,1,0:T(1,128)S(1)} %bitcast.30), channel_id=1, replica_groups=mesh['z'=8,'x'=4,'c'=2,'dp'=4] {'x','dp'}, dimensions={0} | all-to-all | bytes 1048576 | tf_op jit(solution)/shard_map/all_to_all | solution.py:297
  123.1 4.1 %collective-permute-start.3 = (f32[8,128,128]{2,1,0:T(8,128)S(1)}, f32[8,128,128]{2,1,0:T(8,128)S(1)}, u32[]{:S(2)}, u32[]{:S(2)}) collective-permute-start(f32[8,128,128]{2,1,0:T(8,128)S(1)} %bitcast.43), channel_id=1, source_target_pairs={{0,4},{4,0},{1,5},{5,1},{2,6},{6,2},{3,7},{7,3},{8,12},{12,8},{9,1... | collective-permute-start | bytes 1572872 | tf_op jit(solution)/shard_map/ppermute | solution.py:301
  127.2 1.5 %collective-permute-done.3 = f32[8,128,128]{2,1,0:T(8,128)S(1)} collective-permute-done((f32[8,128,128]{2,1,0:T(8,128)S(1)}, f32[8,128,128]{2,1,0:T(8,128)S(1)}, u32[]{:S(2)}, u32[]{:S(2)}) %collective-permute-start.3) | collective-permute-done | bytes 524320 | tf_op jit(solution)/shard_map/ppermute | solution.py:301
  128.7 1.1 broadcast_select_fusion
  (1 shorter events, 0.0 us)
Async XLA Ops:
  7.5 5.1 %collective-permute-start = (f32[8,136,128]{2,1,0:T(8,128)}, f32[8,136,128]{2,1,0:T(8,128)S(1)}, u32[]{:S(2)}, u32[]{:S(2)}) collective-permute-start(f32[8,136,128]{2,1,0:T(8,128)} %get-tuple-element.34), channel_id=1, source_target_pairs={{0,4},{4,0},{1,5},{5,1},{2,6},{6,2},{3,7},{7,3},{8,12},{12,8},{9,1... | collective-permute-start | bytes 1671176 | tf_op jit(solution)/shard_map/ppermute | solution.py:301
  14.5 26.2 %all-to-all-start = ((f32[32,1,4224]{2,1,0:T(1,128)}), f32[32,1,4224]{2,1,0:T(1,128)S(1)}, u32[]{:S(2)}, u32[]{:S(2)}) async-start(f32[32,1,4224]{2,1,0:T(1,128)} %bitcast.6), calls=%async_computation | async-start | bytes 1081344 | tf_op jit(solution)/shard_map/all_to_all | solution.py:297
  37.6 11.0 %copy-start.3 = (f32[8,136,128]{2,1,0:T(8,128)S(1)}, f32[8,136,128]{2,1,0:T(8,128)}, u32[]{:S(2)}) copy-start(f32[8,136,128]{2,1,0:T(8,128)} %get-tuple-element.33.refs_0_) | copy-start | bytes 1671172
  37.6 31.4 %copy-start = (f32[8,128,128]{2,1,0:T(8,128)S(1)}, f32[8,128,128]{2,1,0:T(8,128)}, u32[]{:S(2)}) copy-start(f32[8,128,128]{2,1,0:T(8,128)} %get-tuple-element.36.refs_3_) | copy-start | bytes 1572868
  37.6 31.4 %copy-start.1 = (f32[8,128,128]{2,1,0:T(8,128)S(1)}, f32[8,128,128]{2,1,0:T(8,128)}, u32[]{:S(2)}) copy-start(f32[8,128,128]{2,1,0:T(8,128)} %get-tuple-element.37.refs_4_) | copy-start | bytes 1572868
  37.6 31.4 %copy-start.2 = (f32[8,16,128]{2,1,0:T(8,128)S(1)}, f32[8,16,128]{2,1,0:T(8,128)}, u32[]{:S(2)}) copy-start(f32[8,16,128]{2,1,0:T(8,128)} %get-tuple-element.38.refs_5_) | copy-start | bytes 196612
  42.3 21.7 %all-to-all-start.1 = ((f32[32,1,4096]{2,1,0:T(1,128)}), f32[32,1,4096]{2,1,0:T(1,128)S(1)}, u32[]{:S(2)}, u32[]{:S(2)}) async-start(f32[32,1,4096]{2,1,0:T(1,128)} %bitcast.8), calls=%async_computation.1 | async-start | bytes 1048576 | tf_op jit(solution)/shard_map/all_to_all | solution.py:297
  64.1 4.9 %collective-permute-start.1 = (f32[8,128,128]{2,1,0:T(8,128)S(1)}, f32[8,128,128]{2,1,0:T(8,128)S(1)}, u32[]{:S(2)}, u32[]{:S(2)}) collective-permute-start(f32[8,128,128]{2,1,0:T(8,128)S(1)} %slice_add_fusion), channel_id=1, source_target_pairs={{0,4},{4,0},{1,5},{5,1},{2,6},{6,2},{3,7},{7,3},{8,12},{12,8},{9,1... | collective-permute-start | bytes 1572872 | tf_op jit(solution)/shard_map/ppermute | solution.py:301
  76.8 2.2 %collective-permute-start.2 = (f32[8,128,128]{2,1,0:T(8,128)}, f32[8,128,128]{2,1,0:T(8,128)S(1)}, u32[]{:S(2)}, u32[]{:S(2)}) collective-permute-start(f32[8,128,128]{2,1,0:T(8,128)} %get-tuple-element.48), channel_id=1, source_target_pairs={{0,4},{4,0},{1,5},{5,1},{2,6},{6,2},{3,7},{7,3},{8,12},{12,8},{9,1... | collective-permute-start | bytes 1572872 | tf_op jit(solution)/shard_map/ppermute | solution.py:301
  80.9 16.5 %all-to-all-start.2 = ((f32[16,1,8192]{2,1,0:T(1,128)}), f32[16,1,8192]{2,1,0:T(1,128)S(1)}, u32[]{:S(2)}, u32[]{:S(2)}) async-start(f32[16,1,8192]{2,1,0:T(1,128)} %bitcast.15), calls=%async_computation.2 | async-start | bytes 1048576 | tf_op jit(solution)/shard_map/all_to_all | solution.py:297
  123.1 5.6 %collective-permute-start.3 = (f32[8,128,128]{2,1,0:T(8,128)S(1)}, f32[8,128,128]{2,1,0:T(8,128)S(1)}, u32[]{:S(2)}, u32[]{:S(2)}) collective-permute-start(f32[8,128,128]{2,1,0:T(8,128)S(1)} %bitcast.43), channel_id=1, source_target_pairs={{0,4},{4,0},{1,5},{5,1},{2,6},{6,2},{3,7},{7,3},{8,12},{12,8},{9,1... | collective-permute-start | bytes 1572872 | tf_op jit(solution)/shard_map/ppermute | solution.py:301

commit v4 on v3

v4 whole, which is shorter than its diff:
```python
import math

import jax
import jax.numpy as jnp
from jax import lax
from jax.experimental import pallas as pl
from jax.experimental.pallas import tpu as pltpu
from jax.sharding import Mesh, PartitionSpec as P

BLOCK = 256
HEADS = 8
DH = 128
TOK = 512
HPB = 2
WIDE = 4
SCALE = 1.0 / (DH * math.sqrt(BLOCK))
F32 = jnp.float32
BF16 = jnp.bfloat16
CHIPS = 32
ROWS = HEADS * DH // CHIPS


def dot(a, b, dims=((1,), (0,))):
    return lax.dot_general(a, b, (dims, ((), ())), preferred_element_type=F32)


NT = ((1,), (1,))
TN = ((0,), (0,))


def split3(x):
    hi = x.astype(BF16)
    rest = x - hi.astype(F32)
    mid = rest.astype(BF16)
    low = (rest - mid.astype(F32)).astype(BF16)
    return jnp.concatenate([hi, mid, low], axis=1)


def lower3():
    t = lax.broadcasted_iota(jnp.int32, (BLOCK, BLOCK), 0)
    s = lax.broadcasted_iota(jnp.int32, (BLOCK, BLOCK), 1)
    low = jnp.where(s <= t, 1.0, 0.0).astype(BF16)
    return jnp.concatenate([low, low, low], axis=1)


def cumul_cols(low, row):
    return dot(low, split3(jnp.broadcast_to(row, (DH, BLOCK))), NT)


def cumul_rows(low, rows):
    return dot(split3(rows), low, NT)


def sigmoid(u):
    return jax.nn.sigmoid(u)


def columns(ref, h):
    return ref.at[:, pl.ds(pl.multiple_of(h * DH, DH), DH)]


def head_copies(srcs, bufs, sems, h):
    return [
        pltpu.make_async_copy(columns(src, h) if len(src.shape) == 2 else src.at[h],
                              buf.at[h], sems.at[j, h])
        for j, (src, buf) in enumerate(zip(srcs, bufs))
    ]


def over_heads(srcs, bufs, sems, outs, out_sems, work):
    for h in range(HEADS):
        for copy in head_copies(srcs, bufs, sems, h):
            copy.start()

    def back(h):
        return [
            pltpu.make_async_copy(buf.at[h], dst.at[h], out_sems.at[j, h])
            for j, (buf, dst) in enumerate(outs)
        ]

    def some(step, carry):
        for i in range(HPB):
            for copy in head_copies(srcs, bufs, sems, step * HPB + i):
                copy.wait()
        for i in range(HPB):
            work(step * HPB + i)
        for i in range(HPB):
            for copy in back(step * HPB + i):
                copy.start()
        return carry

    lax.fori_loop(0, HEADS // HPB, some, 0)
    for h in range(HEADS):
        for copy in back(h):
            copy.wait()


def k1_body(core, ld_ref, q, k, v, g, wq, wk, mine_ref, send_ref, own,
            q_ref, k_ref, v_ref, g_ref, wq_ref, wk_ref, own_ref, cum_ref, sems, out_sems):
    first = core[0] == 0
    low = lower3()
    for b in range(2):
        rows = slice(b * BLOCK, (b + 1) * BLOCK)
        cum_ref[:, rows] = cumul_rows(low, ld_ref[:, rows])

    def work(h):
        ups, cons, tots = [], [], []
        all_q = dot(wq_ref[h], q_ref[h], ((0,), (1,)))
        all_k = dot(wk_ref[h], k_ref[h], ((0,), (1,)))
        for b in range(2):
            rows = slice(b * BLOCK, (b + 1) * BLOCK)
            cum = cum_ref[pl.ds(h, 1), rows]
            tot = cum[:, BLOCK - 1:BLOCK]
            pre_q = all_q[:, rows]
            pre_k = all_k[:, rows]
            qf = (pre_q * sigmoid(pre_q)).astype(BF16)
            kf = (pre_k * sigmoid(pre_k)).astype(BF16)
            qdec = (qf.astype(F32) * jnp.exp(cum)).astype(BF16)
            kdec = (kf.astype(F32) * jnp.exp(tot - cum)).astype(BF16)
            ups.append(dot(kdec, v_ref[h, rows]))
            cons.append(dot(qdec, g_ref[h, rows]))
            tots.append(jnp.broadcast_to(tot, (8, DH)))
        d0, d1 = jnp.exp(tots[0]), jnp.exp(tots[1])
        up = d1[0:1] * ups[0] + ups[1]
        con = cons[0] + d0[0:1] * cons[1]
        mine_ref[h, 0:DH, :] = jnp.where(first, up, con)
        send_ref[h, 0:DH, :] = jnp.where(first, con, up)
        mine_ref[h, DH:DH + 8, :] = d0 * d1
        send_ref[h, DH:DH + 8, :] = d0 * d1
        own_ref[h, 0:DH, :] = ups[0]
        own_ref[h, DH:2 * DH, :] = cons[1]
        own_ref[h, 2 * DH:2 * DH + 8, :] = d0
        own_ref[h, 2 * DH + 8:, :] = d1

    over_heads((q, k, v, g, wq, wk), (q_ref, k_ref, v_ref, g_ref, wq_ref, wk_ref), sems,
               [(own_ref, own)], out_sems, work)


def combine_body(mine_ref, recv_ref, out_ref):
    for h in range(HEADS):
        other = recv_ref[h, DH:DH + 1, :]
        agg = other * mine_ref[h, 0:DH, :] + recv_ref[h, 0:DH, :]
        both = other * mine_ref[h, DH:DH + 1, :]
        for part in range(DH // ROWS):
            at = (h * (DH // ROWS) + part) * (ROWS + 1)
            out_ref[at:at + ROWS, :] = agg[part * ROWS:(part + 1) * ROWS, :]
            out_ref[at + ROWS:at + ROWS + 1, :] = both


def scan_body(core, in_ref, out_ref):
    first = core[0] == 0

    def pieces(k):
        at = k * (ROWS + 1)
        return in_ref[at:at + ROWS, :], in_ref[at + ROWS:at + ROWS + 1, :]

    state = jnp.zeros((ROWS, DH), F32)
    for k in range(CHIPS):
        out_ref[k * ROWS:(k + 1) * ROWS, :] = state
        part, decay = pieces(k)
        state = decay * state + part
    state = jnp.zeros((ROWS, DH), F32)
    for k in range(CHIPS - 1, -1, -1):
        rows = slice(k * ROWS, (k + 1) * ROWS)
        out_ref[rows, :] = jnp.where(first, out_ref[rows, :], state)
        part, decay = pieces(k)
        state = decay * state + part


def k2_body(core, q_ref, k_ref, v_ref, g_ref, ld_ref, wq_ref, wk_ref,
            ab_ref, ov_ref, dec_ref, tr_ref, mark_ref, low_ref, cum_ref):
    step = pl.program_id(0)

    @pl.when(step == 0)
    def _():
        low_ref[...] = lower3()
        for b in range(2):
            rows = slice(b * BLOCK, (b + 1) * BLOCK)
            cum_ref[:, rows] = cumul_rows(low_ref[...], ld_ref[:, rows])

    t = lax.broadcasted_iota(jnp.int32, (BLOCK, BLOCK), 0)
    s = lax.broadcasted_iota(jnp.int32, (BLOCK, BLOCK), 1)
    causal = s <= t
    for i in range(HPB):
        lanes = slice(i * DH, (i + 1) * DH)
        tr_ref[i, 0] = q_ref[:, lanes].T
        tr_ref[i, 1] = k_ref[:, lanes].T
        for b in range(2):
            rows = slice(b * BLOCK, (b + 1) * BLOCK)
            head = pl.ds(step * HPB + i, 1)
            cum = cumul_cols(low_ref[...], ld_ref[head, rows])
            across = cum_ref[head, rows]
            tot = cum[BLOCK - 1:BLOCK, :]
            wide = jnp.concatenate([cum, cum], axis=1)
            weights = jnp.exp(jnp.where(causal, wide - across, -1e9))
            v, g = v_ref[rows, lanes], g_ref[rows, lanes]
            pre_q = dot(q_ref[rows, lanes], wq_ref[i])
            pre_k = dot(k_ref[rows, lanes], wk_ref[i])
            sig_q, sig_k = sigmoid(pre_q), sigmoid(pre_k)
            qf, kf = (pre_q * sig_q).astype(BF16), (pre_k * sig_k).astype(BF16)
            probs = (dot(qf, kf, NT) * weights).astype(BF16)
            grads = (dot(g, v, NT) * weights).astype(BF16)
            ov_ref[i, 0, rows] = SCALE * dot(probs, v)
            ov_ref[i, 1, rows] = SCALE * dot(probs, g, TN)
            early, late = jnp.exp(cum), jnp.exp(tot - cum)
            dec_ref[i, 0, rows] = (qf.astype(F32) * early).astype(BF16)
            dec_ref[i, 1, rows] = (kf.astype(F32) * late).astype(BF16)
            slope_q = SCALE * (sig_q * (1.0 + pre_q * (1.0 - sig_q)))
            ab_ref[i, 0, rows] = (dot(grads, kf) * slope_q).astype(BF16)
            ab_ref[i, 1, rows] = (early * slope_q).astype(BF16)
            slope_k = SCALE * (sig_k * (1.0 + pre_k * (1.0 - sig_k)))
            ab_ref[i, 2, rows] = (dot(grads, qf, TN) * slope_k).astype(BF16)
            ab_ref[i, 3, rows] = (late * slope_k).astype(BF16)
    mark_ref[0] = core[0]


def states_body(core, inc_ref, recv_ref, own_ref, st_ref):
    first = core[0] == 0
    for h in range(HEADS):
        inc, recv = inc_ref[h], recv_ref[h]
        state = jnp.where(first, inc, recv)
        after = jnp.where(first, recv, inc)
        d0, d1 = own_ref[h, 2 * DH:2 * DH + 1, :], own_ref[h, 2 * DH + 8:2 * DH + 9, :]
        st_ref[h, 0] = state.astype(BF16)
        st_ref[h, 1] = (d0 * state + own_ref[h, 0:DH, :]).astype(BF16)
        st_ref[h, 2] = (own_ref[h, DH:2 * DH, :] + d1 * after).astype(BF16)
        st_ref[h, 3] = after.astype(BF16)


def k3a_body(core, st, tr, v, g, ab, gp, mine_ref, send_ref,
             st_ref, tr_ref, v_ref, g_ref, ab_ref, gp_ref, sems, out_sems):
    first = core[0] == 0

    def work(h):
        for b in range(2):
            rows = slice(b * BLOCK, (b + 1) * BLOCK)
            from_state = dot(g_ref[h, rows], st_ref[h, b], NT)
            from_after = dot(v_ref[h, rows], st_ref[h, 2 + b], NT)
            gp_ref[h, 0, rows] = (
                ab_ref[h, 0, rows].astype(F32) + ab_ref[h, 1, rows].astype(F32) * from_state
            ).astype(BF16)
            gp_ref[h, 1, rows] = (
                ab_ref[h, 2, rows].astype(F32) + ab_ref[h, 3, rows].astype(F32) * from_after
            ).astype(BF16)
        part_q = dot(tr_ref[h, 0], gp_ref[h, 0])
        part_k = dot(tr_ref[h, 1], gp_ref[h, 1])
        mine_ref[h] = jnp.where(first, part_q, part_k)
        send_ref[h] = jnp.where(first, part_k, part_q)

    over_heads((st, tr, v, g, ab), (st_ref, tr_ref, v_ref, g_ref, ab_ref), sems,
               [(gp_ref, gp)], out_sems, work)


def k3b_body(core, ov_ref, dec_ref, st_ref, gp_ref, wq_ref, wk_ref,
             out_ref, gq_ref, gk_ref, gv_ref, mark_ref):
    mark_ref[0] = core[0]
    for i in range(WIDE):
        lanes = slice(i * DH, (i + 1) * DH)
        for b in range(2):
            rows = slice(b * BLOCK, (b + 1) * BLOCK)
            out_ref[rows, lanes] = (
                ov_ref[i, 0, rows] + SCALE * dot(dec_ref[i, 0, rows], st_ref[i, b])
            ).astype(BF16)
            gv_ref[rows, lanes] = (
                ov_ref[i, 1, rows] + SCALE * dot(dec_ref[i, 1, rows], st_ref[i, 2 + b])
            ).astype(BF16)
            gq_ref[rows, lanes] = dot(gp_ref[i, 0, rows], wq_ref[i], NT).astype(BF16)
            gk_ref[rows, lanes] = dot(gp_ref[i, 1, rows], wk_ref[i], NT).astype(BF16)


def add_body(a_ref, b_ref, out_ref):
    out_ref[...] = a_ref[...] + b_ref[...]


def spread_first_body(core, in_ref, out_ref):
    spread_body(in_ref, out_ref)


def spread_body(in_ref, out_ref):
    total = in_ref[0]
    for k in range(1, in_ref.shape[0]):
        total = total + in_ref[k]
    for k in range(out_ref.shape[0]):
        out_ref[k] = total


def smem():
    return pl.BlockSpec(memory_space=pltpu.SMEM)


def seq(heads=HPB):
    return pl.BlockSpec((TOK, heads * DH), lambda i: (0, i))


def per_head(*tail, heads=HPB):
    zeros = (0,) * len(tail)
    return pl.BlockSpec((heads,) + tail, lambda i: (i,) + zeros)


def whole(*shape):
    zeros = (0,) * len(shape)
    return pl.BlockSpec(shape, lambda i: zeros)


def shape(dims, kind=F32):
    return jax.ShapeDtypeStruct(dims, kind)


def call(body, name, ins, outs, out_shapes, flops=0, grid=HEADS // HPB, after=0,
         scratch=(), grant=None):
    return pl.pallas_call(
        lambda *refs: body(*refs[after:]),
        grid=(grid,),
        in_specs=[pl.BlockSpec(memory_space=pltpu.HBM)] * after + ins,
        out_specs=outs,
        out_shape=out_shapes,
        scratch_shapes=scratch,
        name=name,
        cost_estimate=pl.CostEstimate(flops=flops, transcendentals=0, bytes_accessed=1 << 20),
        compiler_params=pltpu.CompilerParams(
            dimension_semantics=("arbitrary",), vmem_limit_bytes=grant
        ),
    )


def streamed(body, name, slots, back, held, out_shapes, whole_ins=(), scratch=()):
    raw = pl.BlockSpec(memory_space=pltpu.HBM)
    kept = pl.BlockSpec(memory_space=pltpu.VMEM)
    return pl.pallas_call(
        body,
        grid=(1,),
        in_specs=[smem()] + list(whole_ins) + [raw] * len(slots),
        out_specs=[kept if here else raw for here in held],
        out_shape=out_shapes,
        scratch_shapes=list(slots) + list(back) + list(scratch) + [
            pltpu.SemaphoreType.DMA((len(slots), HEADS)),
            pltpu.SemaphoreType.DMA((len(back), HEADS)),
        ],
        name=name,
        compiler_params=pltpu.CompilerParams(dimension_semantics=("arbitrary",)),
    )


def small(body, name, ins, out_shape, out_spec, smem=0, after=0):
    vmem = pl.BlockSpec(memory_space=pltpu.VMEM)
    return pl.pallas_call(
        lambda *refs: body(*refs[after:]),
        grid=(1,),
        in_specs=[pl.BlockSpec(memory_space=pltpu.HBM)] * after
        + [pl.BlockSpec(memory_space=pltpu.SMEM)] * smem + [vmem] * ins,
        out_specs=out_spec,
        out_shape=out_shape,
        name=name,
        compiler_params=pltpu.CompilerParams(vmem_limit_bytes=8 << 20),
    )


def exchange(x, axes):
    return lax.all_to_all(x, axes, 0, 0, tiled=True)


def swap_cores(x):
    return lax.ppermute(x, "c", [(0, 1), (1, 0)])


SEQ_B = shape((TOK, HEADS * DH), BF16)
SEQ_F = shape((TOK, HEADS * DH), F32)
MAT = shape((HEADS, DH, DH), F32)


def local(query, key, value, log_decay, grad_out, query_map, key_map):
    core = lax.axis_index("c").astype(jnp.int32).reshape(1)
    q, k, v, g = (a[0] for a in (query, key, value, grad_out))
    ld = log_decay[0]
    maps = (query_map, key_map)
    seqs = (q, k, v, g)
    ld_spec = whole(HEADS, TOK)
    map_specs = [per_head(DH, DH)] * 2
    slot = pltpu.VMEM((HEADS, TOK, DH), BF16)
    square = pltpu.VMEM((HEADS, DH, DH), BF16)
    cut = pltpu.VMEM((HEADS, DH + 8, DH), F32)
    own_dims = (HEADS, 2 * DH + 16, DH)
    mine, send, own = streamed(
        k1_body, "k1", [slot] * 4 + [square] * 2, [pltpu.VMEM(own_dims, F32)],
        [True, True, False], [cut, cut, pltpu.HBM(own_dims, F32)],
        whole_ins=[ld_spec], scratch=[pltpu.VMEM((HEADS, TOK), F32)],
    )(core, ld, *seqs, *maps)
    recv = swap_cores(send)
    packed = small(
        combine_body, "combine", 2, shape((CHIPS * (ROWS + 1), DH)), whole(CHIPS * (ROWS + 1), DH),
    )(mine, recv)
    swapped = exchange(packed.reshape(CHIPS, (ROWS + 1) * DH), ("z", "x"))
    ab, ov, dec, tr, mark = call(
        k2_body, "k2",
        [smem()] + [seq()] * 4 + [ld_spec] + map_specs,
        [per_head(4, TOK, DH), per_head(2, TOK, DH), per_head(2, TOK, DH), per_head(2, DH, TOK),
         smem()],
        [shape((HEADS, 4, TOK, DH), BF16), shape((HEADS, 2, TOK, DH)),
         shape((HEADS, 2, TOK, DH), BF16), shape((HEADS, 2, DH, TOK), BF16),
         shape((1,), jnp.int32)],
        flops=1 << 30,
        after=1,
        scratch=[pltpu.VMEM((BLOCK, 3 * BLOCK), BF16), pltpu.VMEM((HEADS, TOK), F32)],
    )(packed, core, *seqs, ld, *maps)
    scanned = small(
        scan_body, "scan", 1, shape((CHIPS * ROWS, DH)), whole(CHIPS * ROWS, DH), smem=1,
    )(mark, swapped.reshape(CHIPS * (ROWS + 1), DH))
    inc = exchange(scanned.reshape(CHIPS, ROWS * DH), ("z", "x")).reshape(HEADS, DH, DH)
    passed = mine[:, DH:DH + 1, :] * inc + mine[:, :DH, :]
    recv = swap_cores(passed)
    st = small(
        states_body, "states", 3, pltpu.HBM((HEADS, 4, DH, DH), BF16), whole(HEADS, 4, DH, DH),
        smem=1,
    )(core, inc, recv, own)
    gp_dims = (HEADS, 2, TOK, DH)
    gp, mine, send = streamed(
        k3a_body, "k3a",
        [pltpu.VMEM((HEADS, 4, DH, DH), BF16), pltpu.VMEM((HEADS, 2, DH, TOK), BF16), slot, slot,
         pltpu.VMEM((HEADS, 4, TOK, DH), BF16)],
        [pltpu.VMEM(gp_dims, BF16)], [False, True, True],
        [pltpu.HBM(gp_dims, BF16), pltpu.VMEM((HEADS, DH, DH), F32),
         pltpu.VMEM((HEADS, DH, DH), F32)],
    )(core, st, tr, v, g, ab)
    recv = swap_cores(send)
    chip = small(add_body, "add", 2, MAT, whole(HEADS, DH, DH))(mine, recv)
    pieces = exchange(chip.reshape(16, -1), ("x", "dp"))
    rows = HEADS * DH // 16
    out, gq, gk, gv, mark = call(
        k3b_body, "k3b",
        [smem(), per_head(2, TOK, DH, heads=WIDE), per_head(2, TOK, DH, heads=WIDE),
         per_head(4, DH, DH, heads=WIDE), per_head(2, TOK, DH, heads=WIDE)]
        + [per_head(DH, DH, heads=WIDE)] * 2,
        [seq(WIDE)] * 4 + [smem()],

        [SEQ_B] * 4 + [shape((1,), jnp.int32)],
        flops=1 << 30,
        after=1,
        grid=HEADS // WIDE,
    )(chip, core, ov, dec, st, gp, *maps)
    spread = small(spread_first_body, "spread_z", 1, shape((8, rows, DH)), whole(8, rows, DH), smem=1)(
        mark, pieces.reshape(16, rows, DH)
    )
    pieces = exchange(spread.reshape(8, -1), "z")
    spread = small(spread_body, "spread_xy", 1, shape((16, rows, DH)), whole(16, rows, DH))(
        pieces.reshape(8, rows, DH)
    )
    own = exchange(spread.reshape(16, -1), ("x", "dp")).reshape(HEADS, DH, DH)
    other = swap_cores(own)
    first = core[0] == 0
    query_map_grad = jnp.where(first, own, other)
    key_map_grad = jnp.where(first, other, own)
    return (out[None], gq[None], gk[None], gv[None], query_map_grad, key_map_grad)


def solution(mesh):
    fine = Mesh(mesh.devices.reshape(8, 4, 2, 4), ("z", "x", "c", "dp"))
    ctx = ("z", "x", "c")
    act = P("dp", ctx, None)
    return jax.shard_map(
        local,
        mesh=fine,
        in_specs=(act, act, act, P("dp", None, ctx), act, P(), P()),
        out_specs=(act, act, act, act, P(), P()),
        check_vma=False,
    )
```

time: 131 us -> 126 us (0.962)
  Pallas kernels: 41 us -> 36.7 us
    pallas_call x5, Pallas kernels: 23 us -> 20 us  [the longest x1 6.31 us: local(): streamed(k1_body, 'k1', [slot] * 4 + [square] * 2, [pltpu.VMEM(own_dims,...]
  transfers between devices with their start and end apart: 7 -> 7, of which waited for: 7 -> 7; matrix products, arithmetic and copies ran while one was open for 0% -> 0% of each run, Pallas kernels for 16% -> 15%
where the time goes in v4:
time: 126 us
  Pallas kernels  36.7 us (29%)
  starting transfers between devices  32.6 us (26%)
  waiting for transfers between devices  29.5 us (23%)
  blocking collectives  25.1 us (20%)
    all_to_all x2, blocking collectives, exchange(): return lax.all_to_all(x, axes, 0, 0, tiled=True)  25.1 us
    all_to_all x3, waiting for transfers between devices, exchange(): return lax.all_to_all(x, axes, 0, 0, tiled=True)  23.3 us
    all_to_all x3, starting transfers between devices, exchange(): return lax.all_to_all(x, axes, 0, 0, tiled=True)  21.5 us
    pallas_call x1, Pallas kernels, local(): call(k2_body, 'k2', [smem()] + [seq()] * 4 + [ld_spec] + map_specs, [per_...  13.5 us
    ppermute x4, starting transfers between devices, swap_cores(): return lax.ppermute(x, 'c', [(0, 1), (1, 0)])  11.2 us
    pallas_call x1, Pallas kernels, local(): streamed(k1_body, 'k1', [slot] * 4 + [square] * 2, [pltpu.VMEM(own_dims,...  6.31 us
    ppermute x4, waiting for transfers between devices, swap_cores(): return lax.ppermute(x, 'c', [(0, 1), (1, 0)])  6.19 us
    pallas_call x1, Pallas kernels, local(): streamed(k3a_body, 'k3a', [pltpu.VMEM((HEADS, 4, DH, DH), BF16), pltpu.VM...  5.92 us
  transfers between devices with their start and end apart: 7, of which 7 were waited for; matrix products, arithmetic and copies ran while one was open for 0% of the time, Pallas kernels for 15%

profile of v4, /device:TPU:1, one launch (start us, length us, event | category | flops | bytes accessed | tf_op | source)
XLA Modules:
  0.0 125.7 jit_solution(7032954009149636190)
XLA Ops:
  0.6 6.3 %k1.1 = (f32[8,136,128]{2,1,0:T(8,128)S(1)}, f32[8,136,128]{2,1,0:T(8,128)S(1)}, f32[8,272,128]{2,1,0:T(8,128)}) custom-call(s32[1]{0:T(128)} %bitcast.core.refs_1_.refs_0_, f32[8,512]{1,0:T(8,128)} %bitcast.45, bf16[512,1024]{1,0:T(8,128)(2,1)} %bitcast.39, bf16[512,1024]{1,0:T(8,128)(2,1)} %bitcast.41, bf16[512,1024]{1,0:T(8,128)(2,1)} %bitcast.33, ...), custom_call_target="tpu_custom_call" | custom-call | tf_op jit(solution)/shard_map/k1/pallas_call | solution.py:383
  7.0 3.3 %collective-permute-start = (f32[8,136,128]{2,1,0:T(8,128)S(1)}, f32[8,136,128]{2,1,0:T(8,128)S(1)}, u32[]{:S(2)}, u32[]{:S(2)}) collective-permute-start(f32[8,136,128]{2,1,0:T(8,128)S(1)} %get-tuple-element.23), channel_id=1, source_target_pairs={{0,4},{4,0},{1,5},{5,1},{2,6},{6,2},{3,7},{7,3},{8,12},{12,8},{9,1... | collective-permute-start | bytes 1671176 | tf_op jit(solution)/shard_map/ppermute | solution.py:363
  10.2 1.6 %collective-permute-done.refs_1_ = f32[8,136,128]{2,1,0:T(8,128)S(1)} collective-permute-done((f32[8,136,128]{2,1,0:T(8,128)S(1)}, f32[8,136,128]{2,1,0:T(8,128)S(1)}, u32[]{:S(2)}, u32[]{:S(2)}) %collective-permute-start) | collective-permute-done | bytes 557088 | tf_op jit(solution)/shard_map/ppermute | solution.py:363
  11.8 0.9 combine.1.refs_0_
  12.7 9.3 %all-to-all-start = ((f32[32,1,4224]{2,1,0:T(1,128)}), f32[32,1,4224]{2,1,0:T(1,128)S(1)}, u32[]{:S(2)}, u32[]{:S(2)}) async-start(f32[32,1,4224]{2,1,0:T(1,128)} %bitcast.6), calls=%async_computation | async-start | bytes 1081344 | tf_op jit(solution)/shard_map/all_to_all | solution.py:359
  22.0 13.5 %k2.1 = (bf16[8,4,512,128]{3,2,1,0:T(8,128)(2,1)}, f32[8,2,512,128]{3,2,1,0:T(8,128)}, bf16[8,2,512,128]{3,2,1,0:T(8,128)(2,1)}, bf16[8,2,128,512]{3,2,1,0:T(8,128)(2,1)}, s32[1]{0:T(128)}) custom-call(f32[1056,128]{1,0:T(8,128)} %combine.1.refs_0_, s32[1]{0:T(128)} %bitcast.core.refs_1_.refs_0_, bf16[512,1024]{1,0:T(8,128)(2,1)} %bitcast.40, ...), custom_call_target="tpu_custom_call" | custom-call | flops 1073741824 | bytes 1048576 | tf_op jit(solution)/shard_map/k2/pallas_call | solution.py:393
  35.6 0.0 copy-start
  35.6 3.3 %all-to-all-done = f32[32,1,4224]{2,1,0:T(1,128)S(1)} async-done(((f32[32,1,4224]{2,1,0:T(1,128)}), f32[32,1,4224]{2,1,0:T(1,128)S(1)}, u32[]{:S(2)}, u32[]{:S(2)}) %all-to-all-start) | async-done | bytes 540704 | tf_op jit(solution)/shard_map/all_to_all | solution.py:359
  38.9 1.6 %scan.1 = f32[1024,128]{1,0:T(8,128)} custom-call(s32[1]{0:T(128)} %get-tuple-element.24.refs_0_, f32[1056,128]{1,0:T(8,128)S(1)} %bitcast.28), custom_call_target="tpu_custom_call" | custom-call | tf_op jit(solution)/shard_map/scan/pallas_call | solution.py:405
  40.4 6.0 %all-to-all-start.1 = ((f32[32,1,4096]{2,1,0:T(1,128)}), f32[32,1,4096]{2,1,0:T(1,128)S(1)}, u32[]{:S(2)}, u32[]{:S(2)}) async-start(f32[32,1,4096]{2,1,0:T(1,128)} %bitcast.8), calls=%async_computation.1 | async-start | bytes 1048576 | tf_op jit(solution)/shard_map/all_to_all | solution.py:359
  46.5 15.4 %all-to-all-done.1 = f32[32,1,4096]{2,1,0:T(1,128)S(1)} async-done(((f32[32,1,4096]{2,1,0:T(1,128)}), f32[32,1,4096]{2,1,0:T(1,128)S(1)}, u32[]{:S(2)}, u32[]{:S(2)}) %all-to-all-start.1) | async-done | bytes 524320 | tf_op jit(solution)/shard_map/all_to_all | solution.py:359
  61.9 0.1 slice_add_fusion
  61.9 3.4 %collective-permute-start.1 = (f32[8,128,128]{2,1,0:T(8,128)S(1)}, f32[8,128,128]{2,1,0:T(8,128)S(1)}, u32[]{:S(2)}, u32[]{:S(2)}) collective-permute-start(f32[8,128,128]{2,1,0:T(8,128)S(1)} %slice_add_fusion), channel_id=1, source_target_pairs={{0,4},{4,0},{1,5},{5,1},{2,6},{6,2},{3,7},{7,3},{8,12},{12,8},{9,1... | collective-permute-start | bytes 1572872 | tf_op jit(solution)/shard_map/ppermute | solution.py:363
  65.3 1.5 %collective-permute-done.1.refs_2_ = f32[8,128,128]{2,1,0:T(8,128)S(1)} collective-permute-done((f32[8,128,128]{2,1,0:T(8,128)S(1)}, f32[8,128,128]{2,1,0:T(8,128)S(1)}, u32[]{:S(2)}, u32[]{:S(2)}) %collective-permute-start.1) | collective-permute-done | bytes 524320 | tf_op jit(solution)/shard_map/ppermute | solution.py:363
  66.8 0.0 copy-done
  66.8 1.1 states.1.st.refs_4_
  68.0 5.9 %k3a.1 = (bf16[8,2,512,128]{3,2,1,0:T(8,128)(2,1)}, f32[8,128,128]{2,1,0:T(8,128)S(1)}, f32[8,128,128]{2,1,0:T(8,128)S(1)}) custom-call(s32[1]{0:T(128)} %bitcast.core.refs_1_.refs_0_, bf16[8,4,128,128]{3,2,1,0:T(8,128)(2,1)} %states.1.st.refs_4_, bf16[8,2,128,512]{3,2,1,0:T(8,128)(2,1)} %get-tuple-element.26.tr, bf16[512,1024]{1,0:T(8,128)(2,1)} %bitcast.35, ...), custom_call_target="tpu_custom_call" | custom-call | tf_op jit(solution)/shard_map/k3a/pallas_call | solution.py:416
  73.9 0.5 collective-permute-start.2
  74.4 1.5 %collective-permute-done.2.refs_1_ = f32[8,128,128]{2,1,0:T(8,128)S(1)} collective-permute-done((f32[8,128,128]{2,1,0:T(8,128)S(1)}, f32[8,128,128]{2,1,0:T(8,128)S(1)}, u32[]{:S(2)}, u32[]{:S(2)}) %collective-permute-start.2) | collective-permute-done | bytes 524320 | tf_op jit(solution)/shard_map/ppermute | solution.py:363
  75.9 0.8 add.6.refs_0_
  76.7 6.1 %all-to-all-start.2 = ((f32[16,1,8192]{2,1,0:T(1,128)}), f32[16,1,8192]{2,1,0:T(1,128)S(1)}, u32[]{:S(2)}, u32[]{:S(2)}) async-start(f32[16,1,8192]{2,1,0:T(1,128)} %bitcast.15), calls=%async_computation.2 | async-start | bytes 1048576 | tf_op jit(solution)/shard_map/all_to_all | solution.py:359
  82.9 5.8 %k3b.1 = (bf16[512,1024]{1,0:T(8,128)(2,1)}, bf16[512,1024]{1,0:T(8,128)(2,1)}, bf16[512,1024]{1,0:T(8,128)(2,1)}, bf16[512,1024]{1,0:T(8,128)(2,1)}, s32[1]{0:T(128)}) custom-call(f32[8,128,128]{2,1,0:T(8,128)} %add.6.refs_0_, s32[1]{0:T(128)} %bitcast.core.refs_1_.refs_0_, f32[8,2,512,128]{3,2,1,0:T(8,128)} %get-tuple-element.30.refs_2_, ...), custom_call_target="tpu_custom_call" | custom-call | flops 1073741824 | bytes 1048576 | tf_op jit(solution)/shard_map/k3b/pallas_call | solution.py:428
  88.7 4.6 %all-to-all-done.2 = f32[16,1,8192]{2,1,0:T(1,128)S(1)} async-done(((f32[16,1,8192]{2,1,0:T(1,128)}), f32[16,1,8192]{2,1,0:T(1,128)S(1)}, u32[]{:S(2)}, u32[]{:S(2)}) %all-to-all-start.2) | async-done | bytes 524320 | tf_op jit(solution)/shard_map/all_to_all | solution.py:359
  93.2 0.7 spread_z.1
  93.9 11.6 %all_to_all.45 = f32[8,1,8192]{2,1,0:T(1,128)S(1)} all-to-all(f32[8,1,8192]{2,1,0:T(1,128)S(1)} %bitcast.32), channel_id=1, replica_groups=mesh['z'=8,'x'=4,'c'=2,'dp'=4] {'z'}, dimensions={0} | all-to-all | bytes 524288 | tf_op jit(solution)/shard_map/all_to_all | solution.py:359
  105.5 0.1 spread_xy.1
  105.6 13.5 %all_to_all.46 = f32[16,1,8192]{2,1,0:T(1,128)S(1)} all-to-all(f32[16,1,8192]{2,1,0:T(1,128)S(1)} %bitcast.30), channel_id=1, replica_groups=mesh['z'=8,'x'=4,'c'=2,'dp'=4] {'x','dp'}, dimensions={0} | all-to-all | bytes 1048576 | tf_op jit(solution)/shard_map/all_to_all | solution.py:359
  119.1 4.1 %collective-permute-start.3 = (f32[8,128,128]{2,1,0:T(8,128)S(1)}, f32[8,128,128]{2,1,0:T(8,128)S(1)}, u32[]{:S(2)}, u32[]{:S(2)}) collective-permute-start(f32[8,128,128]{2,1,0:T(8,128)S(1)} %bitcast.43), channel_id=1, source_target_pairs={{0,4},{4,0},{1,5},{5,1},{2,6},{6,2},{3,7},{7,3},{8,12},{12,8},{9,1... | collective-permute-start | bytes 1572872 | tf_op jit(solution)/shard_map/ppermute | solution.py:363
  123.1 1.5 %collective-permute-done.3 = f32[8,128,128]{2,1,0:T(8,128)S(1)} collective-permute-done((f32[8,128,128]{2,1,0:T(8,128)S(1)}, f32[8,128,128]{2,1,0:T(8,128)S(1)}, u32[]{:S(2)}, u32[]{:S(2)}) %collective-permute-start.3) | collective-permute-done | bytes 524320 | tf_op jit(solution)/shard_map/ppermute | solution.py:363
  124.7 1.1 broadcast_select_fusion
  (1 shorter events, 0.0 us)
Async XLA Ops:
  7.0 4.9 %collective-permute-start = (f32[8,136,128]{2,1,0:T(8,128)S(1)}, f32[8,136,128]{2,1,0:T(8,128)S(1)}, u32[]{:S(2)}, u32[]{:S(2)}) collective-permute-start(f32[8,136,128]{2,1,0:T(8,128)S(1)} %get-tuple-element.23), channel_id=1, source_target_pairs={{0,4},{4,0},{1,5},{5,1},{2,6},{6,2},{3,7},{7,3},{8,12},{12,8},{9,1... | collective-permute-start | bytes 1671176 | tf_op jit(solution)/shard_map/ppermute | solution.py:363
  12.7 26.2 %all-to-all-start = ((f32[32,1,4224]{2,1,0:T(1,128)}), f32[32,1,4224]{2,1,0:T(1,128)S(1)}, u32[]{:S(2)}, u32[]{:S(2)}) async-start(f32[32,1,4224]{2,1,0:T(1,128)} %bitcast.6), calls=%async_computation | async-start | bytes 1081344 | tf_op jit(solution)/shard_map/all_to_all | solution.py:359
  35.6 31.3 %copy-start = (f32[8,272,128]{2,1,0:T(8,128)S(1)}, f32[8,272,128]{2,1,0:T(8,128)}, u32[]{:S(2)}) copy-start(f32[8,272,128]{2,1,0:T(8,128)} %get-tuple-element.25.refs_3_) | copy-start | bytes 3342340
  40.4 21.4 %all-to-all-start.1 = ((f32[32,1,4096]{2,1,0:T(1,128)}), f32[32,1,4096]{2,1,0:T(1,128)S(1)}, u32[]{:S(2)}, u32[]{:S(2)}) async-start(f32[32,1,4096]{2,1,0:T(1,128)} %bitcast.8), calls=%async_computation.1 | async-start | bytes 1048576 | tf_op jit(solution)/shard_map/all_to_all | solution.py:359
  61.9 4.9 %collective-permute-start.1 = (f32[8,128,128]{2,1,0:T(8,128)S(1)}, f32[8,128,128]{2,1,0:T(8,128)S(1)}, u32[]{:S(2)}, u32[]{:S(2)}) collective-permute-start(f32[8,128,128]{2,1,0:T(8,128)S(1)} %slice_add_fusion), channel_id=1, source_target_pairs={{0,4},{4,0},{1,5},{5,1},{2,6},{6,2},{3,7},{7,3},{8,12},{12,8},{9,1... | collective-permute-start | bytes 1572872 | tf_op jit(solution)/shard_map/ppermute | solution.py:363
  73.9 2.0 %collective-permute-start.2 = (f32[8,128,128]{2,1,0:T(8,128)S(1)}, f32[8,128,128]{2,1,0:T(8,128)S(1)}, u32[]{:S(2)}, u32[]{:S(2)}) collective-permute-start(f32[8,128,128]{2,1,0:T(8,128)S(1)} %get-tuple-element.29), channel_id=1, source_target_pairs={{0,4},{4,0},{1,5},{5,1},{2,6},{6,2},{3,7},{7,3},{8,12},{12,8},{9,1... | collective-permute-start | bytes 1572872 | tf_op jit(solution)/shard_map/ppermute | solution.py:363
  76.7 16.5 %all-to-all-start.2 = ((f32[16,1,8192]{2,1,0:T(1,128)}), f32[16,1,8192]{2,1,0:T(1,128)S(1)}, u32[]{:S(2)}, u32[]{:S(2)}) async-start(f32[16,1,8192]{2,1,0:T(1,128)} %bitcast.15), calls=%async_computation.2 | async-start | bytes 1048576 | tf_op jit(solution)/shard_map/all_to_all | solution.py:359
  119.1 5.6 %collective-permute-start.3 = (f32[8,128,128]{2,1,0:T(8,128)S(1)}, f32[8,128,128]{2,1,0:T(8,128)S(1)}, u32[]{:S(2)}, u32[]{:S(2)}) collective-permute-start(f32[8,128,128]{2,1,0:T(8,128)S(1)} %bitcast.43), channel_id=1, source_target_pairs={{0,4},{4,0},{1,5},{5,1},{2,6},{6,2},{3,7},{7,3},{8,12},{12,8},{9,1... | collective-permute-start | bytes 1572872 | tf_op jit(solution)/shard_map/ppermute | solution.py:363

commit v5 on v4

--- a/solution.py
+++ b/solution.py
@@ -214,9 +214,12 @@
     mark_ref[0] = core[0]
 
 
-def states_body(core, inc_ref, recv_ref, own_ref, st_ref):
+def k3a_body(core, inc_ref, recv_ref, own_ref, v_ref, g_ref, tr, ab,
+             gp, st, mine_ref, send_ref, tr_ref, ab_ref, gp_ref, st_ref, sems, out_sems):
     first = core[0] == 0
-    for h in range(HEADS):
+
+    def work(h):
+        lanes = pl.ds(pl.multiple_of(h * DH, DH), DH)
         inc, recv = inc_ref[h], recv_ref[h]
         state = jnp.where(first, inc, recv)
         after = jnp.where(first, recv, inc)
@@ -225,17 +228,10 @@
         st_ref[h, 1] = (d0 * state + own_ref[h, 0:DH, :]).astype(BF16)
         st_ref[h, 2] = (own_ref[h, DH:2 * DH, :] + d1 * after).astype(BF16)
         st_ref[h, 3] = after.astype(BF16)
-
-
-def k3a_body(core, st, tr, v, g, ab, gp, mine_ref, send_ref,
-             st_ref, tr_ref, v_ref, g_ref, ab_ref, gp_ref, sems, out_sems):
-    first = core[0] == 0
-
-    def work(h):
         for b in range(2):
             rows = slice(b * BLOCK, (b + 1) * BLOCK)
-            from_state = dot(g_ref[h, rows], st_ref[h, b], NT)
-            from_after = dot(v_ref[h, rows], st_ref[h, 2 + b], NT)
+            from_state = dot(g_ref[rows, lanes], st_ref[h, b], NT)
+            from_after = dot(v_ref[rows, lanes], st_ref[h, 2 + b], NT)
             gp_ref[h, 0, rows] = (
                 ab_ref[h, 0, rows].astype(F32) + ab_ref[h, 1, rows].astype(F32) * from_state
             ).astype(BF16)
@@ -247,8 +243,8 @@
         mine_ref[h] = jnp.where(first, part_q, part_k)
         send_ref[h] = jnp.where(first, part_k, part_q)
 
-    over_heads((st, tr, v, g, ab), (st_ref, tr_ref, v_ref, g_ref, ab_ref), sems,
-               [(gp_ref, gp)], out_sems, work)
+    over_heads((tr, ab), (tr_ref, ab_ref), sems,
+               [(gp_ref, gp), (st_ref, st)], out_sems, work)
 
 
 def k3b_body(core, ov_ref, dec_ref, st_ref, gp_ref, wq_ref, wk_ref,
@@ -272,6 +268,11 @@
     out_ref[...] = a_ref[...] + b_ref[...]
 
 
+def pass_body(mine_ref, inc_ref, out_ref):
+    for h in range(HEADS):
+        out_ref[h] = mine_ref[h, DH:DH + 1, :] * inc_ref[h] + mine_ref[h, 0:DH, :]
+
+
 def spread_first_body(core, in_ref, out_ref):
     spread_body(in_ref, out_ref)
 
@@ -323,7 +324,8 @@
     )
 
 
-def streamed(body, name, slots, back, held, out_shapes, whole_ins=(), scratch=()):
+def streamed(body, name, slots, back, held, out_shapes, whole_ins=(), scratch=(),
+             grant=None):
     raw = pl.BlockSpec(memory_space=pltpu.HBM)
     kept = pl.BlockSpec(memory_space=pltpu.VMEM)
     return pl.pallas_call(
@@ -337,7 +339,9 @@
             pltpu.SemaphoreType.DMA((len(back), HEADS)),
         ],
         name=name,
-        compiler_params=pltpu.CompilerParams(dimension_semantics=("arbitrary",)),
+        compiler_params=pltpu.CompilerParams(
+            dimension_semantics=("arbitrary",), vmem_limit_bytes=grant
+        ),
     )
 
 
@@ -403,24 +407,26 @@
         scratch=[pltpu.VMEM((BLOCK, 3 * BLOCK), BF16), pltpu.VMEM((HEADS, TOK), F32)],
     )(packed, core, *seqs, ld, *maps)
     scanned = small(
-        scan_body, "scan", 1, shape((CHIPS * ROWS, DH)), whole(CHIPS * ROWS, DH), smem=1,
+        scan_body, "scan", 1, pltpu.VMEM((CHIPS * ROWS, DH), F32),
+        pl.BlockSpec(memory_space=pltpu.VMEM), smem=1,
     )(mark, swapped.reshape(CHIPS * (ROWS + 1), DH))
     inc = exchange(scanned.reshape(CHIPS, ROWS * DH), ("z", "x")).reshape(HEADS, DH, DH)
-    passed = mine[:, DH:DH + 1, :] * inc + mine[:, :DH, :]
+    passed = small(
+        pass_body, "pass", 2, pltpu.VMEM((HEADS, DH, DH), F32),
+        pl.BlockSpec(memory_space=pltpu.VMEM),
+    )(mine, inc)
     recv = swap_cores(passed)
-    st = small(
-        states_body, "states", 3, pltpu.HBM((HEADS, 4, DH, DH), BF16), whole(HEADS, 4, DH, DH),
-        smem=1,
-    )(core, inc, recv, own)
     gp_dims = (HEADS, 2, TOK, DH)
-    gp, mine, send = streamed(
+    st_dims = (HEADS, 4, DH, DH)
+    half = pltpu.VMEM((HEADS, DH, DH), F32)
+    gp, st, mine, send = streamed(
         k3a_body, "k3a",
-        [pltpu.VMEM((HEADS, 4, DH, DH), BF16), pltpu.VMEM((HEADS, 2, DH, TOK), BF16), slot, slot,
-         pltpu.VMEM((HEADS, 4, TOK, DH), BF16)],
-        [pltpu.VMEM(gp_dims, BF16)], [False, True, True],
-        [pltpu.HBM(gp_dims, BF16), pltpu.VMEM((HEADS, DH, DH), F32),
-         pltpu.VMEM((HEADS, DH, DH), F32)],
-    )(core, st, tr, v, g, ab)
+        [pltpu.VMEM((HEADS, 2, DH, TOK), BF16), pltpu.VMEM((HEADS, 4, TOK, DH), BF16)],
+        [pltpu.VMEM(gp_dims, BF16), pltpu.VMEM(st_dims, BF16)], [False, False, True, True],
+        [pltpu.HBM(gp_dims, BF16), pltpu.HBM(st_dims, BF16), half, half],
+        whole_ins=[pl.BlockSpec(memory_space=pltpu.VMEM)] * 5, grant=20 << 20,
+    )(core, inc, recv, own, v, g,
+      *(pltpu.with_memory_space_constraint(x, pltpu.HBM) for x in (tr, ab)))
     recv = swap_cores(send)
     chip = small(add_body, "add", 2, MAT, whole(HEADS, DH, DH))(mine, recv)
     pieces = exchange(chip.reshape(16, -1), ("x", "dp"))

time: 126 us -> 124 us (0.984)
  blocking collectives: 25.1 us -> 46.4 us
  waiting for transfers between devices: 29.5 us -> 14.1 us
  starting transfers between devices: 32.6 us -> 26.6 us
  Pallas kernels: 36.7 us -> 34.3 us
    all_to_all x2 -> x3, blocking collectives: 25.1 us -> 46.4 us  [exchange(): return lax.all_to_all(x, axes, 0, 0, tiled=True)]
    all_to_all x3 -> x2, waiting for transfers between devices: 23.3 us -> 7.86 us  [exchange(): return lax.all_to_all(x, axes, 0, 0, tiled=True)]
    all_to_all x3 -> x2, starting transfers between devices: 21.5 us -> 15.4 us  [exchange(): return lax.all_to_all(x, axes, 0, 0, tiled=True)]
    pallas_call x3, Pallas kernels: 8.6 us -> 6.26 us  [the longest x1 5.33 us: local(): streamed(k3a_body, 'k3a', [pltpu.VMEM((HEADS, 2, DH, TOK), BF16), pltpu.V...]
  transfers between devices with their start and end apart: 7 -> 6, of which waited for: 7 -> 6; matrix products, arithmetic and copies ran while one was open for 0% -> 0% of each run, Pallas kernels for 15% -> 16%
where the time goes in v5:
time: 124 us; the launch traced here: 123 us
  blocking collectives  46.4 us (37%)
  Pallas kernels  34.3 us (28%)
  starting transfers between devices  26.6 us (21%)
  waiting for transfers between devices  14.1 us (11%)
    all_to_all x3, blocking collectives, exchange(): return lax.all_to_all(x, axes, 0, 0, tiled=True)  46.4 us
    all_to_all x2, starting transfers between devices, exchange(): return lax.all_to_all(x, axes, 0, 0, tiled=True)  15.4 us
    pallas_call x1, Pallas kernels, local(): call(k2_body, 'k2', [smem()] + [seq()] * 4 + [ld_spec] + map_specs, [per_...  13.5 us
    ppermute x4, starting transfers between devices, swap_cores(): return lax.ppermute(x, 'c', [(0, 1), (1, 0)])  11.2 us
    all_to_all x2, waiting for transfers between devices, exchange(): return lax.all_to_all(x, axes, 0, 0, tiled=True)  7.86 us
    pallas_call x1, Pallas kernels, local(): streamed(k1_body, 'k1', [slot] * 4 + [square] * 2, [pltpu.VMEM(own_dims,...  6.31 us
    ppermute x4, waiting for transfers between devices, swap_cores(): return lax.ppermute(x, 'c', [(0, 1), (1, 0)])  6.19 us
    pallas_call x1, Pallas kernels, local(): call(k3b_body, 'k3b', [smem(), per_head(2, TOK, DH, heads=WIDE), per_head...  5.8 us
  transfers between devices with their start and end apart: 6, of which 6 were waited for; matrix products, arithmetic and copies ran while one was open for 0% of the time, Pallas kernels for 16%

profile of v5, /device:TPU:1, one launch (start us, length us, event | category | flops | bytes accessed | tf_op | source)
XLA Modules:
  0.0 123.2 jit_solution(13886431614602878814)
XLA Ops:
  0.6 6.3 %k1.1 = (f32[8,136,128]{2,1,0:T(8,128)S(1)}, f32[8,136,128]{2,1,0:T(8,128)S(1)}, f32[8,272,128]{2,1,0:T(8,128)}) custom-call(s32[1]{0:T(128)} %bitcast.core.refs_1_, f32[8,512]{1,0:T(8,128)} %bitcast.43, bf16[512,1024]{1,0:T(8,128)(2,1)} %bitcast.37, bf16[512,1024]{1,0:T(8,128)(2,1)} %bitcast.39, bf16[512,1024]{1,0:T(8,128)(2,1)} %bitcast.23, ...), custom_call_target="tpu_custom_call" | custom-call | tf_op jit(solution)/shard_map/k1/pallas_call | solution.py:387
  7.0 3.3 %collective-permute-start = (f32[8,136,128]{2,1,0:T(8,128)S(1)}, f32[8,136,128]{2,1,0:T(8,128)S(1)}, u32[]{:S(2)}, u32[]{:S(2)}) collective-permute-start(f32[8,136,128]{2,1,0:T(8,128)S(1)} %get-tuple-element.24), channel_id=1, source_target_pairs={{0,4},{4,0},{1,5},{5,1},{2,6},{6,2},{3,7},{7,3},{8,12},{12,8},{9,1... | collective-permute-start | bytes 1671176 | tf_op jit(solution)/shard_map/ppermute | solution.py:367
  10.2 1.6 %collective-permute-done.refs_1_ = f32[8,136,128]{2,1,0:T(8,128)S(1)} collective-permute-done((f32[8,136,128]{2,1,0:T(8,128)S(1)}, f32[8,136,128]{2,1,0:T(8,128)S(1)}, u32[]{:S(2)}, u32[]{:S(2)}) %collective-permute-start) | collective-permute-done | bytes 557088 | tf_op jit(solution)/shard_map/ppermute | solution.py:367
  11.8 0.9 combine.1.refs_0_
  12.7 9.3 %all-to-all-start = ((f32[32,1,4224]{2,1,0:T(1,128)}), f32[32,1,4224]{2,1,0:T(1,128)S(1)}, u32[]{:S(2)}, u32[]{:S(2)}) async-start(f32[32,1,4224]{2,1,0:T(1,128)} %bitcast.6), calls=%async_computation | async-start | bytes 1081344 | tf_op jit(solution)/shard_map/all_to_all | solution.py:363
  22.0 13.5 %k2.1 = (bf16[8,4,512,128]{3,2,1,0:T(8,128)(2,1)}, f32[8,2,512,128]{3,2,1,0:T(8,128)}, bf16[8,2,512,128]{3,2,1,0:T(8,128)(2,1)}, bf16[8,2,128,512]{3,2,1,0:T(8,128)(2,1)}, s32[1]{0:T(128)}) custom-call(f32[1056,128]{1,0:T(8,128)} %combine.1.refs_0_, s32[1]{0:T(128)} %bitcast.core.refs_1_, bf16[512,1024]{1,0:T(8,128)(2,1)} %bitcast.38, ...), custom_call_target="tpu_custom_call" | custom-call | flops 1073741824 | bytes 1048576 | tf_op jit(solution)/shard_map/k2/pallas_call | solution.py:397
  35.6 0.0 copy-start
  35.6 0.0 copy-start.1
  35.6 3.3 %all-to-all-done = f32[32,1,4224]{2,1,0:T(1,128)S(1)} async-done(((f32[32,1,4224]{2,1,0:T(1,128)}), f32[32,1,4224]{2,1,0:T(1,128)S(1)}, u32[]{:S(2)}, u32[]{:S(2)}) %all-to-all-start) | async-done | bytes 540704 | tf_op jit(solution)/shard_map/all_to_all | solution.py:363
  38.9 0.0 copy-start.2
  38.9 0.9 scan.1
  39.7 21.4 %all_to_all.45 = f32[32,1,4096]{2,1,0:T(1,128)S(1)} all-to-all(f32[32,1,4096]{2,1,0:T(1,128)S(1)} %bitcast.33), channel_id=1, replica_groups=mesh['z'=8,'x'=4,'c'=2,'dp'=4] {'z','x'}, dimensions={0} | all-to-all | bytes 1048576 | tf_op jit(solution)/shard_map/all_to_all | solution.py:363
  61.1 0.1 pass.1
  61.2 3.4 %collective-permute-start.1 = (f32[8,128,128]{2,1,0:T(8,128)S(1)}, f32[8,128,128]{2,1,0:T(8,128)S(1)}, u32[]{:S(2)}, u32[]{:S(2)}) collective-permute-start(f32[8,128,128]{2,1,0:T(8,128)S(1)} %pass.1), channel_id=1, source_target_pairs={{0,4},{4,0},{1,5},{5,1},{2,6},{6,2},{3,7},{7,3},{8,12},{12,8},{9,1... | collective-permute-start | bytes 1572872 | tf_op jit(solution)/shard_map/ppermute | solution.py:367
  64.5 1.5 %collective-permute-done.1.recv_ref = f32[8,128,128]{2,1,0:T(8,128)S(1)} collective-permute-done((f32[8,128,128]{2,1,0:T(8,128)S(1)}, f32[8,128,128]{2,1,0:T(8,128)S(1)}, u32[]{:S(2)}, u32[]{:S(2)}) %collective-permute-start.1) | collective-permute-done | bytes 524320 | tf_op jit(solution)/shard_map/ppermute | solution.py:367
  66.1 0.0 copy-done
  66.1 0.0 copy-done.1
  66.1 0.0 copy-done.2
  66.1 5.3 %k3a.1 = (bf16[8,2,512,128]{3,2,1,0:T(8,128)(2,1)}, bf16[8,4,128,128]{3,2,1,0:T(8,128)(2,1)}, f32[8,128,128]{2,1,0:T(8,128)S(1)}, f32[8,128,128]{2,1,0:T(8,128)S(1)}) custom-call(s32[1]{0:T(128)} %bitcast.core.refs_1_, f32[8,128,128]{2,1,0:T(8,128)S(1)} %bitcast.30, f32[8,128,128]{2,1,0:T(8,128)S(1)} %collective-permute-done.1.recv_ref, ...), custom_call_target="tpu_custom_call" | custom-call | tf_op jit(solution)/shard_map/k3a/pallas_call | solution.py:422
  71.4 0.5 collective-permute-start.2
  71.9 1.5 %collective-permute-done.2.refs_1_ = f32[8,128,128]{2,1,0:T(8,128)S(1)} collective-permute-done((f32[8,128,128]{2,1,0:T(8,128)S(1)}, f32[8,128,128]{2,1,0:T(8,128)S(1)}, u32[]{:S(2)}, u32[]{:S(2)}) %collective-permute-start.2) | collective-permute-done | bytes 524320 | tf_op jit(solution)/shard_map/ppermute | solution.py:367
  73.4 0.8 add.1.refs_0_
  74.3 6.1 %all-to-all-start.2 = ((f32[16,1,8192]{2,1,0:T(1,128)}), f32[16,1,8192]{2,1,0:T(1,128)S(1)}, u32[]{:S(2)}, u32[]{:S(2)}) async-start(f32[16,1,8192]{2,1,0:T(1,128)} %bitcast.14), calls=%async_computation.2 | async-start | bytes 1048576 | tf_op jit(solution)/shard_map/all_to_all | solution.py:363
  80.4 5.8 %k3b.1 = (bf16[512,1024]{1,0:T(8,128)(2,1)}, bf16[512,1024]{1,0:T(8,128)(2,1)}, bf16[512,1024]{1,0:T(8,128)(2,1)}, bf16[512,1024]{1,0:T(8,128)(2,1)}, s32[1]{0:T(128)}) custom-call(f32[8,128,128]{2,1,0:T(8,128)} %add.1.refs_0_, s32[1]{0:T(128)} %bitcast.core.refs_1_, f32[8,2,512,128]{3,2,1,0:T(8,128)} %get-tuple-element.31.refs_2_, ...), custom_call_target="tpu_custom_call" | custom-call | flops 1073741824 | bytes 1048576 | tf_op jit(solution)/shard_map/k3b/pallas_call | solution.py:434
  86.2 4.6 %all-to-all-done.2 = f32[16,1,8192]{2,1,0:T(1,128)S(1)} async-done(((f32[16,1,8192]{2,1,0:T(1,128)}), f32[16,1,8192]{2,1,0:T(1,128)S(1)}, u32[]{:S(2)}, u32[]{:S(2)}) %all-to-all-start.2) | async-done | bytes 524320 | tf_op jit(solution)/shard_map/all_to_all | solution.py:363
  90.8 0.7 spread_z.1
  91.4 11.6 %all_to_all.46 = f32[8,1,8192]{2,1,0:T(1,128)S(1)} all-to-all(f32[8,1,8192]{2,1,0:T(1,128)S(1)} %bitcast.36), channel_id=1, replica_groups=mesh['z'=8,'x'=4,'c'=2,'dp'=4] {'z'}, dimensions={0} | all-to-all | bytes 524288 | tf_op jit(solution)/shard_map/all_to_all | solution.py:363
  103.1 0.1 spread_xy.1
  103.1 13.4 %all_to_all.47 = f32[16,1,8192]{2,1,0:T(1,128)S(1)} all-to-all(f32[16,1,8192]{2,1,0:T(1,128)S(1)} %bitcast.34), channel_id=1, replica_groups=mesh['z'=8,'x'=4,'c'=2,'dp'=4] {'x','dp'}, dimensions={0} | all-to-all | bytes 1048576 | tf_op jit(solution)/shard_map/all_to_all | solution.py:363
  116.6 4.1 %collective-permute-start.3 = (f32[8,128,128]{2,1,0:T(8,128)S(1)}, f32[8,128,128]{2,1,0:T(8,128)S(1)}, u32[]{:S(2)}, u32[]{:S(2)}) collective-permute-start(f32[8,128,128]{2,1,0:T(8,128)S(1)} %bitcast.41), channel_id=1, source_target_pairs={{0,4},{4,0},{1,5},{5,1},{2,6},{6,2},{3,7},{7,3},{8,12},{12,8},{9,1... | collective-permute-start | bytes 1572872 | tf_op jit(solution)/shard_map/ppermute | solution.py:367
  120.6 1.5 %collective-permute-done.3 = f32[8,128,128]{2,1,0:T(8,128)S(1)} collective-permute-done((f32[8,128,128]{2,1,0:T(8,128)S(1)}, f32[8,128,128]{2,1,0:T(8,128)S(1)}, u32[]{:S(2)}, u32[]{:S(2)}) %collective-permute-start.3) | collective-permute-done | bytes 524320 | tf_op jit(solution)/shard_map/ppermute | solution.py:367
  122.2 1.1 broadcast_select_fusion
Async XLA Ops:
  7.0 4.9 %collective-permute-start = (f32[8,136,128]{2,1,0:T(8,128)S(1)}, f32[8,136,128]{2,1,0:T(8,128)S(1)}, u32[]{:S(2)}, u32[]{:S(2)}) collective-permute-start(f32[8,136,128]{2,1,0:T(8,128)S(1)} %get-tuple-element.24), channel_id=1, source_target_pairs={{0,4},{4,0},{1,5},{5,1},{2,6},{6,2},{3,7},{7,3},{8,12},{12,8},{9,1... | collective-permute-start | bytes 1671176 | tf_op jit(solution)/shard_map/ppermute | solution.py:367
  12.7 26.2 %all-to-all-start = ((f32[32,1,4224]{2,1,0:T(1,128)}), f32[32,1,4224]{2,1,0:T(1,128)S(1)}, u32[]{:S(2)}, u32[]{:S(2)}) async-start(f32[32,1,4224]{2,1,0:T(1,128)} %bitcast.6), calls=%async_computation | async-start | bytes 1081344 | tf_op jit(solution)/shard_map/all_to_all | solution.py:363
  35.6 30.5 %copy-start = (bf16[1,512,1024]{2,1,0:T(8,128)(2,1)S(1)}, bf16[1,512,1024]{2,1,0:T(8,128)(2,1)}, u32[]{:S(2)}) copy-start(bf16[1,512,1024]{2,1,0:T(8,128)(2,1)} %param.9) | copy-start | bytes 3145732
  35.6 30.5 %copy-start.1 = (bf16[1,512,1024]{2,1,0:T(8,128)(2,1)S(1)}, bf16[1,512,1024]{2,1,0:T(8,128)(2,1)}, u32[]{:S(2)}) copy-start(bf16[1,512,1024]{2,1,0:T(8,128)(2,1)} %param.11) | copy-start | bytes 3145732
  38.9 27.2 %copy-start.2 = (f32[8,272,128]{2,1,0:T(8,128)S(1)}, f32[8,272,128]{2,1,0:T(8,128)}, u32[]{:S(2)}) copy-start(f32[8,272,128]{2,1,0:T(8,128)} %get-tuple-element.26.own_ref) | copy-start | bytes 3342340
  61.2 4.9 %collective-permute-start.1 = (f32[8,128,128]{2,1,0:T(8,128)S(1)}, f32[8,128,128]{2,1,0:T(8,128)S(1)}, u32[]{:S(2)}, u32[]{:S(2)}) collective-permute-start(f32[8,128,128]{2,1,0:T(8,128)S(1)} %pass.1), channel_id=1, source_target_pairs={{0,4},{4,0},{1,5},{5,1},{2,6},{6,2},{3,7},{7,3},{8,12},{12,8},{9,1... | collective-permute-start | bytes 1572872 | tf_op jit(solution)/shard_map/ppermute | solution.py:367
  71.4 2.0 %collective-permute-start.2 = (f32[8,128,128]{2,1,0:T(8,128)S(1)}, f32[8,128,128]{2,1,0:T(8,128)S(1)}, u32[]{:S(2)}, u32[]{:S(2)}) collective-permute-start(f32[8,128,128]{2,1,0:T(8,128)S(1)} %get-tuple-element.30), channel_id=1, source_target_pairs={{0,4},{4,0},{1,5},{5,1},{2,6},{6,2},{3,7},{7,3},{8,12},{12,8},{9,1... | collective-permute-start | bytes 1572872 | tf_op jit(solution)/shard_map/ppermute | solution.py:367
  74.3 16.5 %all-to-all-start.2 = ((f32[16,1,8192]{2,1,0:T(1,128)}), f32[16,1,8192]{2,1,0:T(1,128)S(1)}, u32[]{:S(2)}, u32[]{:S(2)}) async-start(f32[16,1,8192]{2,1,0:T(1,128)} %bitcast.14), calls=%async_computation.2 | async-start | bytes 1048576 | tf_op jit(solution)/shard_map/all_to_all | solution.py:363
  116.6 5.6 %collective-permute-start.3 = (f32[8,128,128]{2,1,0:T(8,128)S(1)}, f32[8,128,128]{2,1,0:T(8,128)S(1)}, u32[]{:S(2)}, u32[]{:S(2)}) collective-permute-start(f32[8,128,128]{2,1,0:T(8,128)S(1)} %bitcast.41), channel_id=1, source_target_pairs={{0,4},{4,0},{1,5},{5,1},{2,6},{6,2},{3,7},{7,3},{8,12},{12,8},{9,1... | collective-permute-start | bytes 1572872 | tf_op jit(solution)/shard_map/ppermute | solution.py:367

commit v6 on v5

--- a/solution.py
+++ b/solution.py
@@ -67,10 +67,12 @@
     ]
 
 
-def over_heads(srcs, bufs, sems, outs, out_sems, work):
+def over_heads(srcs, bufs, sems, outs, out_sems, work, before=None):
     for h in range(HEADS):
         for copy in head_copies(srcs, bufs, sems, h):
             copy.start()
+    if before is not None:
+        before()
 
     def back(h):
         return [
@@ -95,13 +97,19 @@
             copy.wait()
 
 
-def k1_body(core, ld_ref, q, k, v, g, wq, wk, mine_ref, send_ref, own,
-            q_ref, k_ref, v_ref, g_ref, wq_ref, wk_ref, own_ref, cum_ref, sems, out_sems):
+def k1_body(core, ld, q, k, v, g, wq, wk, mine_ref, send_ref, own,
+            q_ref, k_ref, v_ref, g_ref, wq_ref, wk_ref, own_ref, ld_ref, cum_ref, ld_sem,
+            sems, out_sems):
     first = core[0] == 0
-    low = lower3()
-    for b in range(2):
-        rows = slice(b * BLOCK, (b + 1) * BLOCK)
-        cum_ref[:, rows] = cumul_rows(low, ld_ref[:, rows])
+    decays = pltpu.make_async_copy(ld, ld_ref, ld_sem.at[0])
+    decays.start()
+
+    def running_sums():
+        low = lower3()
+        decays.wait()
+        for b in range(2):
+            rows = slice(b * BLOCK, (b + 1) * BLOCK)
+            cum_ref[:, rows] = cumul_rows(low, ld_ref[:, rows])
 
     def work(h):
         ups, cons, tots = [], [], []
@@ -133,7 +141,7 @@
         own_ref[h, 2 * DH + 8:, :] = d1
 
     over_heads((q, k, v, g, wq, wk), (q_ref, k_ref, v_ref, g_ref, wq_ref, wk_ref), sems,
-               [(own_ref, own)], out_sems, work)
+               [(own_ref, own)], out_sems, work, running_sums)
 
 
 def combine_body(mine_ref, recv_ref, out_ref):
@@ -247,8 +255,7 @@
                [(gp_ref, gp), (st_ref, st)], out_sems, work)
 
 
-def k3b_body(core, ov_ref, dec_ref, st_ref, gp_ref, wq_ref, wk_ref,
-             out_ref, gq_ref, gk_ref, gv_ref, mark_ref):
+def k3b_body(core, ov_ref, dec_ref, st_ref, out_ref, gv_ref, mark_ref):
     mark_ref[0] = core[0]
     for i in range(WIDE):
         lanes = slice(i * DH, (i + 1) * DH)
@@ -260,8 +267,14 @@
             gv_ref[rows, lanes] = (
                 ov_ref[i, 1, rows] + SCALE * dot(dec_ref[i, 1, rows], st_ref[i, 2 + b])
             ).astype(BF16)
-            gq_ref[rows, lanes] = dot(gp_ref[i, 0, rows], wq_ref[i], NT).astype(BF16)
-            gk_ref[rows, lanes] = dot(gp_ref[i, 1, rows], wk_ref[i], NT).astype(BF16)
+
+
+def k3c_body(core, gp_ref, wq_ref, wk_ref, gq_ref, gk_ref, mark_ref):
+    mark_ref[0] = core[0]
+    for i in range(WIDE):
+        lanes = slice(i * DH, (i + 1) * DH)
+        gq_ref[:, lanes] = dot(gp_ref[i, 0], wq_ref[i], NT).astype(BF16)
+        gk_ref[:, lanes] = dot(gp_ref[i, 1], wk_ref[i], NT).astype(BF16)
 
 
 def add_body(a_ref, b_ref, out_ref):
@@ -387,7 +400,8 @@
     mine, send, own = streamed(
         k1_body, "k1", [slot] * 4 + [square] * 2, [pltpu.VMEM(own_dims, F32)],
         [True, True, False], [cut, cut, pltpu.HBM(own_dims, F32)],
-        whole_ins=[ld_spec], scratch=[pltpu.VMEM((HEADS, TOK), F32)],
+        whole_ins=[pl.BlockSpec(memory_space=pltpu.HBM)],
+        scratch=[pltpu.VMEM((HEADS, TOK), F32)] * 2 + [pltpu.SemaphoreType.DMA((1,))],
     )(core, ld, *seqs, *maps)
     recv = swap_cores(send)
     packed = small(
@@ -431,25 +445,32 @@
     chip = small(add_body, "add", 2, MAT, whole(HEADS, DH, DH))(mine, recv)
     pieces = exchange(chip.reshape(16, -1), ("x", "dp"))
     rows = HEADS * DH // 16
-    out, gq, gk, gv, mark = call(
+    wide = [per_head(2, TOK, DH, heads=WIDE)]
+    out, gv, mark = call(
         k3b_body, "k3b",
-        [smem(), per_head(2, TOK, DH, heads=WIDE), per_head(2, TOK, DH, heads=WIDE),
-         per_head(4, DH, DH, heads=WIDE), per_head(2, TOK, DH, heads=WIDE)]
-        + [per_head(DH, DH, heads=WIDE)] * 2,
-        [seq(WIDE)] * 4 + [smem()],
-
-        [SEQ_B] * 4 + [shape((1,), jnp.int32)],
+        [smem()] + wide * 2 + [per_head(4, DH, DH, heads=WIDE)],
+        [seq(WIDE)] * 2 + [smem()],
+        [SEQ_B] * 2 + [shape((1,), jnp.int32)],
         flops=1 << 30,
         after=1,
         grid=HEADS // WIDE,
-    )(chip, core, ov, dec, st, gp, *maps)
-    spread = small(spread_first_body, "spread_z", 1, shape((8, rows, DH)), whole(8, rows, DH), smem=1)(
-        mark, pieces.reshape(16, rows, DH)
-    )
+    )(chip, core, ov, dec, st)
+    spread = small(
+        spread_first_body, "spread_z", 1, pltpu.HBM((8, rows, DH), F32), whole(8, rows, DH), smem=1
+    )(mark, pieces.reshape(16, rows, DH))
     pieces = exchange(spread.reshape(8, -1), "z")
-    spread = small(spread_body, "spread_xy", 1, shape((16, rows, DH)), whole(16, rows, DH))(
-        pieces.reshape(8, rows, DH)
-    )
+    gq, gk, mark = call(
+        k3c_body, "k3c",
+        [smem()] + wide + [per_head(DH, DH, heads=WIDE)] * 2,
+        [seq(WIDE)] * 2 + [smem()],
+        [SEQ_B] * 2 + [shape((1,), jnp.int32)],
+        flops=1 << 30,
+        after=1,
+        grid=HEADS // WIDE,
+    )(spread, core, gp, *maps)
+    spread = small(
+        spread_first_body, "spread_xy", 1, shape((16, rows, DH)), whole(16, rows, DH), smem=1
+    )(mark, pieces.reshape(8, rows, DH))
     own = exchange(spread.reshape(16, -1), ("x", "dp")).reshape(HEADS, DH, DH)
     other = swap_cores(own)
     first = core[0] == 0

time: 124 us -> 127 us (1.024)
  blocking collectives: 46.4 us -> 34.8 us
  waiting for transfers between devices: 14.1 us -> 21.3 us
  Pallas kernels: 34.3 us -> 38.1 us
  starting transfers between devices: 26.6 us -> 30 us
    all_to_all x3 -> x2, blocking collectives: 46.4 us -> 34.8 us  [exchange(): return lax.all_to_all(x, axes, 0, 0, tiled=True)]
    all_to_all x2 -> x3, waiting for transfers between devices: 7.86 us -> 15.1 us  [exchange(): return lax.all_to_all(x, axes, 0, 0, tiled=True)]
    all_to_all x2 -> x3, starting transfers between devices: 15.4 us -> 18.9 us  [exchange(): return lax.all_to_all(x, axes, 0, 0, tiled=True)]
    pallas_call x3 -> x4, Pallas kernels: 6.51 us -> 9.8 us  [the longest x1 4.48 us: local(): call(k3b_body, 'k3b', [smem()] + wide * 2 + [per_head(4, DH, DH, heads=WI...]
  transfers between devices with their start and end apart: 6 -> 7, of which waited for: 6 -> 7; matrix products, arithmetic and copies ran while one was open for 0% -> 0% of each run, Pallas kernels for 16% -> 17%
where the time goes in v6:
time: 127 us; the launch traced here: 126 us
  Pallas kernels  38.1 us (30%)
  blocking collectives  34.8 us (27%)
  starting transfers between devices  30 us (24%)
  waiting for transfers between devices  21.3 us (17%)
    all_to_all x2, blocking collectives, exchange(): return lax.all_to_all(x, axes, 0, 0, tiled=True)  34.8 us
    all_to_all x3, starting transfers between devices, exchange(): return lax.all_to_all(x, axes, 0, 0, tiled=True)  18.9 us
    all_to_all x3, waiting for transfers between devices, exchange(): return lax.all_to_all(x, axes, 0, 0, tiled=True)  15.1 us
    pallas_call x1, Pallas kernels, local(): call(k2_body, 'k2', [smem()] + [seq()] * 4 + [ld_spec] + map_specs, [per_...  13.5 us
    ppermute x4, starting transfers between devices, swap_cores(): return lax.ppermute(x, 'c', [(0, 1), (1, 0)])  11.2 us
    pallas_call x1, Pallas kernels, local(): streamed(k1_body, 'k1', [slot] * 4 + [square] * 2, [pltpu.VMEM(own_dims,...  6.93 us
    ppermute x4, waiting for transfers between devices, swap_cores(): return lax.ppermute(x, 'c', [(0, 1), (1, 0)])  6.19 us
    pallas_call x1, Pallas kernels, local(): streamed(k3a_body, 'k3a', [pltpu.VMEM((HEADS, 2, DH, TOK), BF16), pltpu.V...  5.25 us
  transfers between devices with their start and end apart: 7, of which 7 were waited for; matrix products, arithmetic and copies ran while one was open for 0% of the time, Pallas kernels for 17%

profile of v6, /device:TPU:1, one launch (start us, length us, event | category | flops | bytes accessed | tf_op | source)
XLA Modules:
  0.0 126.1 jit_solution(11880367185111996975)
XLA Ops:
  0.6 6.9 %k1.1 = (f32[8,136,128]{2,1,0:T(8,128)S(1)}, f32[8,136,128]{2,1,0:T(8,128)S(1)}, f32[8,272,128]{2,1,0:T(8,128)}) custom-call(s32[1]{0:T(128)} %bitcast.core.refs_1_, f32[8,512]{1,0:T(8,128)} %bitcast.43, bf16[512,1024]{1,0:T(8,128)(2,1)} %bitcast.36, bf16[512,1024]{1,0:T(8,128)(2,1)} %bitcast.38, bf16[512,1024]{1,0:T(8,128)(2,1)} %bitcast.23, ...), custom_call_target="tpu_custom_call" | custom-call | tf_op jit(solution)/shard_map/k1/pallas_call | solution.py:400
  7.6 3.3 %collective-permute-start = (f32[8,136,128]{2,1,0:T(8,128)S(1)}, f32[8,136,128]{2,1,0:T(8,128)S(1)}, u32[]{:S(2)}, u32[]{:S(2)}) collective-permute-start(f32[8,136,128]{2,1,0:T(8,128)S(1)} %get-tuple-element.25), channel_id=1, source_target_pairs={{0,4},{4,0},{1,5},{5,1},{2,6},{6,2},{3,7},{7,3},{8,12},{12,8},{9,1... | collective-permute-start | bytes 1671176 | tf_op jit(solution)/shard_map/ppermute | solution.py:380
  10.9 1.6 %collective-permute-done.refs_1_ = f32[8,136,128]{2,1,0:T(8,128)S(1)} collective-permute-done((f32[8,136,128]{2,1,0:T(8,128)S(1)}, f32[8,136,128]{2,1,0:T(8,128)S(1)}, u32[]{:S(2)}, u32[]{:S(2)}) %collective-permute-start) | collective-permute-done | bytes 557088 | tf_op jit(solution)/shard_map/ppermute | solution.py:380
  12.4 0.9 combine.1.refs_0_
  13.3 9.3 %all-to-all-start = ((f32[32,1,4224]{2,1,0:T(1,128)}), f32[32,1,4224]{2,1,0:T(1,128)S(1)}, u32[]{:S(2)}, u32[]{:S(2)}) async-start(f32[32,1,4224]{2,1,0:T(1,128)} %bitcast.6), calls=%async_computation | async-start | bytes 1081344 | tf_op jit(solution)/shard_map/all_to_all | solution.py:376
  22.6 13.5 %k2.1 = (bf16[8,4,512,128]{3,2,1,0:T(8,128)(2,1)}, f32[8,2,512,128]{3,2,1,0:T(8,128)}, bf16[8,2,512,128]{3,2,1,0:T(8,128)(2,1)}, bf16[8,2,128,512]{3,2,1,0:T(8,128)(2,1)}, s32[1]{0:T(128)}) custom-call(f32[1056,128]{1,0:T(8,128)} %combine.1.refs_0_, s32[1]{0:T(128)} %bitcast.core.refs_1_, bf16[512,1024]{1,0:T(8,128)(2,1)} %bitcast.37, ...), custom_call_target="tpu_custom_call" | custom-call | flops 1073741824 | bytes 1048576 | tf_op jit(solution)/shard_map/k2/pallas_call | solution.py:411
  36.2 0.0 copy-start
  36.2 0.0 copy-start.1
  36.2 3.3 %all-to-all-done = f32[32,1,4224]{2,1,0:T(1,128)S(1)} async-done(((f32[32,1,4224]{2,1,0:T(1,128)}), f32[32,1,4224]{2,1,0:T(1,128)S(1)}, u32[]{:S(2)}, u32[]{:S(2)}) %all-to-all-start) | async-done | bytes 540704 | tf_op jit(solution)/shard_map/all_to_all | solution.py:376
  39.5 0.0 copy-start.2
  39.5 0.9 scan.1
  40.3 21.4 %all_to_all.45 = f32[32,1,4096]{2,1,0:T(1,128)S(1)} all-to-all(f32[32,1,4096]{2,1,0:T(1,128)S(1)} %bitcast.33), channel_id=1, replica_groups=mesh['z'=8,'x'=4,'c'=2,'dp'=4] {'z','x'}, dimensions={0} | all-to-all | bytes 1048576 | tf_op jit(solution)/shard_map/all_to_all | solution.py:376
  61.7 0.1 pass.1
  61.8 3.4 %collective-permute-start.1 = (f32[8,128,128]{2,1,0:T(8,128)S(1)}, f32[8,128,128]{2,1,0:T(8,128)S(1)}, u32[]{:S(2)}, u32[]{:S(2)}) collective-permute-start(f32[8,128,128]{2,1,0:T(8,128)S(1)} %pass.1), channel_id=1, source_target_pairs={{0,4},{4,0},{1,5},{5,1},{2,6},{6,2},{3,7},{7,3},{8,12},{12,8},{9,1... | collective-permute-start | bytes 1572872 | tf_op jit(solution)/shard_map/ppermute | solution.py:380
  65.1 1.5 %collective-permute-done.1.recv_ref = f32[8,128,128]{2,1,0:T(8,128)S(1)} collective-permute-done((f32[8,128,128]{2,1,0:T(8,128)S(1)}, f32[8,128,128]{2,1,0:T(8,128)S(1)}, u32[]{:S(2)}, u32[]{:S(2)}) %collective-permute-start.1) | collective-permute-done | bytes 524320 | tf_op jit(solution)/shard_map/ppermute | solution.py:380
  66.7 0.0 copy-done
  66.7 0.0 copy-done.1
  66.7 0.0 copy-done.2
  66.7 5.3 %k3a.1 = (bf16[8,2,512,128]{3,2,1,0:T(8,128)(2,1)}, bf16[8,4,128,128]{3,2,1,0:T(8,128)(2,1)}, f32[8,128,128]{2,1,0:T(8,128)S(1)}, f32[8,128,128]{2,1,0:T(8,128)S(1)}) custom-call(s32[1]{0:T(128)} %bitcast.core.refs_1_, f32[8,128,128]{2,1,0:T(8,128)S(1)} %bitcast.30, f32[8,128,128]{2,1,0:T(8,128)S(1)} %collective-permute-done.1.recv_ref, ...), custom_call_target="tpu_custom_call" | custom-call | tf_op jit(solution)/shard_map/k3a/pallas_call | solution.py:436
  71.9 0.5 collective-permute-start.2
  72.4 1.5 %collective-permute-done.2.refs_1_ = f32[8,128,128]{2,1,0:T(8,128)S(1)} collective-permute-done((f32[8,128,128]{2,1,0:T(8,128)S(1)}, f32[8,128,128]{2,1,0:T(8,128)S(1)}, u32[]{:S(2)}, u32[]{:S(2)}) %collective-permute-start.2) | collective-permute-done | bytes 524320 | tf_op jit(solution)/shard_map/ppermute | solution.py:380
  73.9 0.8 add.1.refs_0_
  74.8 6.1 %all-to-all-start.2 = ((f32[16,1,8192]{2,1,0:T(1,128)}), f32[16,1,8192]{2,1,0:T(1,128)S(1)}, u32[]{:S(2)}, u32[]{:S(2)}) async-start(f32[16,1,8192]{2,1,0:T(1,128)} %bitcast.11), calls=%async_computation.2 | async-start | bytes 1048576 | tf_op jit(solution)/shard_map/all_to_all | solution.py:376
  80.9 4.5 %k3b.1 = (bf16[512,1024]{1,0:T(8,128)(2,1)}, bf16[512,1024]{1,0:T(8,128)(2,1)}, s32[1]{0:T(128)}) custom-call(f32[8,128,128]{2,1,0:T(8,128)} %add.1.refs_0_, s32[1]{0:T(128)} %bitcast.core.refs_1_, f32[8,2,512,128]{3,2,1,0:T(8,128)} %get-tuple-element.32.refs_2_, bf16[8,2,512,128]{3,2,1,0:T(8,128)(2,1)} %get-tuple-element.33.refs_3_, ...), custom_call_target="tpu_custom_call" | custom-call | flops 1073741824 | bytes 1048576 | tf_op jit(solution)/shard_map/k3b/pallas_call | solution.py:449
  85.4 5.9 %all-to-all-done.2 = f32[16,1,8192]{2,1,0:T(1,128)S(1)} async-done(((f32[16,1,8192]{2,1,0:T(1,128)}), f32[16,1,8192]{2,1,0:T(1,128)S(1)}, u32[]{:S(2)}, u32[]{:S(2)}) %all-to-all-start.2) | async-done | bytes 524320 | tf_op jit(solution)/shard_map/all_to_all | solution.py:376
  91.3 1.4 %spread_z.1.refs_0_ = f32[8,64,128]{2,1,0:T(8,128)} custom-call(s32[1]{0:T(128)} %get-tuple-element.36.refs_0_, f32[16,64,128]{2,1,0:T(8,128)S(1)} %bitcast.32), custom_call_target="tpu_custom_call" | custom-call | tf_op jit(solution)/shard_map/spread_z/pallas_call | solution.py:458
  92.7 3.4 %all-to-all-start.3 = ((f32[8,1,8192]{2,1,0:T(1,128)}), f32[8,1,8192]{2,1,0:T(1,128)S(1)}, u32[]{:S(2)}, u32[]{:S(2)}) async-start(f32[8,1,8192]{2,1,0:T(1,128)} %bitcast.42), calls=%async_computation.3 | async-start | bytes 524288 | tf_op jit(solution)/shard_map/all_to_all | solution.py:376
  96.1 3.2 %k3c.1 = (bf16[512,1024]{1,0:T(8,128)(2,1)}, bf16[512,1024]{1,0:T(8,128)(2,1)}, s32[1]{0:T(128)}) custom-call(f32[8,64,128]{2,1,0:T(8,128)} %spread_z.1.refs_0_, s32[1]{0:T(128)} %bitcast.core.refs_1_, bf16[8,2,512,128]{3,2,1,0:T(8,128)(2,1)} %get-tuple-element.37.refs_2_, bf16[8,128,128]{2,1,0:T(8,128)(2,1)} %refs_3_.1, bf16[8,128,128]{2,1,0:T(8,128)(2,1)} %refs_4_.1), custom_call_target="tpu_custom_call" | custom-call | flops 1073741824 | bytes 1048576 | tf_op jit(solution)/shard_map/k3c/pallas_call | solution.py:462
  99.3 5.9 %all-to-all-done.3 = f32[8,1,8192]{2,1,0:T(1,128)S(1)} async-done(((f32[8,1,8192]{2,1,0:T(1,128)}), f32[8,1,8192]{2,1,0:T(1,128)S(1)}, u32[]{:S(2)}, u32[]{:S(2)}) %all-to-all-start.3) | async-done | bytes 262176 | tf_op jit(solution)/shard_map/all_to_all | solution.py:376
  105.2 0.7 spread_xy.1
  106.0 13.5 %all_to_all.46 = f32[16,1,8192]{2,1,0:T(1,128)S(1)} all-to-all(f32[16,1,8192]{2,1,0:T(1,128)S(1)} %bitcast.34), channel_id=1, replica_groups=mesh['z'=8,'x'=4,'c'=2,'dp'=4] {'x','dp'}, dimensions={0} | all-to-all | bytes 1048576 | tf_op jit(solution)/shard_map/all_to_all | solution.py:376
  119.4 4.1 %collective-permute-start.3 = (f32[8,128,128]{2,1,0:T(8,128)S(1)}, f32[8,128,128]{2,1,0:T(8,128)S(1)}, u32[]{:S(2)}, u32[]{:S(2)}) collective-permute-start(f32[8,128,128]{2,1,0:T(8,128)S(1)} %bitcast.40), channel_id=1, source_target_pairs={{0,4},{4,0},{1,5},{5,1},{2,6},{6,2},{3,7},{7,3},{8,12},{12,8},{9,1... | collective-permute-start | bytes 1572872 | tf_op jit(solution)/shard_map/ppermute | solution.py:380
  123.5 1.5 %collective-permute-done.3 = f32[8,128,128]{2,1,0:T(8,128)S(1)} collective-permute-done((f32[8,128,128]{2,1,0:T(8,128)S(1)}, f32[8,128,128]{2,1,0:T(8,128)S(1)}, u32[]{:S(2)}, u32[]{:S(2)}) %collective-permute-start.3) | collective-permute-done | bytes 524320 | tf_op jit(solution)/shard_map/ppermute | solution.py:380
  125.0 1.1 broadcast_select_fusion
Async XLA Ops:
  7.6 4.9 %collective-permute-start = (f32[8,136,128]{2,1,0:T(8,128)S(1)}, f32[8,136,128]{2,1,0:T(8,128)S(1)}, u32[]{:S(2)}, u32[]{:S(2)}) collective-permute-start(f32[8,136,128]{2,1,0:T(8,128)S(1)} %get-tuple-element.25), channel_id=1, source_target_pairs={{0,4},{4,0},{1,5},{5,1},{2,6},{6,2},{3,7},{7,3},{8,12},{12,8},{9,1... | collective-permute-start | bytes 1671176 | tf_op jit(solution)/shard_map/ppermute | solution.py:380
  13.3 26.2 %all-to-all-start = ((f32[32,1,4224]{2,1,0:T(1,128)}), f32[32,1,4224]{2,1,0:T(1,128)S(1)}, u32[]{:S(2)}, u32[]{:S(2)}) async-start(f32[32,1,4224]{2,1,0:T(1,128)} %bitcast.6), calls=%async_computation | async-start | bytes 1081344 | tf_op jit(solution)/shard_map/all_to_all | solution.py:376
  36.2 30.5 %copy-start = (bf16[1,512,1024]{2,1,0:T(8,128)(2,1)S(1)}, bf16[1,512,1024]{2,1,0:T(8,128)(2,1)}, u32[]{:S(2)}) copy-start(bf16[1,512,1024]{2,1,0:T(8,128)(2,1)} %param.9) | copy-start | bytes 3145732
  36.2 30.5 %copy-start.1 = (bf16[1,512,1024]{2,1,0:T(8,128)(2,1)S(1)}, bf16[1,512,1024]{2,1,0:T(8,128)(2,1)}, u32[]{:S(2)}) copy-start(bf16[1,512,1024]{2,1,0:T(8,128)(2,1)} %param.11) | copy-start | bytes 3145732
  39.5 27.2 %copy-start.2 = (f32[8,272,128]{2,1,0:T(8,128)S(1)}, f32[8,272,128]{2,1,0:T(8,128)}, u32[]{:S(2)}) copy-start(f32[8,272,128]{2,1,0:T(8,128)} %get-tuple-element.27.own_ref) | copy-start | bytes 3342340
  61.8 4.9 %collective-permute-start.1 = (f32[8,128,128]{2,1,0:T(8,128)S(1)}, f32[8,128,128]{2,1,0:T(8,128)S(1)}, u32[]{:S(2)}, u32[]{:S(2)}) collective-permute-start(f32[8,128,128]{2,1,0:T(8,128)S(1)} %pass.1), channel_id=1, source_target_pairs={{0,4},{4,0},{1,5},{5,1},{2,6},{6,2},{3,7},{7,3},{8,12},{12,8},{9,1... | collective-permute-start | bytes 1572872 | tf_op jit(solution)/shard_map/ppermute | solution.py:380
  71.9 2.0 %collective-permute-start.2 = (f32[8,128,128]{2,1,0:T(8,128)S(1)}, f32[8,128,128]{2,1,0:T(8,128)S(1)}, u32[]{:S(2)}, u32[]{:S(2)}) collective-permute-start(f32[8,128,128]{2,1,0:T(8,128)S(1)} %get-tuple-element.31), channel_id=1, source_target_pairs={{0,4},{4,0},{1,5},{5,1},{2,6},{6,2},{3,7},{7,3},{8,12},{12,8},{9,1... | collective-permute-start | bytes 1572872 | tf_op jit(solution)/shard_map/ppermute | solution.py:380
  74.8 16.5 %all-to-all-start.2 = ((f32[16,1,8192]{2,1,0:T(1,128)}), f32[16,1,8192]{2,1,0:T(1,128)S(1)}, u32[]{:S(2)}, u32[]{:S(2)}) async-start(f32[16,1,8192]{2,1,0:T(1,128)} %bitcast.11), calls=%async_computation.2 | async-start | bytes 1048576 | tf_op jit(solution)/shard_map/all_to_all | solution.py:376
  92.7 12.5 %all-to-all-start.3 = ((f32[8,1,8192]{2,1,0:T(1,128)}), f32[8,1,8192]{2,1,0:T(1,128)S(1)}, u32[]{:S(2)}, u32[]{:S(2)}) async-start(f32[8,1,8192]{2,1,0:T(1,128)} %bitcast.42), calls=%async_computation.3 | async-start | bytes 524288 | tf_op jit(solution)/shard_map/all_to_all | solution.py:376
  119.4 5.6 %collective-permute-start.3 = (f32[8,128,128]{2,1,0:T(8,128)S(1)}, f32[8,128,128]{2,1,0:T(8,128)S(1)}, u32[]{:S(2)}, u32[]{:S(2)}) collective-permute-start(f32[8,128,128]{2,1,0:T(8,128)S(1)} %bitcast.40), channel_id=1, source_target_pairs={{0,4},{4,0},{1,5},{5,1},{2,6},{6,2},{3,7},{7,3},{8,12},{12,8},{9,1... | collective-permute-start | bytes 1572872 | tf_op jit(solution)/shard_map/ppermute | solution.py:380

commit v7 on v5

--- a/solution.py
+++ b/solution.py
@@ -67,7 +67,7 @@
     ]
 
 
-def over_heads(srcs, bufs, sems, outs, out_sems, work):
+def over_heads(srcs, bufs, sems, outs, out_sems, work, together=1):
     for h in range(HEADS):
         for copy in head_copies(srcs, bufs, sems, h):
             copy.start()
@@ -82,7 +82,7 @@
         for i in range(HPB):
             for copy in head_copies(srcs, bufs, sems, step * HPB + i):
                 copy.wait()
-        for i in range(HPB):
+        for i in range(0, HPB, together):
             work(step * HPB + i)
         for i in range(HPB):
             for copy in back(step * HPB + i):
@@ -103,10 +103,21 @@
         rows = slice(b * BLOCK, (b + 1) * BLOCK)
         cum_ref[:, rows] = cumul_rows(low, ld_ref[:, rows])
 
-    def work(h):
+    def both(ref, w_ref, h):
+        zero = jnp.zeros((DH, DH), BF16)
+        maps = jnp.concatenate([
+            jnp.concatenate([w_ref[h], zero], axis=1),
+            jnp.concatenate([zero, w_ref[h + 1]], axis=1),
+        ], axis=0)
+        return dot(maps, jnp.concatenate([ref[h], ref[h + 1]], axis=1), ((0,), (1,)))
+
+    def pair(h):
+        two_q, two_k = both(q_ref, wq_ref, h), both(k_ref, wk_ref, h)
+        for i in range(2):
+            work(h + i, two_q[i * DH:(i + 1) * DH], two_k[i * DH:(i + 1) * DH])
+
+    def work(h, all_q, all_k):
         ups, cons, tots = [], [], []
-        all_q = dot(wq_ref[h], q_ref[h], ((0,), (1,)))
-        all_k = dot(wk_ref[h], k_ref[h], ((0,), (1,)))
         for b in range(2):
             rows = slice(b * BLOCK, (b + 1) * BLOCK)
             cum = cum_ref[pl.ds(h, 1), rows]
@@ -133,7 +144,7 @@
         own_ref[h, 2 * DH + 8:, :] = d1
 
     over_heads((q, k, v, g, wq, wk), (q_ref, k_ref, v_ref, g_ref, wq_ref, wk_ref), sems,
-               [(own_ref, own)], out_sems, work)
+               [(own_ref, own)], out_sems, pair, together=2)
 
 
 def combine_body(mine_ref, recv_ref, out_ref):
@@ -218,33 +229,49 @@
              gp, st, mine_ref, send_ref, tr_ref, ab_ref, gp_ref, st_ref, sems, out_sems):
     first = core[0] == 0
 
-    def work(h):
-        lanes = pl.ds(pl.multiple_of(h * DH, DH), DH)
+    def diagonal(a, b):
+        zero = jnp.zeros((DH, DH), BF16)
+        return jnp.concatenate([
+            jnp.concatenate([a, zero], axis=1), jnp.concatenate([zero, b], axis=1)
+        ], axis=0)
+
+    def rounded(h):
         inc, recv = inc_ref[h], recv_ref[h]
         state = jnp.where(first, inc, recv)
         after = jnp.where(first, recv, inc)
         d0, d1 = own_ref[h, 2 * DH:2 * DH + 1, :], own_ref[h, 2 * DH + 8:2 * DH + 9, :]
-        st_ref[h, 0] = state.astype(BF16)
-        st_ref[h, 1] = (d0 * state + own_ref[h, 0:DH, :]).astype(BF16)
-        st_ref[h, 2] = (own_ref[h, DH:2 * DH, :] + d1 * after).astype(BF16)
-        st_ref[h, 3] = after.astype(BF16)
+        four = (
+            state.astype(BF16),
+            (d0 * state + own_ref[h, 0:DH, :]).astype(BF16),
+            (own_ref[h, DH:2 * DH, :] + d1 * after).astype(BF16),
+            after.astype(BF16),
+        )
+        for j in range(4):
+            st_ref[h, j] = four[j]
+        return four
+
+    def pair(h):
+        lanes = pl.ds(pl.multiple_of(h * DH, 2 * DH), 2 * DH)
+        one, two = rounded(h), rounded(h + 1)
         for b in range(2):
             rows = slice(b * BLOCK, (b + 1) * BLOCK)
-            from_state = dot(g_ref[rows, lanes], st_ref[h, b], NT)
-            from_after = dot(v_ref[rows, lanes], st_ref[h, 2 + b], NT)
-            gp_ref[h, 0, rows] = (
-                ab_ref[h, 0, rows].astype(F32) + ab_ref[h, 1, rows].astype(F32) * from_state
-            ).astype(BF16)
-            gp_ref[h, 1, rows] = (
-                ab_ref[h, 2, rows].astype(F32) + ab_ref[h, 3, rows].astype(F32) * from_after
-            ).astype(BF16)
-        part_q = dot(tr_ref[h, 0], gp_ref[h, 0])
-        part_k = dot(tr_ref[h, 1], gp_ref[h, 1])
-        mine_ref[h] = jnp.where(first, part_q, part_k)
-        send_ref[h] = jnp.where(first, part_k, part_q)
+            from_state = dot(g_ref[rows, lanes], diagonal(one[b], two[b]), NT)
+            from_after = dot(v_ref[rows, lanes], diagonal(one[2 + b], two[2 + b]), NT)
+            for i in range(2):
+                cols = slice(i * DH, (i + 1) * DH)
+                for j, x in enumerate((from_state, from_after)):
+                    gp_ref[h + i, j, rows] = (
+                        ab_ref[h + i, 2 * j, rows].astype(F32)
+                        + ab_ref[h + i, 2 * j + 1, rows].astype(F32) * x[:, cols]
+                    ).astype(BF16)
+        for i in range(2):
+            part_q = dot(tr_ref[h + i, 0], gp_ref[h + i, 0])
+            part_k = dot(tr_ref[h + i, 1], gp_ref[h + i, 1])
+            mine_ref[h + i] = jnp.where(first, part_q, part_k)
+            send_ref[h + i] = jnp.where(first, part_k, part_q)
 
     over_heads((tr, ab), (tr_ref, ab_ref), sems,
-               [(gp_ref, gp), (st_ref, st)], out_sems, work)
+               [(gp_ref, gp), (st_ref, st)], out_sems, pair, together=2)
 
 
 def k3b_body(core, ov_ref, dec_ref, st_ref, gp_ref, wq_ref, wk_ref,

time: 124 us -> 123 us (level)
  no operation moved by 1% of the time
where the time goes in v7:
time: 123 us; the launch traced here: 122 us
  blocking collectives  46.5 us (38%)
  Pallas kernels  33.3 us (27%)
  starting transfers between devices  26.6 us (22%)
  waiting for transfers between devices  14.1 us (11%)
    all_to_all x3, blocking collectives, exchange(): return lax.all_to_all(x, axes, 0, 0, tiled=True)  46.5 us
    all_to_all x2, starting transfers between devices, exchange(): return lax.all_to_all(x, axes, 0, 0, tiled=True)  15.4 us
    pallas_call x1, Pallas kernels, local(): call(k2_body, 'k2', [smem()] + [seq()] * 4 + [ld_spec] + map_specs, [per_...  13.5 us
    ppermute x4, starting transfers between devices, swap_cores(): return lax.ppermute(x, 'c', [(0, 1), (1, 0)])  11.2 us
    all_to_all x2, waiting for transfers between devices, exchange(): return lax.all_to_all(x, axes, 0, 0, tiled=True)  7.86 us
    ppermute x4, waiting for transfers between devices, swap_cores(): return lax.ppermute(x, 'c', [(0, 1), (1, 0)])  6.19 us
    pallas_call x1, Pallas kernels, local(): call(k3b_body, 'k3b', [smem(), per_head(2, TOK, DH, heads=WIDE), per_head...  5.8 us
    pallas_call x1, Pallas kernels, local(): streamed(k1_body, 'k1', [slot] * 4 + [square] * 2, [pltpu.VMEM(own_dims,...  5.75 us
  transfers between devices with their start and end apart: 6, of which 6 were waited for; matrix products, arithmetic and copies ran while one was open for 0% of the time, Pallas kernels for 16%

profile of v7, /device:TPU:1, one launch (start us, length us, event | category | flops | bytes accessed | tf_op | source)
XLA Modules:
  0.0 122.2 jit_solution(11445449630770426668)
XLA Ops:
  0.6 5.8 %k1.1 = (f32[8,136,128]{2,1,0:T(8,128)S(1)}, f32[8,136,128]{2,1,0:T(8,128)S(1)}, f32[8,272,128]{2,1,0:T(8,128)}) custom-call(s32[1]{0:T(128)} %bitcast.core.refs_1_, f32[8,512]{1,0:T(8,128)} %bitcast.43, bf16[512,1024]{1,0:T(8,128)(2,1)} %bitcast.37, bf16[512,1024]{1,0:T(8,128)(2,1)} %bitcast.39, bf16[512,1024]{1,0:T(8,128)(2,1)} %bitcast.23, ...), custom_call_target="tpu_custom_call" | custom-call | tf_op jit(solution)/shard_map/k1/pallas_call | solution.py:414
  6.4 3.3 %collective-permute-start = (f32[8,136,128]{2,1,0:T(8,128)S(1)}, f32[8,136,128]{2,1,0:T(8,128)S(1)}, u32[]{:S(2)}, u32[]{:S(2)}) collective-permute-start(f32[8,136,128]{2,1,0:T(8,128)S(1)} %get-tuple-element.24), channel_id=1, source_target_pairs={{0,4},{4,0},{1,5},{5,1},{2,6},{6,2},{3,7},{7,3},{8,12},{12,8},{9,1... | collective-permute-start | bytes 1671176 | tf_op jit(solution)/shard_map/ppermute | solution.py:394
  9.7 1.6 %collective-permute-done.refs_1_ = f32[8,136,128]{2,1,0:T(8,128)S(1)} collective-permute-done((f32[8,136,128]{2,1,0:T(8,128)S(1)}, f32[8,136,128]{2,1,0:T(8,128)S(1)}, u32[]{:S(2)}, u32[]{:S(2)}) %collective-permute-start) | collective-permute-done | bytes 557088 | tf_op jit(solution)/shard_map/ppermute | solution.py:394
  11.3 0.9 combine.1.refs_0_
  12.1 9.3 %all-to-all-start = ((f32[32,1,4224]{2,1,0:T(1,128)}), f32[32,1,4224]{2,1,0:T(1,128)S(1)}, u32[]{:S(2)}, u32[]{:S(2)}) async-start(f32[32,1,4224]{2,1,0:T(1,128)} %bitcast.6), calls=%async_computation | async-start | bytes 1081344 | tf_op jit(solution)/shard_map/all_to_all | solution.py:390
  21.5 13.5 %k2.1 = (bf16[8,4,512,128]{3,2,1,0:T(8,128)(2,1)}, f32[8,2,512,128]{3,2,1,0:T(8,128)}, bf16[8,2,512,128]{3,2,1,0:T(8,128)(2,1)}, bf16[8,2,128,512]{3,2,1,0:T(8,128)(2,1)}, s32[1]{0:T(128)}) custom-call(f32[1056,128]{1,0:T(8,128)} %combine.1.refs_0_, s32[1]{0:T(128)} %bitcast.core.refs_1_, bf16[512,1024]{1,0:T(8,128)(2,1)} %bitcast.38, ...), custom_call_target="tpu_custom_call" | custom-call | flops 1073741824 | bytes 1048576 | tf_op jit(solution)/shard_map/k2/pallas_call | solution.py:424
  35.0 0.0 copy-start
  35.0 0.0 copy-start.1
  35.0 3.3 %all-to-all-done = f32[32,1,4224]{2,1,0:T(1,128)S(1)} async-done(((f32[32,1,4224]{2,1,0:T(1,128)}), f32[32,1,4224]{2,1,0:T(1,128)S(1)}, u32[]{:S(2)}, u32[]{:S(2)}) %all-to-all-start) | async-done | bytes 540704 | tf_op jit(solution)/shard_map/all_to_all | solution.py:390
  38.3 0.0 copy-start.2
  38.3 0.9 scan.1
  39.2 21.4 %all_to_all.45 = f32[32,1,4096]{2,1,0:T(1,128)S(1)} all-to-all(f32[32,1,4096]{2,1,0:T(1,128)S(1)} %bitcast.33), channel_id=1, replica_groups=mesh['z'=8,'x'=4,'c'=2,'dp'=4] {'z','x'}, dimensions={0} | all-to-all | bytes 1048576 | tf_op jit(solution)/shard_map/all_to_all | solution.py:390
  60.5 0.1 pass.1
  60.6 3.4 %collective-permute-start.1 = (f32[8,128,128]{2,1,0:T(8,128)S(1)}, f32[8,128,128]{2,1,0:T(8,128)S(1)}, u32[]{:S(2)}, u32[]{:S(2)}) collective-permute-start(f32[8,128,128]{2,1,0:T(8,128)S(1)} %pass.1), channel_id=1, source_target_pairs={{0,4},{4,0},{1,5},{5,1},{2,6},{6,2},{3,7},{7,3},{8,12},{12,8},{9,1... | collective-permute-start | bytes 1572872 | tf_op jit(solution)/shard_map/ppermute | solution.py:394
  64.0 1.5 %collective-permute-done.1.recv_ref = f32[8,128,128]{2,1,0:T(8,128)S(1)} collective-permute-done((f32[8,128,128]{2,1,0:T(8,128)S(1)}, f32[8,128,128]{2,1,0:T(8,128)S(1)}, u32[]{:S(2)}, u32[]{:S(2)}) %collective-permute-start.1) | collective-permute-done | bytes 524320 | tf_op jit(solution)/shard_map/ppermute | solution.py:394
  65.5 0.0 copy-done
  65.5 0.0 copy-done.1
  65.5 0.0 copy-done.2
  65.5 4.9 %k3a.1 = (bf16[8,2,512,128]{3,2,1,0:T(8,128)(2,1)}, bf16[8,4,128,128]{3,2,1,0:T(8,128)(2,1)}, f32[8,128,128]{2,1,0:T(8,128)S(1)}, f32[8,128,128]{2,1,0:T(8,128)S(1)}) custom-call(s32[1]{0:T(128)} %bitcast.core.refs_1_, f32[8,128,128]{2,1,0:T(8,128)S(1)} %bitcast.30, f32[8,128,128]{2,1,0:T(8,128)S(1)} %collective-permute-done.1.recv_ref, ...), custom_call_target="tpu_custom_call" | custom-call | tf_op jit(solution)/shard_map/k3a/pallas_call | solution.py:449
  70.4 0.5 collective-permute-start.2
  70.9 1.5 %collective-permute-done.2.refs_1_ = f32[8,128,128]{2,1,0:T(8,128)S(1)} collective-permute-done((f32[8,128,128]{2,1,0:T(8,128)S(1)}, f32[8,128,128]{2,1,0:T(8,128)S(1)}, u32[]{:S(2)}, u32[]{:S(2)}) %collective-permute-start.2) | collective-permute-done | bytes 524320 | tf_op jit(solution)/shard_map/ppermute | solution.py:394
  72.4 0.8 add.1.refs_0_
  73.2 6.1 %all-to-all-start.2 = ((f32[16,1,8192]{2,1,0:T(1,128)}), f32[16,1,8192]{2,1,0:T(1,128)S(1)}, u32[]{:S(2)}, u32[]{:S(2)}) async-start(f32[16,1,8192]{2,1,0:T(1,128)} %bitcast.14), calls=%async_computation.2 | async-start | bytes 1048576 | tf_op jit(solution)/shard_map/all_to_all | solution.py:390
  79.4 5.8 %k3b.1 = (bf16[512,1024]{1,0:T(8,128)(2,1)}, bf16[512,1024]{1,0:T(8,128)(2,1)}, bf16[512,1024]{1,0:T(8,128)(2,1)}, bf16[512,1024]{1,0:T(8,128)(2,1)}, s32[1]{0:T(128)}) custom-call(f32[8,128,128]{2,1,0:T(8,128)} %add.1.refs_0_, s32[1]{0:T(128)} %bitcast.core.refs_1_, f32[8,2,512,128]{3,2,1,0:T(8,128)} %get-tuple-element.31.refs_2_, ...), custom_call_target="tpu_custom_call" | custom-call | flops 1073741824 | bytes 1048576 | tf_op jit(solution)/shard_map/k3b/pallas_call | solution.py:461
  85.2 4.6 %all-to-all-done.2 = f32[16,1,8192]{2,1,0:T(1,128)S(1)} async-done(((f32[16,1,8192]{2,1,0:T(1,128)}), f32[16,1,8192]{2,1,0:T(1,128)S(1)}, u32[]{:S(2)}, u32[]{:S(2)}) %all-to-all-start.2) | async-done | bytes 524320 | tf_op jit(solution)/shard_map/all_to_all | solution.py:390
  89.7 0.7 spread_z.1
  90.4 11.6 %all_to_all.46 = f32[8,1,8192]{2,1,0:T(1,128)S(1)} all-to-all(f32[8,1,8192]{2,1,0:T(1,128)S(1)} %bitcast.36), channel_id=1, replica_groups=mesh['z'=8,'x'=4,'c'=2,'dp'=4] {'z'}, dimensions={0} | all-to-all | bytes 524288 | tf_op jit(solution)/shard_map/all_to_all | solution.py:390
  102.0 0.1 spread_xy.1
  102.1 13.4 %all_to_all.47 = f32[16,1,8192]{2,1,0:T(1,128)S(1)} all-to-all(f32[16,1,8192]{2,1,0:T(1,128)S(1)} %bitcast.34), channel_id=1, replica_groups=mesh['z'=8,'x'=4,'c'=2,'dp'=4] {'x','dp'}, dimensions={0} | all-to-all | bytes 1048576 | tf_op jit(solution)/shard_map/all_to_all | solution.py:390
  115.5 4.1 %collective-permute-start.3 = (f32[8,128,128]{2,1,0:T(8,128)S(1)}, f32[8,128,128]{2,1,0:T(8,128)S(1)}, u32[]{:S(2)}, u32[]{:S(2)}) collective-permute-start(f32[8,128,128]{2,1,0:T(8,128)S(1)} %bitcast.41), channel_id=1, source_target_pairs={{0,4},{4,0},{1,5},{5,1},{2,6},{6,2},{3,7},{7,3},{8,12},{12,8},{9,1... | collective-permute-start | bytes 1572872 | tf_op jit(solution)/shard_map/ppermute | solution.py:394
  119.6 1.5 %collective-permute-done.3 = f32[8,128,128]{2,1,0:T(8,128)S(1)} collective-permute-done((f32[8,128,128]{2,1,0:T(8,128)S(1)}, f32[8,128,128]{2,1,0:T(8,128)S(1)}, u32[]{:S(2)}, u32[]{:S(2)}) %collective-permute-start.3) | collective-permute-done | bytes 524320 | tf_op jit(solution)/shard_map/ppermute | solution.py:394
  121.1 1.1 broadcast_select_fusion
Async XLA Ops:
  6.4 4.9 %collective-permute-start = (f32[8,136,128]{2,1,0:T(8,128)S(1)}, f32[8,136,128]{2,1,0:T(8,128)S(1)}, u32[]{:S(2)}, u32[]{:S(2)}) collective-permute-start(f32[8,136,128]{2,1,0:T(8,128)S(1)} %get-tuple-element.24), channel_id=1, source_target_pairs={{0,4},{4,0},{1,5},{5,1},{2,6},{6,2},{3,7},{7,3},{8,12},{12,8},{9,1... | collective-permute-start | bytes 1671176 | tf_op jit(solution)/shard_map/ppermute | solution.py:394
  12.1 26.2 %all-to-all-start = ((f32[32,1,4224]{2,1,0:T(1,128)}), f32[32,1,4224]{2,1,0:T(1,128)S(1)}, u32[]{:S(2)}, u32[]{:S(2)}) async-start(f32[32,1,4224]{2,1,0:T(1,128)} %bitcast.6), calls=%async_computation | async-start | bytes 1081344 | tf_op jit(solution)/shard_map/all_to_all | solution.py:390
  35.0 30.5 %copy-start = (bf16[1,512,1024]{2,1,0:T(8,128)(2,1)S(1)}, bf16[1,512,1024]{2,1,0:T(8,128)(2,1)}, u32[]{:S(2)}) copy-start(bf16[1,512,1024]{2,1,0:T(8,128)(2,1)} %param.9) | copy-start | bytes 3145732
  35.0 30.5 %copy-start.1 = (bf16[1,512,1024]{2,1,0:T(8,128)(2,1)S(1)}, bf16[1,512,1024]{2,1,0:T(8,128)(2,1)}, u32[]{:S(2)}) copy-start(bf16[1,512,1024]{2,1,0:T(8,128)(2,1)} %param.11) | copy-start | bytes 3145732
  38.3 27.2 %copy-start.2 = (f32[8,272,128]{2,1,0:T(8,128)S(1)}, f32[8,272,128]{2,1,0:T(8,128)}, u32[]{:S(2)}) copy-start(f32[8,272,128]{2,1,0:T(8,128)} %get-tuple-element.26.own_ref) | copy-start | bytes 3342340
  60.6 4.9 %collective-permute-start.1 = (f32[8,128,128]{2,1,0:T(8,128)S(1)}, f32[8,128,128]{2,1,0:T(8,128)S(1)}, u32[]{:S(2)}, u32[]{:S(2)}) collective-permute-start(f32[8,128,128]{2,1,0:T(8,128)S(1)} %pass.1), channel_id=1, source_target_pairs={{0,4},{4,0},{1,5},{5,1},{2,6},{6,2},{3,7},{7,3},{8,12},{12,8},{9,1... | collective-permute-start | bytes 1572872 | tf_op jit(solution)/shard_map/ppermute | solution.py:394
  70.4 2.0 %collective-permute-start.2 = (f32[8,128,128]{2,1,0:T(8,128)S(1)}, f32[8,128,128]{2,1,0:T(8,128)S(1)}, u32[]{:S(2)}, u32[]{:S(2)}) collective-permute-start(f32[8,128,128]{2,1,0:T(8,128)S(1)} %get-tuple-element.30), channel_id=1, source_target_pairs={{0,4},{4,0},{1,5},{5,1},{2,6},{6,2},{3,7},{7,3},{8,12},{12,8},{9,1... | collective-permute-start | bytes 1572872 | tf_op jit(solution)/shard_map/ppermute | solution.py:394
  73.2 16.5 %all-to-all-start.2 = ((f32[16,1,8192]{2,1,0:T(1,128)}), f32[16,1,8192]{2,1,0:T(1,128)S(1)}, u32[]{:S(2)}, u32[]{:S(2)}) async-start(f32[16,1,8192]{2,1,0:T(1,128)} %bitcast.14), calls=%async_computation.2 | async-start | bytes 1048576 | tf_op jit(solution)/shard_map/all_to_all | solution.py:390
  115.5 5.6 %collective-permute-start.3 = (f32[8,128,128]{2,1,0:T(8,128)S(1)}, f32[8,128,128]{2,1,0:T(8,128)S(1)}, u32[]{:S(2)}, u32[]{:S(2)}) collective-permute-start(f32[8,128,128]{2,1,0:T(8,128)S(1)} %bitcast.41), channel_id=1, source_target_pairs={{0,4},{4,0},{1,5},{5,1},{2,6},{6,2},{3,7},{7,3},{8,12},{12,8},{9,1... | collective-permute-start | bytes 1572872 | tf_op jit(solution)/shard_map/ppermute | solution.py:394
